TPU v7x, 32 devices: a whole 2x2x4 slice. The times are simulated.
32 devices in a mesh: ctx: 8 (over z, core), fsdp: 4 (over y, x).
Axes of the slice: x: 2, y: 2, z: 4, core: 2. Of those that a mesh axis runs over, the one named last changes fastest.
Arguments:
- inputs: bfloat16 [4096, 5376], P('ctx'), may hold values from -400 to 400
- output_cotangent: bfloat16 [4096, 4096], P('ctx', 'fsdp'), may hold values from -96 to 96
- w_query: bfloat16 [5376, 4096], P('ctx', 'fsdp'), may hold values from -0.078125 to 0.078125
- key_projection: bfloat16 [5376, 2048], P('ctx', 'fsdp'), may hold values from -0.078125 to 0.078125
- value_projection: bfloat16 [5376, 2048], P('ctx', 'fsdp'), may hold values from -0.078125 to 0.078125
- norm_gain: float32 [5376], replicated, may hold values from 0.25 to 1.75
- q_gain: float32 [128], replicated, may hold values from 0.25 to 1.75
- key_norm_gain: float32 [128], replicated, may hold values from 0.25 to 1.75
- half_lengths: int32 [4], replicated, may hold values from 1 to 3072, 4096 in all
Outputs:
- grad_inputs: bfloat16 [4096, 5376], P('ctx', 'fsdp')
- grad_w_query: bfloat16 [5376, 4096], P('ctx', 'fsdp')
- grad_w_key: bfloat16 [5376, 2048], P('ctx', 'fsdp')
- grad_w_value: bfloat16 [5376, 2048], P('ctx', 'fsdp')
- grad_norm_gain: float32 [5376], P(('fsdp', 'ctx'))
- grad_q_gain: float32 [128], replicated
- grad_k_gain: float32 [128], replicated
- norm_row_dots: float32 [4096], P('ctx')
Inputs may be any that keep to these rules, and one draw needn't show every extreme that they name: `half_lengths`: the halves add up to 4096 tokens, and the longest holds exactly 3072.
All inputs are finite; a program needn't handle non-finite values.
Results may differ from a plain program's by a relative error of at most 0.035.
Values may be sent and summed in bfloat16 or wider, within the bound.
No kernel may reach another device: no remote copies, remote signals or barrier semaphores. Data moves between devices by JAX's collectives and lax.ppermute only.
A program may use at most 192 MiB of HBM per device.

v0:
```python
import functools

import jax
import jax.numpy as jnp
from jax import lax
from jax.experimental import pallas as pl
from jax.experimental.pallas import tpu as pltpu
from jax.sharding import PartitionSpec as P


WIN = 1024
REACH = 2
BLOCKED = -1e30

epsilon = 1e-06
query_scale = 168.0 ** (-0.5)

NT = (((1,), (1,)), ((), ()))


def shift(value, axis, steps):
    count = lax.axis_size(axis)
    initial, last = (max(0, -steps), min(count, count - steps))
    return lax.ppermute(value, axis, [(s, s + steps) for s in range(initial, last)])


def swap(value, axis, flip):
    return lax.ppermute(value, axis, [(s, s ^ flip) for s in range(lax.axis_size(axis))])


def dot(a, b, dims=(((1,), (0,)), ((), ()))):
    return lax.dot_general(a, b, dims, preferred_element_type=jnp.float32)


def everywhere(value, axes):
    for axis in axes:
        flip = 1
        while flip < lax.axis_size(axis):
            value = value + swap(value, axis, flip)
            flip *= 2
    return value


def share_of_columns(normed_turned, shard_rows):
    chips = lax.axis_size("ctx") // 2
    shares = lax.axis_size("fsdp")
    tokens = normed_turned.shape[1]
    blocks = normed_turned.reshape(chips, 2, shares, shard_rows // shares, tokens)
    return lax.dynamic_index_in_dim(blocks, lax.axis_index("fsdp"), 2, keepdims=False)


def start_columns(blocks):
    chips = blocks.shape[0]
    chip = lax.axis_index("ctx") // 2
    pieces = []
    for m in range(chips):
        piece = lax.dynamic_index_in_dim(blocks, chip ^ m, 0, keepdims=False)
        if m:
            piece = swap(piece, "ctx", 2 * m)
        pieces.append(piece)
    return pieces


def finish_columns(pieces, gate):
    chips = len(pieces)
    chip = lax.axis_index("ctx") // 2
    core = lax.axis_index("ctx") % 2
    shares = lax.axis_size("fsdp")
    share = lax.axis_index("fsdp")
    pieces, _ = lax.optimization_barrier((jnp.stack(pieces), gate))
    piece, tokens = pieces.shape[2:]
    kept = lax.dynamic_index_in_dim(pieces, core, 1, keepdims=False)
    other = swap(lax.dynamic_index_in_dim(pieces, 1 - core, 1, keepdims=False), "ctx", 1)
    first, second = jnp.where(core == 0, kept, other), jnp.where(core == 0, other, kept)
    both = jnp.stack([first, second], axis=1)
    bit = 1
    while bit < chips:
        grouped = both.reshape(chips // (2 * bit), 2, bit, 2, piece, tokens)
        both = jnp.where((chip & bit) > 0, grouped[:, ::-1], grouped).reshape(both.shape)
        bit *= 2
    mine = jnp.transpose(both, (2, 0, 1, 3)).reshape(piece, chips * 2 * tokens)
    columns = jnp.zeros((shares,) + mine.shape, mine.dtype)
    columns = lax.dynamic_update_index_in_dim(columns, mine, share, 0)
    for m in range(1, shares):
        part = swap(mine, "fsdp", m)
        columns = lax.dynamic_update_index_in_dim(columns, part, share ^ m, 0)
    return columns.reshape(shares * piece, chips * 2 * tokens)


def key_body(k_ref, v_ref, gain_ref, kv_ref):
    k = k_ref[...]
    inv = lax.rsqrt(jnp.mean(k * k, axis=1, keepdims=True) + epsilon)
    kv_ref[0] = (k * inv * gain_ref[...]).astype(jnp.bfloat16)
    kv_ref[1] = v_ref[...].astype(jnp.bfloat16)


def key_rows_of(projected, gain, kv_heads, head_dim):
    tokens = projected.shape[0]
    return pl.pallas_call(
        key_body,
        grid=(kv_heads,),
        in_specs=[
            pl.BlockSpec((tokens, head_dim), lambda g: (0, g)),
            pl.BlockSpec((tokens, head_dim), lambda g: (0, kv_heads + g)),
            pl.BlockSpec((1, head_dim), lambda g: (0, 0)),
        ],
        out_specs=pl.BlockSpec((2, tokens, head_dim), lambda g: (0, 0, g)),
        out_shape=jax.ShapeDtypeStruct((2, tokens, kv_heads * head_dim), jnp.bfloat16),
        name="key_rows",
    )(projected, projected, gain[None, :])


def key_grad_body(own_ref, near_ref, far_ref, k_ref, gain_ref, dk_ref, dv_ref, sum_ref):
    total = own_ref[...] + near_ref[...].astype(jnp.float32) + far_ref[...].astype(jnp.float32)
    k = k_ref[...]
    inv = lax.rsqrt(jnp.mean(k * k, axis=1, keepdims=True) + epsilon)
    k_hat = k * inv
    d = total[0]
    u = d * gain_ref[...]
    dk_ref[...] = (inv * (u - k_hat * jnp.mean(u * k_hat, axis=1, keepdims=True))).astype(
        jnp.bfloat16
    )
    dv_ref[...] = total[1].astype(jnp.bfloat16)

    @pl.when(pl.program_id(0) == 0)
    def _():
        sum_ref[...] = jnp.zeros_like(sum_ref)

    sum_ref[...] += jnp.sum(d * k_hat, axis=0, keepdims=True)


def key_grads_of(own, near, far, projected, gain, kv_heads, head_dim):
    tokens = projected.shape[0]
    stacked = pl.BlockSpec((2, tokens, head_dim), lambda g: (0, 0, g))
    flat = pl.BlockSpec((tokens, head_dim), lambda g: (0, g))
    row = pl.BlockSpec((1, head_dim), lambda g: (0, 0))
    half = jax.ShapeDtypeStruct((tokens, kv_heads * head_dim), jnp.bfloat16)
    return pl.pallas_call(
        key_grad_body,
        grid=(kv_heads,),
        in_specs=[stacked, stacked, stacked, flat, row],
        out_specs=(flat, flat, row),
        out_shape=(half, half, jax.ShapeDtypeStruct((1, head_dim), jnp.float32)),
        name="key_grads",
    )(own, near, far, projected, gain[None, :])


def attention_body(
    start_ref,
    ends_ref,
    q_ref,
    go_ref,
    own_ref,
    near_ref,
    far_ref,
    mult_ref,
    dq_ref,
    d_own_ref,
    d_near_ref,
    d_far_ref,
    sum_ref,
    bias_ref,
    k_ref,
    v_ref,
    kt_ref,
    vt_ref,
    dk_ref,
    dv_ref,
    *,
    rows,
    heads,
    segments,
):
    g = pl.program_id(0)
    s = pl.program_id(1)
    last = pl.num_programs(1) - 1
    tokens, head_dim = own_ref.shape[1:]
    reach = WIN
    span = reach + rows
    offset = pl.multiple_of(s * rows, rows)

    @pl.when(g == 0)
    def _():
        first = start_ref[0]
        key_pos = (first - reach + s * rows) + lax.broadcasted_iota(jnp.int32, (span, 1), 0)
        query_pos = (first + s * rows) + lax.broadcasted_iota(jnp.int32, (1, rows), 1)
        key_seg = jnp.zeros((span, 1), jnp.int32)
        query_seg = jnp.zeros((1, rows), jnp.int32)
        for i in range(segments):
            key_seg += (ends_ref[i] <= key_pos).astype(jnp.int32)
            query_seg += (ends_ref[i] <= query_pos).astype(jnp.int32)
        distance = query_pos - key_pos
        allowed = (
            (key_seg == query_seg) & (distance >= 0) & (distance < WIN) & (key_pos >= 0)
        )
        bias_ref[s] = jnp.where(allowed, 0.0, BLOCKED)

    @pl.when(s == 0)
    def _():
        for at, ref in enumerate((far_ref, near_ref, own_ref)):
            k_ref[pl.ds(at * tokens, tokens), :] = ref[0]
            v_ref[pl.ds(at * tokens, tokens), :] = ref[1]
        dk_ref[...] = jnp.zeros_like(dk_ref)
        dv_ref[...] = jnp.zeros_like(dv_ref)

    @pl.when((s == 0) & (g == 0))
    def _():
        sum_ref[...] = jnp.zeros_like(sum_ref)

    k = k_ref[pl.ds(offset, span), :]
    v = v_ref[pl.ds(offset, span), :]
    kt_ref[...] = jnp.transpose(k)
    vt_ref[...] = jnp.transpose(v)
    mult = mult_ref[...]
    bias = bias_ref[s]
    for h in range(heads):
        at = slice(h * head_dim, (h + 1) * head_dim)
        q = q_ref[:, at]
        inv = lax.rsqrt(jnp.mean(q * q, axis=1, keepdims=True) + epsilon)
        q_hat = q * inv
        q16 = (q_hat * mult).astype(jnp.bfloat16)
        go = go_ref[:, at]
        weights = jnp.exp(dot(k, q16, NT) + bias)
        over = 1.0 / jnp.sum(weights, axis=0, keepdims=True)
        out_t = dot(vt_ref[...], weights.astype(jnp.bfloat16)) * over
        delta = jnp.sum(jnp.transpose(go.astype(jnp.float32)) * out_t, axis=0, keepdims=True)
        probs = weights * over
        dv_ref[pl.ds(offset, span), :] += dot(probs.astype(jnp.bfloat16), go)
        d_scores = (probs * (dot(v, go, NT) - delta)).astype(jnp.bfloat16)
        dk_ref[pl.ds(offset, span), :] += dot(d_scores, q16)
        d_query = jnp.transpose(dot(kt_ref[...], d_scores))
        u = d_query * mult
        dq_ref[:, at] = (
            inv * (u - q_hat * jnp.mean(u * q_hat, axis=1, keepdims=True))
        ).astype(jnp.bfloat16)
        sum_ref[...] += jnp.sum(d_query * q_hat, axis=0, keepdims=True)

    @pl.when(s == last)
    def _():
        for at, ref in enumerate((d_far_ref, d_near_ref, d_own_ref)):
            ref[0] = dk_ref[pl.ds(at * tokens, tokens), :].astype(ref.dtype)
            ref[1] = dv_ref[pl.ds(at * tokens, tokens), :].astype(ref.dtype)


def attention(start, ends, q_raw, go, own, near, far, mult, kv_heads, head_dim):
    tokens, q_cols = q_raw.shape
    heads = q_cols // (kv_heads * head_dim)
    rows = min(256, tokens)
    steps = tokens // rows
    span = WIN + rows
    stacked = pl.BlockSpec((2, tokens, head_dim), lambda g, s, *_: (0, 0, g))
    by_query = pl.BlockSpec((rows, heads * head_dim), lambda g, s, *_: (s, g))
    row = pl.BlockSpec((1, head_dim), lambda g, s, *_: (0, 0))
    half = jax.ShapeDtypeStruct(own.shape, jnp.bfloat16)
    keys = WIN + tokens
    return pl.pallas_call(
        functools.partial(attention_body, rows=rows, heads=heads, segments=ends.shape[0]),
        grid_spec=pltpu.PrefetchScalarGridSpec(
            num_scalar_prefetch=2,
            grid=(kv_heads, steps),
            in_specs=[by_query, by_query, stacked, stacked, stacked, row],
            out_specs=(by_query, stacked, stacked, stacked, row),
            scratch_shapes=[
                pltpu.VMEM((steps, span, rows), jnp.float32),
                pltpu.VMEM((keys, head_dim), jnp.bfloat16),
                pltpu.VMEM((keys, head_dim), jnp.bfloat16),
                pltpu.VMEM((head_dim, span), jnp.bfloat16),
                pltpu.VMEM((head_dim, span), jnp.bfloat16),
                pltpu.VMEM((keys, head_dim), jnp.float32),
                pltpu.VMEM((keys, head_dim), jnp.float32),
            ],
        ),
        out_shape=(
            jax.ShapeDtypeStruct((tokens, q_cols), jnp.bfloat16),
            jax.ShapeDtypeStruct(own.shape, jnp.float32),
            half,
            half,
            jax.ShapeDtypeStruct((1, head_dim), jnp.float32),
        ),
        compiler_params=pltpu.CompilerParams(
            dimension_semantics=("arbitrary", "arbitrary"), vmem_limit_bytes=48 << 20
        ),
        name="attention",
    )(start, ends, q_raw, go, own, near, far, mult)


def layer(
    inputs,
    output_cotangent,
    w_query,
    key_projection,
    value_projection,
    norm_gain,
    q_gain,
    key_norm_gain,
    half_lengths,
):
    tokens, model_width = inputs.shape
    head_dim = q_gain.shape[0]
    kv_cols = key_projection.shape[1]
    kv_heads = kv_cols // head_dim
    ctx_count = lax.axis_size("ctx")
    fsdp_count = lax.axis_size("fsdp")
    ctx_index = lax.axis_index("ctx")
    fsdp_index = lax.axis_index("fsdp")
    on_first_core = ctx_index % 2 == 0
    grad_scale = float(tokens * ctx_count) ** (-0.5)
    shard_rows = w_query.shape[0]
    features = model_width // fsdp_count

    key_value = jnp.concatenate([key_projection, value_projection], axis=1)
    wide_kv = lax.all_gather(key_value, "ctx", axis=0, tiled=True)
    wide_q = lax.all_gather(w_query, "ctx", axis=0, tiled=True)

    widened = inputs.astype(jnp.float32)
    turned = jnp.transpose(inputs)
    inv_rms = lax.rsqrt(jnp.mean(widened * widened, axis=1, keepdims=True) + epsilon)
    x_hat = widened * inv_rms
    normed = lax.optimization_barrier((x_hat * norm_gain).astype(jnp.bfloat16))
    inv_row = jnp.transpose(inv_rms)

    kv_raw = dot(normed, wide_kv)
    own = key_rows_of(kv_raw, key_norm_gain, kv_heads, head_dim)
    normed_turned = (turned.astype(jnp.float32) * inv_row * norm_gain[:, None]).astype(
        jnp.bfloat16
    )
    blocks, own = lax.optimization_barrier((share_of_columns(normed_turned, shard_rows), own))
    far = shift(own, "ctx", REACH)
    picked = jnp.where(on_first_core, own, far)
    near = swap(picked, "ctx", 1)

    blocks, _ = lax.optimization_barrier((blocks, wide_q))
    pieces = start_columns(blocks)
    q_raw = dot(normed, wide_q)
    query_multiplier = (q_gain * query_scale)[None, :]
    dq16, d_own, d_near, d_far, q_sum = attention(
        jnp.full((1,), ctx_index * tokens, jnp.int32),
        jnp.cumsum(half_lengths).astype(jnp.int32),
        q_raw,
        output_cotangent,
        own,
        near,
        far,
        query_multiplier,
        kv_heads,
        head_dim,
    )

    all_dq = lax.all_gather(dq16, "ctx", axis=0, tiled=True)

    crossed = swap(d_near, "ctx", 1)
    nothing = jnp.zeros_like(crossed)
    outgoing = d_far + jnp.where(on_first_core, nothing, crossed)
    returned = shift(outgoing, "ctx", -REACH)
    query_part = dot(wide_q, dq16, NT)
    query_part = lax.optimization_barrier(query_part)
    dk16, dv16, k_sum = key_grads_of(
        d_own,
        jnp.where(on_first_core, crossed, nothing),
        returned,
        kv_raw,
        key_norm_gain,
        kv_heads,
        head_dim,
    )
    dkv16 = jnp.concatenate([dk16, dv16], axis=1)
    all_dkv = lax.all_gather(dkv16, "ctx", axis=0, tiled=True)

    columns = finish_columns(pieces, dq16)

    head_part = (query_part + dot(wide_kv, dkv16, NT)).astype(jnp.bfloat16)
    row_dot = everywhere(
        jnp.sum(
            head_part.astype(jnp.float32) * (turned.astype(jnp.float32) * norm_gain[:, None]),
            axis=0,
            keepdims=True,
        )
        * inv_row,
        ("fsdp",),
    )

    def part_of(array, index):
        return lax.dynamic_slice_in_dim(array, index * features, features, 0)

    sent = [swap(part_of(head_part, fsdp_index ^ m), "fsdp", m) for m in range(1, fsdp_count)]
    d_mine = part_of(head_part, fsdp_index).astype(jnp.float32)
    for part in sent:
        d_mine = d_mine + part.astype(jnp.float32)
    hat_mine = part_of(turned, fsdp_index).astype(jnp.float32) * inv_row
    upstream = d_mine * part_of(norm_gain, fsdp_index)[:, None]
    grad_inputs = jnp.transpose(
        (inv_row * (upstream - hat_mine * row_dot / model_width)).astype(jnp.bfloat16)
    )
    norm_row_dots = row_dot[0] * float(model_width) ** (-0.5)
    gain_term = grad_scale * jnp.sum(d_mine * hat_mine, axis=1)
    gain_sum = lax.dynamic_slice_in_dim(
        everywhere(gain_term, ("ctx",)),
        ctx_index * (features // ctx_count),
        features // ctx_count,
        0,
    )

    q_weights = (grad_scale * dot(columns, all_dq)).astype(jnp.bfloat16)
    k_weights = (grad_scale * dot(columns, all_dkv[:, :kv_cols])).astype(jnp.bfloat16)
    v_weights = (grad_scale * dot(columns, all_dkv[:, kv_cols:])).astype(jnp.bfloat16)

    gains = everywhere(
        jnp.concatenate([q_sum * (grad_scale * query_scale), k_sum * grad_scale], axis=0),
        ("fsdp", "ctx"),
    )
    return (
        grad_inputs,
        q_weights,
        k_weights,
        v_weights,
        gain_sum,
        gains[0],
        gains[1],
        norm_row_dots,
    )


def solution(mesh):
    placed = (
        P("ctx", None),
        P("ctx", "fsdp"),
        P("ctx", "fsdp"),
        P("ctx", "fsdp"),
        P("ctx", "fsdp"),
        P(),
        P(),
        P(),
        P(),
    )
    return jax.shard_map(
        layer,
        mesh=mesh,
        in_specs=placed,
        out_specs=(
            P("ctx", "fsdp"),
            P("ctx", "fsdp"),
            P("ctx", "fsdp"),
            P("ctx", "fsdp"),
            P(("fsdp", "ctx")),
            P(),
            P(),
            P("ctx"),
        ),
        check_vma=False,
    )
```

profile of v0, /device:TPU:0, one launch (start us, length us, event | category | flops | bytes accessed | tf_op | source)
XLA Modules:
  0.0 618.2 jit_solution(3428044519235440803)
XLA Ops:
  10.6 3.9 fusion
  14.8 4.3 fusion.48
  19.1 8.5 %copy.28 = bf16[5376,512]{1,0:T(8,128)(2,1)} copy(bf16[5376,512]{0,1:T(8,128)(2,1)} %fusion.48) | data formatting | bytes 11010048 | tf_op jit(solution)/shard_map/convert_element_type | solution.py:324
  27.6 6.9 %fusion.2 = bf16[512,5376]{1,0:T(8,128)(2,1)} fusion(bf16[512,5376]{1,0:T(8,128)(2,1)} %param.9, f32[5376]{0:T(1024)S(1)} %copy-done.10, f32[512]{0:T(512)S(1)} %add_rsqrt_fusion), kind=kLoop, calls=%fused_computation.5 | loop fusion | flops 11010048 | bytes 11033600 | tf_op jit(solution)/shard_map/convert_element_type | solution.py:319
  37.1 79.6 %all-gather.7.cloned.1.call-done = bf16[5376,1024]{1,0:T(8,128)(2,1)} async-done(((bf16[672,1024]{1,0:T(8,128)(2,1)}), bf16[5376,1024]{1,0:T(8,128)(2,1)}) %all-gather.7.cloned.1.call-update) | async-done | bytes 11010064 | tf_op jit(solution)/shard_map/all_gather | solution.py:312
  116.7 11.3 %fusion.33.k_ref.v_ref = f32[512,1024]{1,0:T(8,128)} fusion(bf16[512,5376]{1,0:T(8,128)(2,1)} %fusion.2, bf16[5376,1024]{1,0:T(8,128)(2,1)} %all-gather.7.cloned.1.call-done), kind=kOutput, calls=%fused_computation.70 | convolution fusion | flops 5637144576 | bytes 18612224 | tf_op jit(solution)/shard_map/dot_general | solution.py:32
  127.9 3.8 key_rows.1.own_ref
  133.6 45.6 %collective-permute-done.far_ref = bf16[2,512,512]{2,1,0:T(8,128)(2,1)S(1)} collective-permute-done((bf16[2,512,512]{2,1,0:T(8,128)(2,1)}, bf16[2,512,512]{2,1,0:T(8,128)(2,1)S(1)}, u32[]{:S(2)}, u32[]{:S(2)}) %collective-permute-start) | collective-permute-done | bytes 1048608 | tf_op jit(solution)/shard_map/ppermute | solution.py:24
  182.0 55.3 %all-gather.5.cloned.1.call-done = bf16[5376,1024]{1,0:T(8,128)(2,1)} async-done(((bf16[672,1024]{1,0:T(8,128)(2,1)}), bf16[5376,1024]{1,0:T(8,128)(2,1)}) %all-gather.5.cloned.1.call-update) | async-done | bytes 11010064 | tf_op jit(solution)/shard_map/all_gather | solution.py:313
  237.2 11.2 %fusion.32.q_ref = f32[512,1024]{1,0:T(8,128)} fusion(bf16[512,5376]{1,0:T(8,128)(2,1)} %fusion.2, bf16[5376,1024]{1,0:T(8,128)(2,1)} %all-gather.5.cloned.1.call-done), kind=kOutput, calls=%fused_computation.69 | convolution fusion | flops 5637144576 | bytes 18612224 | tf_op jit(solution)/shard_map/dot_general | solution.py:32
  248.4 25.4 %attention.1 = (bf16[512,1024]{1,0:T(8,128)(2,1)}, f32[2,512,512]{2,1,0:T(8,128)}, bf16[2,512,512]{2,1,0:T(8,128)(2,1)S(1)}, bf16[2,512,512]{2,1,0:T(8,128)(2,1)S(1)}, f32[1,128]{1,0:T(1,128)S(1)}) custom-call(s32[1]{0:T(128)} %bitcast.start_ref, s32[4]{0:T(128)S(1)} %bitcast.84, f32[512,1024]{1,0:T(8,128)} %fusion.32.q_ref, ...), custom_call_target="tpu_custom_call" | custom-call | tf_op jit(solution)/shard_map/attention/pallas_call | solution.py:256
  280.7 64.9 %collective-permute-done.3.far_ref = bf16[2,512,512]{2,1,0:T(8,128)(2,1)S(1)} collective-permute-done((bf16[2,512,512]{2,1,0:T(8,128)(2,1)S(1)}, bf16[2,512,512]{2,1,0:T(8,128)(2,1)S(1)}, u32[]{:S(2)}, u32[]{:S(2)}) %collective-permute-start.3) | collective-permute-done | bytes 1048608 | tf_op jit(solution)/shard_map/ppermute | solution.py:24
  346.6 4.7 key_grads.1
  360.9 28.6 %collective-permute-done.9 = bf16[2,168,512]{2,1,0:T(8,128)(2,1)S(1)} collective-permute-done((bf16[2,168,512]{2,1,0:T(8,128)(2,1)S(1)}, bf16[2,168,512]{2,1,0:T(8,128)(2,1)S(1)}, u32[]{:S(2)}, u32[]{:S(2)}) %collective-permute-start.9) | collective-permute-done | bytes 344096 | tf_op jit(solution)/shard_map/ppermute | solution.py:28
  389.5 10.7 %collective-permute-done.10 = bf16[2,168,512]{2,1,0:T(8,128)(2,1)S(1)} collective-permute-done((bf16[2,168,512]{2,1,0:T(8,128)(2,1)S(1)}, bf16[2,168,512]{2,1,0:T(8,128)(2,1)S(1)}, u32[]{:S(2)}, u32[]{:S(2)}) %collective-permute-start.10) | collective-permute-done | bytes 344096 | tf_op jit(solution)/shard_map/ppermute | solution.py:28
  400.5 12.8 %convolution_bitcast_fusion = f32[5376,512]{0,1:T(8,128)} fusion(bf16[512,1024]{1,0:T(8,128)(2,1)} %get-tuple-element.21, bf16[5376,1024]{1,0:T(8,128)(2,1)} %all-gather.5.cloned.1.call-done), kind=kOutput, calls=%fused_computation.10 | convolution fusion | flops 5637144576 | bytes 23068672 | tf_op jit(solution)/shard_map/dot_general | solution.py:32
  427.1 13.5 %fusion.34 = f32[5376,512]{0,1:T(8,128)} fusion(bf16[5376,1024]{1,0:T(8,128)(2,1)} %all-gather.7.cloned.1.call-done, bf16[512,1024]{1,0:T(8,128)(2,1)S(1)} %copy-done.8), kind=kOutput, calls=%fused_computation.71 | convolution fusion | flops 5637144576 | bytes 23068672 | tf_op jit(solution)/shard_map/dot_general | solution.py:32
  440.7 6.5 %fusion.5 = (f32[512]{0:T(512)S(1)}, bf16[5376,512]{0,1:T(8,128)(2,1)S(1)}) fusion(bf16[512,5376]{1,0:T(8,128)(2,1)S(1)} %bitcast.86, f32[5376]{0:T(1024)S(1)} %copy-done.10, f32[5376,512]{0,1:T(8,128)S(1)} %bitcast.88, f32[5376,512]{0,1:T(8,128)} %fusion.34), kind=kLoop, calls=%fused_computation.8 | loop fusion | flops 19267072 | bytes 33053696 | tf_op jit(solution)/shard_map/reduce_sum | solution.py:373
  474.2 80.1 %collective-permute-done.8 = f32[1,512]{1,0:T(1,128)S(1)} collective-permute-done((f32[1,512]{1,0:T(1,128)S(1)}, f32[1,512]{1,0:T(1,128)S(1)}, u32[]{:S(2)}, u32[]{:S(2)}) %collective-permute-start.8) | collective-permute-done | bytes 2080 | tf_op jit(solution)/shard_map/ppermute | solution.py:28
  554.3 8.5 %collective-permute-start.22 = (f32[2,128]{1,0:T(2,128)S(1)}, f32[2,128]{1,0:T(2,128)S(1)}, u32[]{:S(2)}, u32[]{:S(2)}) collective-permute-start(f32[2,128]{1,0:T(2,128)S(1)} %add.157), channel_id=1, source_target_pairs={{0,8},{4,12},{8,0},{12,4},{16,24},{20,28},{24,16},{28,20},{1,9},{5... | collective-permute-start | bytes 3080 | tf_op jit(solution)/shard_map/ppermute | solution.py:28
  568.7 4.7 fusion.14
  585.9 11.3 %multiply_convert_fusion = bf16[672,1024]{1,0:T(8,128)(2,1)} fusion(bf16[672,4096]{1,0:T(8,128)(2,1)} %bitcast.33, bf16[4096,1024]{1,0:T(8,128)(2,1)} %all-gather.9.cloned.1.call-done), kind=kOutput, calls=%fused_computation.24 | convolution fusion | flops 5638520832 | bytes 15269888 | tf_op jit(solution)/shard_map/dot_general | solution.py:32
  597.2 7.8 %fusion.23 = bf16[672,512]{1,0:T(8,128)(2,1)} fusion(bf16[672,4096]{1,0:T(8,128)(2,1)} %bitcast.33, bf16[4096,1024]{1,0:T(8,128)(2,1)} %all-gather.11.cloned.1.call-done), kind=kOutput, calls=%fused_computation.38 | convolution fusion | flops 2819260416 | bytes 10387456 | tf_op jit(solution)/shard_map/dot_general | solution.py:32
  605.0 6.4 %fusion.26 = bf16[672,512]{1,0:T(8,128)(2,1)} fusion(bf16[672,4096]{1,0:T(8,128)(2,1)} %bitcast.33, bf16[4096,1024]{1,0:T(8,128)(2,1)S(1)} %copy-done.11), kind=kOutput, calls=%fused_computation.39 | convolution fusion | flops 2819260416 | bytes 10387456 | tf_op jit(solution)/shard_map/dot_general | solution.py:32
  (144 shorter events, 87.4 us)
Async XLA Ops:
  7.2 109.5 %all-gather.7.cloned.1.call-start = ((), (), s32[]{:S(2)}) async-start(), calls=%async_computation.1 | async-start | bytes 12386304 | tf_op jit(solution)/shard_map/all_gather | solution.py:312
  9.8 227.5 %all-gather.5.cloned.1.call-start = ((), (), s32[]{:S(2)}) async-start(), calls=%async_computation | async-start | bytes 12386304 | tf_op jit(solution)/shard_map/all_gather | solution.py:313
  10.5 575.3 %all-gather.9.cloned.1.call-start = ((), (), s32[]{:S(2)}) async-start(), calls=%async_computation.2 | async-start | bytes 9437184 | tf_op jit(solution)/shard_map/all_gather | solution.py:349
  131.8 47.5 %collective-permute-start = (bf16[2,512,512]{2,1,0:T(8,128)(2,1)}, bf16[2,512,512]{2,1,0:T(8,128)(2,1)S(1)}, u32[]{:S(2)}, u32[]{:S(2)}) collective-permute-start(bf16[2,512,512]{2,1,0:T(8,128)(2,1)} %key_rows.1.own_ref), channel_id=1, source_target_pairs={{0,8},{4,12},{8,16},{12,20},{16,24},{20,28},{1,9},{5,13},{9,17},{1... | collective-permute-start | bytes 3145736 | tf_op jit(solution)/shard_map/ppermute | solution.py:24
  182.0 66.5 %collective-permute-start.1 = (bf16[2,512,512]{2,1,0:T(8,128)(2,1)}, bf16[2,512,512]{2,1,0:T(8,128)(2,1)}, u32[]{:S(2)}, u32[]{:S(2)}) collective-permute-start(bf16[2,512,512]{2,1,0:T(8,128)(2,1)} %broadcast_select_fusion.1), channel_id=1, source_target_pairs={{0,4},{4,0},{8,12},{12,8},{16,20},{20,16},{24,28},{28,24},{1,5},{5... | collective-permute-start | bytes 3145736 | tf_op jit(solution)/shard_map/ppermute | solution.py:28
  274.8 322.3 %all-gather.11.cloned.1.call-start = ((), (), s32[]{:S(2)}) async-start(), calls=%async_computation.3 | async-start | bytes 9437184 | tf_op jit(solution)/shard_map/all_gather | solution.py:367
  278.9 66.7 %collective-permute-start.3 = (bf16[2,512,512]{2,1,0:T(8,128)(2,1)S(1)}, bf16[2,512,512]{2,1,0:T(8,128)(2,1)S(1)}, u32[]{:S(2)}, u32[]{:S(2)}) collective-permute-start(bf16[2,512,512]{2,1,0:T(8,128)(2,1)S(1)} %get-tuple-element.69), channel_id=1, source_target_pairs={{8,0},{12,4},{16,8},{20,12},{24,16},{28,20},{9,1},{13,5},{17,9},{2... | collective-permute-start | bytes 3145736 | tf_op jit(solution)/shard_map/ppermute | solution.py:24
  354.8 34.7 %collective-permute-start.9 = (bf16[2,168,512]{2,1,0:T(8,128)(2,1)S(1)}, bf16[2,168,512]{2,1,0:T(8,128)(2,1)S(1)}, u32[]{:S(2)}, u32[]{:S(2)}) collective-permute-start(bf16[2,168,512]{2,1,0:T(8,128)(2,1)S(1)} %get-tuple-element.68), channel_id=1, source_target_pairs={{0,8},{4,12},{8,0},{12,4},{16,24},{20,28},{24,16},{28,20},{1,9},{5... | collective-permute-start | bytes 1032200 | tf_op jit(solution)/shard_map/ppermute | solution.py:28
  358.4 41.8 %collective-permute-start.10 = (bf16[2,168,512]{2,1,0:T(8,128)(2,1)S(1)}, bf16[2,168,512]{2,1,0:T(8,128)(2,1)S(1)}, u32[]{:S(2)}, u32[]{:S(2)}) collective-permute-start(bf16[2,168,512]{2,1,0:T(8,128)(2,1)S(1)} %get-tuple-element.67), channel_id=1, source_target_pairs={{0,16},{4,20},{8,24},{12,28},{16,0},{20,4},{24,8},{28,12},{1,17},{... | collective-permute-start | bytes 1032200 | tf_op jit(solution)/shard_map/ppermute | solution.py:28
  358.4 41.8 %collective-permute-start.11 = (bf16[2,168,512]{2,1,0:T(8,128)(2,1)S(1)}, bf16[2,168,512]{2,1,0:T(8,128)(2,1)S(1)}, u32[]{:S(2)}, u32[]{:S(2)}) collective-permute-start(bf16[2,168,512]{2,1,0:T(8,128)(2,1)S(1)} %get-tuple-element.66), channel_id=1, source_target_pairs={{0,24},{4,28},{8,16},{12,20},{16,8},{20,12},{24,0},{28,4},{1,25},{... | collective-permute-start | bytes 1032200 | tf_op jit(solution)/shard_map/ppermute | solution.py:28
  400.4 12.9 %collective-permute-start.12 = (bf16[4,168,512]{2,1,0:T(8,128)(2,1)S(1)}, bf16[4,168,512]{2,1,0:T(8,128)(2,1)S(1)}, u32[]{:S(2)}, u32[]{:S(2)}) collective-permute-start(bf16[4,168,512]{2,1,0:T(8,128)(2,1)S(1)} %dynamic-slice_bitcast_fusion.1), channel_id=1, source_target_pairs={{0,4},{4,0},{8,12},{12,8},{16,20},{20,16},{24,28},{28,24},{1,5},{5... | collective-permute-start | bytes 2064392 | tf_op jit(solution)/shard_map/ppermute | solution.py:28
  418.8 45.7 %collective-permute-start.13 = (bf16[168,4096]{1,0:T(8,128)(2,1)}, bf16[168,4096]{1,0:T(8,128)(2,1)}, u32[]{:S(2)}, u32[]{:S(2)}) collective-permute-start(bf16[168,4096]{1,0:T(8,128)(2,1)} %reshape.105), channel_id=1, source_target_pairs={{0,1},{1,0},{2,3},{3,2},{4,5},{5,4},{6,7},{7,6},{8,9},{9,8},{10,11... | collective-permute-start | bytes 4128776 | tf_op jit(solution)/shard_map/ppermute | solution.py:28
  420.5 48.1 %collective-permute-start.14 = (bf16[168,4096]{1,0:T(8,128)(2,1)}, bf16[168,4096]{1,0:T(8,128)(2,1)}, u32[]{:S(2)}, u32[]{:S(2)}) collective-permute-start(bf16[168,4096]{1,0:T(8,128)(2,1)} %reshape.105), channel_id=1, source_target_pairs={{0,2},{1,3},{2,0},{3,1},{4,6},{5,7},{6,4},{7,5},{8,10},{9,11},{10,... | collective-permute-start | bytes 4128776 | tf_op jit(solution)/shard_map/ppermute | solution.py:28
  426.4 25.3 %collective-permute-start.19 = (f32[2,128]{1,0:T(2,128)S(1)}, f32[2,128]{1,0:T(2,128)S(1)}, u32[]{:S(2)}, u32[]{:S(2)}) collective-permute-start(f32[2,128]{1,0:T(2,128)S(1)} %pad_maximum_fusion.3), channel_id=1, source_target_pairs={{0,1},{1,0},{2,3},{3,2},{4,5},{5,4},{6,7},{7,6},{8,9},{9,8},{10,11... | collective-permute-start | bytes 3080 | tf_op jit(solution)/shard_map/ppermute | solution.py:28
  447.2 18.8 %collective-permute-start.7 = (f32[1,512]{1,0:T(1,128)S(1)}, f32[1,512]{1,0:T(1,128)S(1)}, u32[]{:S(2)}, u32[]{:S(2)}) collective-permute-start(f32[1,512]{1,0:T(1,128)S(1)} %bitcast.98), channel_id=1, source_target_pairs={{0,1},{1,0},{2,3},{3,2},{4,5},{5,4},{6,7},{7,6},{8,9},{9,8},{10,11... | collective-permute-start | bytes 6152 | tf_op jit(solution)/shard_map/ppermute | solution.py:28
  451.8 12.1 %collective-permute-start.20 = (f32[2,128]{1,0:T(2,128)S(1)}, f32[2,128]{1,0:T(2,128)S(1)}, u32[]{:S(2)}, u32[]{:S(2)}) collective-permute-start(f32[2,128]{1,0:T(2,128)S(1)} %fusion.30), channel_id=1, source_target_pairs={{0,2},{1,3},{2,0},{3,1},{4,6},{5,7},{6,4},{7,5},{8,10},{9,11},{10,... | collective-permute-start | bytes 3080 | tf_op jit(solution)/shard_map/ppermute | solution.py:28
  459.4 103.4 %collective-permute-start.4 = (bf16[1344,512]{1,0:T(8,128)(2,1)}, bf16[1344,512]{1,0:T(8,128)(2,1)}, u32[]{:S(2)}, u32[]{:S(2)}) collective-permute-start(bf16[1344,512]{1,0:T(8,128)(2,1)} %copy.30), channel_id=1, source_target_pairs={{0,1},{1,0},{2,3},{3,2},{4,5},{5,4},{6,7},{7,6},{8,9},{9,8},{10,11... | collective-permute-start | bytes 4128776 | tf_op jit(solution)/shard_map/ppermute | solution.py:28
  463.9 100.8 %collective-permute-start.5 = (bf16[1344,512]{1,0:T(8,128)(2,1)}, bf16[1344,512]{1,0:T(8,128)(2,1)S(1)}, u32[]{:S(2)}, u32[]{:S(2)}) collective-permute-start(bf16[1344,512]{1,0:T(8,128)(2,1)} %copy.32), channel_id=1, source_target_pairs={{0,2},{1,3},{2,0},{3,1},{4,6},{5,7},{6,4},{7,5},{8,10},{9,11},{10,... | collective-permute-start | bytes 4128776 | tf_op jit(solution)/shard_map/ppermute | solution.py:28
  464.5 101.8 %collective-permute-start.6 = (bf16[1344,512]{1,0:T(8,128)(2,1)}, bf16[1344,512]{1,0:T(8,128)(2,1)}, u32[]{:S(2)}, u32[]{:S(2)}) collective-permute-start(bf16[1344,512]{1,0:T(8,128)(2,1)} %copy.34), channel_id=1, source_target_pairs={{0,3},{1,2},{2,1},{3,0},{4,7},{5,6},{6,5},{7,4},{8,11},{9,10},{10,... | collective-permute-start | bytes 4128776 | tf_op jit(solution)/shard_map/ppermute | solution.py:28
  468.6 105.0 %collective-permute-start.15 = (bf16[168,4096]{1,0:T(8,128)(2,1)}, bf16[168,4096]{1,0:T(8,128)(2,1)}, u32[]{:S(2)}, u32[]{:S(2)}) collective-permute-start(bf16[168,4096]{1,0:T(8,128)(2,1)} %reshape.105), channel_id=1, source_target_pairs={{0,3},{1,2},{2,1},{3,0},{4,7},{5,6},{6,5},{7,4},{8,11},{9,10},{10,... | collective-permute-start | bytes 4128776 | tf_op jit(solution)/shard_map/ppermute | solution.py:28
  470.2 84.1 %collective-permute-start.8 = (f32[1,512]{1,0:T(1,128)S(1)}, f32[1,512]{1,0:T(1,128)S(1)}, u32[]{:S(2)}, u32[]{:S(2)}) collective-permute-start(f32[1,512]{1,0:T(1,128)S(1)} %add.140), channel_id=1, source_target_pairs={{0,2},{1,3},{2,0},{3,1},{4,6},{5,7},{6,4},{7,5},{8,10},{9,11},{10,... | collective-permute-start | bytes 6152 | tf_op jit(solution)/shard_map/ppermute | solution.py:28
  554.3 21.8 %collective-permute-start.22 = (f32[2,128]{1,0:T(2,128)S(1)}, f32[2,128]{1,0:T(2,128)S(1)}, u32[]{:S(2)}, u32[]{:S(2)}) collective-permute-start(f32[2,128]{1,0:T(2,128)S(1)} %add.157), channel_id=1, source_target_pairs={{0,8},{4,12},{8,0},{12,4},{16,24},{20,28},{24,16},{28,20},{1,9},{5... | collective-permute-start | bytes 3080 | tf_op jit(solution)/shard_map/ppermute | solution.py:28
  576.1 4.5 collective-permute-start.23
  580.6 4.6 collective-permute-start.18
  (24 other events, 352.8 us)
Sparse Core Ops, SparseCore 0:
  10.2 106.4 all-gather.6
  118.3 118.8 all-gather.4
  275.0 126.2 all-gather.8
  402.8 80.1 all-gather.10
where the time goes:
time: 625 us; the launch traced here: 618 us
  waiting for transfers between devices  376 us (60%)
  matrix products  74.3 us (12%)
  local copies, waits for them, and re-layouts  50.3 us (8%)
  other arithmetic  35.1 us (6%)
  starting transfers between devices  34.3 us (5%)
  Pallas kernels  34 us (5%)
  between operations  14.4 us (2%)
    ppermute x22, waiting for transfers between devices, swap(): lax.ppermute(value, axis, [(s, s ^ flip) for s in range(lax.axis_size(axi...  130 us
    ppermute x2, waiting for transfers between devices, shift(): lax.ppermute(value, axis, [(s, s + steps) for s in range(initial, last)])  111 us
    all_gather x1, waiting for transfers between devices, layer(): wide_kv = lax.all_gather(key_value, 'ctx', axis=0, tiled=True)  79.6 us
    dot_general x7, matrix products, dot(): return lax.dot_general(a, b, dims, preferred_element_type=jnp.float32)  74.3 us
    all_gather x1, waiting for transfers between devices, layer(): wide_q = lax.all_gather(w_query, 'ctx', axis=0, tiled=True)  55.3 us
    ppermute x22, starting transfers between devices, swap(): lax.ppermute(value, axis, [(s, s ^ flip) for s in range(lax.axis_size(axi...  30.7 us
    pallas_call x1, Pallas kernels, attention(): pl.pallas_call(functools.partial(attention_body, rows=rows, heads=heads,...  25.4 us
  transfers between devices with their start and end apart: 28, of which 11 were waited for; matrix products, arithmetic and copies ran while one was open for 23% of the time, Pallas kernels for 1%

commit v1 on v0

--- a/solution.py
+++ b/solution.py
@@ -70,7 +70,8 @@
     pieces, _ = lax.optimization_barrier((jnp.stack(pieces), gate))
     piece, tokens = pieces.shape[2:]
     kept = lax.dynamic_index_in_dim(pieces, core, 1, keepdims=False)
-    other = swap(lax.dynamic_index_in_dim(pieces, 1 - core, 1, keepdims=False), "ctx", 1)
+    other = lax.dynamic_index_in_dim(pieces, 1 - core, 1, keepdims=False)
+    other = swap(other, "ctx", 1)
     first, second = jnp.where(core == 0, kept, other), jnp.where(core == 0, other, kept)
     both = jnp.stack([first, second], axis=1)
     bit = 1
@@ -346,12 +347,12 @@
         head_dim,
     )
 
-    all_dq = lax.all_gather(dq16, "ctx", axis=0, tiled=True)
-
     crossed = swap(d_near, "ctx", 1)
     nothing = jnp.zeros_like(crossed)
     outgoing = d_far + jnp.where(on_first_core, nothing, crossed)
     returned = shift(outgoing, "ctx", -REACH)
+    gated, returned = lax.optimization_barrier((dq16, returned))
+    all_dq = lax.all_gather(gated, "ctx", axis=0, tiled=True)
     query_part = dot(wide_q, dq16, NT)
     query_part = lax.optimization_barrier(query_part)
     dk16, dv16, k_sum = key_grads_of(
@@ -382,7 +383,8 @@
     def part_of(array, index):
         return lax.dynamic_slice_in_dim(array, index * features, features, 0)
 
-    sent = [swap(part_of(head_part, fsdp_index ^ m), "fsdp", m) for m in range(1, fsdp_count)]
+    sent = [part_of(head_part, fsdp_index ^ m) for m in range(1, fsdp_count)]
+    sent = [swap(part, "fsdp", 1 + m) for m, part in enumerate(sent)]
     d_mine = part_of(head_part, fsdp_index).astype(jnp.float32)
     for part in sent:
         d_mine = d_mine + part.astype(jnp.float32)
@@ -404,10 +406,9 @@
     k_weights = (grad_scale * dot(columns, all_dkv[:, :kv_cols])).astype(jnp.bfloat16)
     v_weights = (grad_scale * dot(columns, all_dkv[:, kv_cols:])).astype(jnp.bfloat16)
 
-    gains = everywhere(
-        jnp.concatenate([q_sum * (grad_scale * query_scale), k_sum * grad_scale], axis=0),
-        ("fsdp", "ctx"),
-    )
+    gains = jnp.concatenate([q_sum * (grad_scale * query_scale), k_sum * grad_scale], axis=0)
+    gains = everywhere(gains, ("fsdp",))
+    gains = everywhere(gains, ("ctx",))
     return (
         grad_inputs,
         q_weights,

time: 625 us -> 597 us (0.955)
  waiting for transfers between devices: 376 us -> 335 us
  starting transfers between devices: 34.3 us -> 49.6 us
    ppermute x2, waiting for transfers between devices: 111 us -> 73.7 us  [shift(): lax.ppermute(value, axis, [(s, s + steps) for s in range(initial, last)])]
    ppermute x22, starting transfers between devices: 30.7 us -> 46.4 us  [swap(): lax.ppermute(value, axis, [(s, s ^ flip) for s in range(lax.axis_size(axi...]
  transfers between devices with their start and end apart: 28 -> 28, of which waited for: 11 -> 12; matrix products, arithmetic and copies ran while one was open for 23% -> 23% of each run, Pallas kernels for 1% -> 1%
where the time goes in v1:
time: 597 us; the launch traced here: 591 us
  waiting for transfers between devices  335 us (56%)
  matrix products  74.3 us (12%)
  starting transfers between devices  49.6 us (8%)
  local copies, waits for them, and re-layouts  49.3 us (8%)
  other arithmetic  34.8 us (6%)
  Pallas kernels  33.9 us (6%)
  between operations  14.4 us (2%)
    ppermute x22, waiting for transfers between devices, swap(): lax.ppermute(value, axis, [(s, s ^ flip) for s in range(lax.axis_size(axi...  124 us
    all_gather x1, waiting for transfers between devices, layer(): wide_kv = lax.all_gather(key_value, 'ctx', axis=0, tiled=True)  80.7 us
    dot_general x7, matrix products, dot(): return lax.dot_general(a, b, dims, preferred_element_type=jnp.float32)  74.3 us
    ppermute x2, waiting for transfers between devices, shift(): lax.ppermute(value, axis, [(s, s + steps) for s in range(initial, last)])  73.7 us
    all_gather x1, waiting for transfers between devices, layer(): wide_q = lax.all_gather(w_query, 'ctx', axis=0, tiled=True)  54.7 us
    ppermute x22, starting transfers between devices, swap(): lax.ppermute(value, axis, [(s, s ^ flip) for s in range(lax.axis_size(axi...  46.4 us
    pallas_call x1, Pallas kernels, attention(): pl.pallas_call(functools.partial(attention_body, rows=rows, heads=heads,...  25.3 us
  transfers between devices with their start and end apart: 28, of which 12 were waited for; matrix products, arithmetic and copies ran while one was open for 23% of the time, Pallas kernels for 1%

profile of v1, /device:TPU:0, one launch (start us, length us, event | category | flops | bytes accessed | tf_op | source)
XLA Modules:
  0.0 591.0 jit_solution(2780183611110322755)
XLA Ops:
  10.6 3.9 fusion
  14.8 4.4 fusion.48
  19.1 8.5 %copy.28 = bf16[5376,512]{1,0:T(8,128)(2,1)} copy(bf16[5376,512]{0,1:T(8,128)(2,1)} %fusion.48) | data formatting | bytes 11010048 | tf_op jit(solution)/shard_map/convert_element_type | solution.py:325
  27.6 6.9 %fusion.2 = bf16[512,5376]{1,0:T(8,128)(2,1)} fusion(bf16[512,5376]{1,0:T(8,128)(2,1)} %param.9, f32[5376]{0:T(1024)S(1)} %copy-done.8, f32[512]{0:T(512)S(1)} %add_rsqrt_fusion), kind=kLoop, calls=%fused_computation.5 | loop fusion | flops 11010048 | bytes 11033600 | tf_op jit(solution)/shard_map/convert_element_type | solution.py:320
  36.0 80.7 %all-gather.7.cloned.1.call-done = bf16[5376,1024]{1,0:T(8,128)(2,1)} async-done(((bf16[672,1024]{1,0:T(8,128)(2,1)}), bf16[5376,1024]{1,0:T(8,128)(2,1)}) %all-gather.7.cloned.1.call-update) | async-done | bytes 11010064 | tf_op jit(solution)/shard_map/all_gather | solution.py:313
  116.7 11.3 %fusion.33.k_ref.v_ref = f32[512,1024]{1,0:T(8,128)} fusion(bf16[512,5376]{1,0:T(8,128)(2,1)} %fusion.2, bf16[5376,1024]{1,0:T(8,128)(2,1)} %all-gather.7.cloned.1.call-done), kind=kOutput, calls=%fused_computation.70 | convolution fusion | flops 5637144576 | bytes 18612224 | tf_op jit(solution)/shard_map/dot_general | solution.py:32
  127.9 3.8 key_rows.1.own_ref
  133.8 45.5 %collective-permute-done.far_ref = bf16[2,512,512]{2,1,0:T(8,128)(2,1)S(1)} collective-permute-done((bf16[2,512,512]{2,1,0:T(8,128)(2,1)}, bf16[2,512,512]{2,1,0:T(8,128)(2,1)S(1)}, u32[]{:S(2)}, u32[]{:S(2)}) %collective-permute-start) | collective-permute-done | bytes 1048608 | tf_op jit(solution)/shard_map/ppermute | solution.py:24
  182.6 54.7 %all-gather.5.cloned.1.call-done = bf16[5376,1024]{1,0:T(8,128)(2,1)} async-done(((bf16[672,1024]{1,0:T(8,128)(2,1)}), bf16[5376,1024]{1,0:T(8,128)(2,1)}) %all-gather.5.cloned.1.call-update) | async-done | bytes 11010064 | tf_op jit(solution)/shard_map/all_gather | solution.py:314
  237.2 11.2 %fusion.32.q_ref = f32[512,1024]{1,0:T(8,128)} fusion(bf16[512,5376]{1,0:T(8,128)(2,1)} %fusion.2, bf16[5376,1024]{1,0:T(8,128)(2,1)} %all-gather.5.cloned.1.call-done), kind=kOutput, calls=%fused_computation.69 | convolution fusion | flops 5637144576 | bytes 18612224 | tf_op jit(solution)/shard_map/dot_general | solution.py:32
  248.5 25.3 %attention.1 = (bf16[512,1024]{1,0:T(8,128)(2,1)}, f32[2,512,512]{2,1,0:T(8,128)}, bf16[2,512,512]{2,1,0:T(8,128)(2,1)S(1)}, bf16[2,512,512]{2,1,0:T(8,128)(2,1)S(1)}, f32[1,128]{1,0:T(1,128)S(1)}) custom-call(s32[1]{0:T(128)} %bitcast.start_ref, s32[4]{0:T(128)S(1)} %bitcast.84, f32[512,1024]{1,0:T(8,128)} %fusion.32.q_ref, ...), custom_call_target="tpu_custom_call" | custom-call | tf_op jit(solution)/shard_map/attention/pallas_call | solution.py:257
  278.9 28.2 %collective-permute-done.3.far_ref = bf16[2,512,512]{2,1,0:T(8,128)(2,1)S(1)} collective-permute-done((bf16[2,512,512]{2,1,0:T(8,128)(2,1)S(1)}, bf16[2,512,512]{2,1,0:T(8,128)(2,1)S(1)}, u32[]{:S(2)}, u32[]{:S(2)}) %collective-permute-start.3) | collective-permute-done | bytes 1048608 | tf_op jit(solution)/shard_map/ppermute | solution.py:24
  308.1 4.7 key_grads.1
  321.2 20.4 %collective-permute-done.9 = bf16[2,168,512]{2,1,0:T(8,128)(2,1)S(1)} collective-permute-done((bf16[2,168,512]{2,1,0:T(8,128)(2,1)S(1)}, bf16[2,168,512]{2,1,0:T(8,128)(2,1)S(1)}, u32[]{:S(2)}, u32[]{:S(2)}) %collective-permute-start.9) | collective-permute-done | bytes 344096 | tf_op jit(solution)/shard_map/ppermute | solution.py:28
  341.6 14.6 %collective-permute-done.10 = bf16[2,168,512]{2,1,0:T(8,128)(2,1)S(1)} collective-permute-done((bf16[2,168,512]{2,1,0:T(8,128)(2,1)S(1)}, bf16[2,168,512]{2,1,0:T(8,128)(2,1)S(1)}, u32[]{:S(2)}, u32[]{:S(2)}) %collective-permute-start.10) | collective-permute-done | bytes 344096 | tf_op jit(solution)/shard_map/ppermute | solution.py:28
  357.6 13.0 %convolution_bitcast_fusion = f32[5376,512]{0,1:T(8,128)} fusion(bf16[512,1024]{1,0:T(8,128)(2,1)} %get-tuple-element.33, bf16[5376,1024]{1,0:T(8,128)(2,1)} %all-gather.5.cloned.1.call-done), kind=kOutput, calls=%fused_computation.10 | convolution fusion | flops 5637144576 | bytes 23068672 | tf_op jit(solution)/shard_map/dot_general | solution.py:32
  384.3 13.5 %fusion.34 = f32[5376,512]{0,1:T(8,128)} fusion(bf16[5376,1024]{1,0:T(8,128)(2,1)} %all-gather.7.cloned.1.call-done, bf16[512,1024]{1,0:T(8,128)(2,1)S(1)} %copy-done.6), kind=kOutput, calls=%fused_computation.71 | convolution fusion | flops 5637144576 | bytes 23068672 | tf_op jit(solution)/shard_map/dot_general | solution.py:32
  397.8 6.5 %fusion.5 = (f32[512]{0:T(512)S(1)}, bf16[5376,512]{0,1:T(8,128)(2,1)S(1)}) fusion(bf16[512,5376]{1,0:T(8,128)(2,1)S(1)} %bitcast.86, f32[5376]{0:T(1024)S(1)} %copy-done.8, f32[5376,512]{0,1:T(8,128)S(1)} %bitcast.88, f32[5376,512]{0,1:T(8,128)} %fusion.34), kind=kLoop, calls=%fused_computation.8 | loop fusion | flops 19267072 | bytes 33053696 | tf_op jit(solution)/shard_map/reduce_sum | solution.py:374
  431.4 80.0 %collective-permute-done.8 = f32[1,512]{1,0:T(1,128)S(1)} collective-permute-done((f32[1,512]{1,0:T(1,128)S(1)}, f32[1,512]{1,0:T(1,128)S(1)}, u32[]{:S(2)}, u32[]{:S(2)}) %collective-permute-start.8) | collective-permute-done | bytes 2080 | tf_op jit(solution)/shard_map/ppermute | solution.py:28
  511.5 24.4 %collective-permute-start.22 = (f32[2,128]{1,0:T(2,128)S(1)}, f32[2,128]{1,0:T(2,128)S(1)}, u32[]{:S(2)}, u32[]{:S(2)}) collective-permute-start(f32[2,128]{1,0:T(2,128)S(1)} %add.157), channel_id=1, source_target_pairs={{0,8},{4,12},{8,0},{12,4},{16,24},{20,28},{24,16},{28,20},{1,9},{5... | collective-permute-start | bytes 3080 | tf_op jit(solution)/shard_map/ppermute | solution.py:28
  541.8 4.7 fusion.14
  559.0 7.8 %fusion.23 = bf16[672,512]{1,0:T(8,128)(2,1)} fusion(bf16[672,4096]{1,0:T(8,128)(2,1)} %bitcast.33, bf16[4096,1024]{1,0:T(8,128)(2,1)} %all-gather.11.cloned.1.call-done), kind=kOutput, calls=%fused_computation.38 | convolution fusion | flops 2819260416 | bytes 10387456 | tf_op jit(solution)/shard_map/dot_general | solution.py:32
  566.8 6.4 %fusion.26 = bf16[672,512]{1,0:T(8,128)(2,1)} fusion(bf16[672,4096]{1,0:T(8,128)(2,1)} %bitcast.33, bf16[4096,1024]{1,0:T(8,128)(2,1)S(1)} %copy-done.9), kind=kOutput, calls=%fused_computation.39 | convolution fusion | flops 2819260416 | bytes 10387456 | tf_op jit(solution)/shard_map/dot_general | solution.py:32
  573.2 11.1 %multiply_convert_fusion = bf16[672,1024]{1,0:T(8,128)(2,1)} fusion(bf16[672,4096]{1,0:T(8,128)(2,1)} %bitcast.33, bf16[4096,1024]{1,0:T(8,128)(2,1)} %all-gather.9.cloned.1.call-done), kind=kOutput, calls=%fused_computation.24 | convolution fusion | flops 5638520832 | bytes 15269888 | tf_op jit(solution)/shard_map/dot_general | solution.py:32
  (140 shorter events, 85.0 us)
Async XLA Ops:
  7.2 109.5 %all-gather.7.cloned.1.call-start = ((), (), s32[]{:S(2)}) async-start(), calls=%async_computation.1 | async-start | bytes 12386304 | tf_op jit(solution)/shard_map/all_gather | solution.py:313
  9.8 227.5 %all-gather.5.cloned.1.call-start = ((), (), s32[]{:S(2)}) async-start(), calls=%async_computation | async-start | bytes 12386304 | tf_op jit(solution)/shard_map/all_gather | solution.py:314
  10.5 548.4 %all-gather.11.cloned.1.call-start = ((), (), s32[]{:S(2)}) async-start(), calls=%async_computation.3 | async-start | bytes 9437184 | tf_op jit(solution)/shard_map/all_gather | solution.py:368
  131.8 47.5 %collective-permute-start = (bf16[2,512,512]{2,1,0:T(8,128)(2,1)}, bf16[2,512,512]{2,1,0:T(8,128)(2,1)S(1)}, u32[]{:S(2)}, u32[]{:S(2)}) collective-permute-start(bf16[2,512,512]{2,1,0:T(8,128)(2,1)} %key_rows.1.own_ref), channel_id=1, source_target_pairs={{0,8},{4,12},{8,16},{12,20},{16,24},{20,28},{1,9},{5,13},{9,17},{1... | collective-permute-start | bytes 3145736 | tf_op jit(solution)/shard_map/ppermute | solution.py:24
  182.6 65.9 %collective-permute-start.1 = (bf16[2,512,512]{2,1,0:T(8,128)(2,1)}, bf16[2,512,512]{2,1,0:T(8,128)(2,1)}, u32[]{:S(2)}, u32[]{:S(2)}) collective-permute-start(bf16[2,512,512]{2,1,0:T(8,128)(2,1)} %broadcast_select_fusion.1), channel_id=1, source_target_pairs={{0,4},{4,0},{8,12},{12,8},{16,20},{20,16},{24,28},{28,24},{1,5},{5... | collective-permute-start | bytes 3145736 | tf_op jit(solution)/shard_map/ppermute | solution.py:28
  277.6 29.5 %collective-permute-start.3 = (bf16[2,512,512]{2,1,0:T(8,128)(2,1)S(1)}, bf16[2,512,512]{2,1,0:T(8,128)(2,1)S(1)}, u32[]{:S(2)}, u32[]{:S(2)}) collective-permute-start(bf16[2,512,512]{2,1,0:T(8,128)(2,1)S(1)} %get-tuple-element.73), channel_id=1, source_target_pairs={{8,0},{12,4},{16,8},{20,12},{24,16},{28,20},{9,1},{13,5},{17,9},{2... | collective-permute-start | bytes 3145736 | tf_op jit(solution)/shard_map/ppermute | solution.py:24
  315.9 257.3 %all-gather.9.cloned.1.call-start = ((), (), s32[]{:S(2)}) async-start(), calls=%async_computation.2 | async-start | bytes 9437184 | tf_op jit(solution)/shard_map/all_gather | solution.py:355
  316.7 25.0 %collective-permute-start.9 = (bf16[2,168,512]{2,1,0:T(8,128)(2,1)S(1)}, bf16[2,168,512]{2,1,0:T(8,128)(2,1)S(1)}, u32[]{:S(2)}, u32[]{:S(2)}) collective-permute-start(bf16[2,168,512]{2,1,0:T(8,128)(2,1)S(1)} %get-tuple-element.72), channel_id=1, source_target_pairs={{0,8},{4,12},{8,0},{12,4},{16,24},{20,28},{24,16},{28,20},{1,9},{5... | collective-permute-start | bytes 1032200 | tf_op jit(solution)/shard_map/ppermute | solution.py:28
  318.5 37.8 %collective-permute-start.10 = (bf16[2,168,512]{2,1,0:T(8,128)(2,1)S(1)}, bf16[2,168,512]{2,1,0:T(8,128)(2,1)S(1)}, u32[]{:S(2)}, u32[]{:S(2)}) collective-permute-start(bf16[2,168,512]{2,1,0:T(8,128)(2,1)S(1)} %get-tuple-element.71), channel_id=1, source_target_pairs={{0,16},{4,20},{8,24},{12,28},{16,0},{20,4},{24,8},{28,12},{1,17},{... | collective-permute-start | bytes 1032200 | tf_op jit(solution)/shard_map/ppermute | solution.py:28
  318.5 38.8 %collective-permute-start.11 = (bf16[2,168,512]{2,1,0:T(8,128)(2,1)S(1)}, bf16[2,168,512]{2,1,0:T(8,128)(2,1)S(1)}, u32[]{:S(2)}, u32[]{:S(2)}) collective-permute-start(bf16[2,168,512]{2,1,0:T(8,128)(2,1)S(1)} %get-tuple-element.70), channel_id=1, source_target_pairs={{0,24},{4,28},{8,16},{12,20},{16,8},{20,12},{24,0},{28,4},{1,25},{... | collective-permute-start | bytes 1032200 | tf_op jit(solution)/shard_map/ppermute | solution.py:28
  357.5 13.1 %collective-permute-start.12 = (bf16[4,168,512]{2,1,0:T(8,128)(2,1)S(1)}, bf16[4,168,512]{2,1,0:T(8,128)(2,1)S(1)}, u32[]{:S(2)}, u32[]{:S(2)}) collective-permute-start(bf16[4,168,512]{2,1,0:T(8,128)(2,1)S(1)} %dynamic-slice_bitcast_fusion.1), channel_id=1, source_target_pairs={{0,4},{4,0},{8,12},{12,8},{16,20},{20,16},{24,28},{28,24},{1,5},{5... | collective-permute-start | bytes 2064392 | tf_op jit(solution)/shard_map/ppermute | solution.py:28
  376.1 45.6 %collective-permute-start.13 = (bf16[168,4096]{1,0:T(8,128)(2,1)}, bf16[168,4096]{1,0:T(8,128)(2,1)}, u32[]{:S(2)}, u32[]{:S(2)}) collective-permute-start(bf16[168,4096]{1,0:T(8,128)(2,1)} %reshape.105), channel_id=1, source_target_pairs={{0,1},{1,0},{2,3},{3,2},{4,5},{5,4},{6,7},{7,6},{8,9},{9,8},{10,11... | collective-permute-start | bytes 4128776 | tf_op jit(solution)/shard_map/ppermute | solution.py:28
  377.7 48.0 %collective-permute-start.14 = (bf16[168,4096]{1,0:T(8,128)(2,1)}, bf16[168,4096]{1,0:T(8,128)(2,1)}, u32[]{:S(2)}, u32[]{:S(2)}) collective-permute-start(bf16[168,4096]{1,0:T(8,128)(2,1)} %reshape.105), channel_id=1, source_target_pairs={{0,2},{1,3},{2,0},{3,1},{4,6},{5,7},{6,4},{7,5},{8,10},{9,11},{10,... | collective-permute-start | bytes 4128776 | tf_op jit(solution)/shard_map/ppermute | solution.py:28
  383.7 25.3 %collective-permute-start.19 = (f32[2,128]{1,0:T(2,128)S(1)}, f32[2,128]{1,0:T(2,128)S(1)}, u32[]{:S(2)}, u32[]{:S(2)}) collective-permute-start(f32[2,128]{1,0:T(2,128)S(1)} %pad_maximum_fusion.3), channel_id=1, source_target_pairs={{0,1},{1,0},{2,3},{3,2},{4,5},{5,4},{6,7},{7,6},{8,9},{9,8},{10,11... | collective-permute-start | bytes 3080 | tf_op jit(solution)/shard_map/ppermute | solution.py:28
  404.4 18.8 %collective-permute-start.7 = (f32[1,512]{1,0:T(1,128)S(1)}, f32[1,512]{1,0:T(1,128)S(1)}, u32[]{:S(2)}, u32[]{:S(2)}) collective-permute-start(f32[1,512]{1,0:T(1,128)S(1)} %bitcast.98), channel_id=1, source_target_pairs={{0,1},{1,0},{2,3},{3,2},{4,5},{5,4},{6,7},{7,6},{8,9},{9,8},{10,11... | collective-permute-start | bytes 6152 | tf_op jit(solution)/shard_map/ppermute | solution.py:28
  409.0 12.0 %collective-permute-start.20 = (f32[2,128]{1,0:T(2,128)S(1)}, f32[2,128]{1,0:T(2,128)S(1)}, u32[]{:S(2)}, u32[]{:S(2)}) collective-permute-start(f32[2,128]{1,0:T(2,128)S(1)} %fusion.30), channel_id=1, source_target_pairs={{0,2},{1,3},{2,0},{3,1},{4,6},{5,7},{6,4},{7,5},{8,10},{9,11},{10,... | collective-permute-start | bytes 3080 | tf_op jit(solution)/shard_map/ppermute | solution.py:28
  416.6 119.3 %collective-permute-start.4 = (bf16[1344,512]{1,0:T(8,128)(2,1)}, bf16[1344,512]{1,0:T(8,128)(2,1)}, u32[]{:S(2)}, u32[]{:S(2)}) collective-permute-start(bf16[1344,512]{1,0:T(8,128)(2,1)} %copy.30), channel_id=1, source_target_pairs={{0,1},{1,0},{2,3},{3,2},{4,5},{5,4},{6,7},{7,6},{8,9},{9,8},{10,11... | collective-permute-start | bytes 4128776 | tf_op jit(solution)/shard_map/ppermute | solution.py:28
  421.1 116.6 %collective-permute-start.5 = (bf16[1344,512]{1,0:T(8,128)(2,1)}, bf16[1344,512]{1,0:T(8,128)(2,1)S(1)}, u32[]{:S(2)}, u32[]{:S(2)}) collective-permute-start(bf16[1344,512]{1,0:T(8,128)(2,1)} %copy.32), channel_id=1, source_target_pairs={{0,2},{1,3},{2,0},{3,1},{4,6},{5,7},{6,4},{7,5},{8,10},{9,11},{10,... | collective-permute-start | bytes 4128776 | tf_op jit(solution)/shard_map/ppermute | solution.py:28
  421.7 117.6 %collective-permute-start.6 = (bf16[1344,512]{1,0:T(8,128)(2,1)}, bf16[1344,512]{1,0:T(8,128)(2,1)}, u32[]{:S(2)}, u32[]{:S(2)}) collective-permute-start(bf16[1344,512]{1,0:T(8,128)(2,1)} %copy.34), channel_id=1, source_target_pairs={{0,3},{1,2},{2,1},{3,0},{4,7},{5,6},{6,5},{7,4},{8,11},{9,10},{10,... | collective-permute-start | bytes 4128776 | tf_op jit(solution)/shard_map/ppermute | solution.py:28
  425.8 120.9 %collective-permute-start.15 = (bf16[168,4096]{1,0:T(8,128)(2,1)}, bf16[168,4096]{1,0:T(8,128)(2,1)}, u32[]{:S(2)}, u32[]{:S(2)}) collective-permute-start(bf16[168,4096]{1,0:T(8,128)(2,1)} %reshape.105), channel_id=1, source_target_pairs={{0,3},{1,2},{2,1},{3,0},{4,7},{5,6},{6,5},{7,4},{8,11},{9,10},{10,... | collective-permute-start | bytes 4128776 | tf_op jit(solution)/shard_map/ppermute | solution.py:28
  427.4 84.1 %collective-permute-start.8 = (f32[1,512]{1,0:T(1,128)S(1)}, f32[1,512]{1,0:T(1,128)S(1)}, u32[]{:S(2)}, u32[]{:S(2)}) collective-permute-start(f32[1,512]{1,0:T(1,128)S(1)} %add.140), channel_id=1, source_target_pairs={{0,2},{1,3},{2,0},{3,1},{4,6},{5,7},{6,4},{7,5},{8,10},{9,11},{10,... | collective-permute-start | bytes 6152 | tf_op jit(solution)/shard_map/ppermute | solution.py:28
  511.5 37.8 %collective-permute-start.22 = (f32[2,128]{1,0:T(2,128)S(1)}, f32[2,128]{1,0:T(2,128)S(1)}, u32[]{:S(2)}, u32[]{:S(2)}) collective-permute-start(f32[2,128]{1,0:T(2,128)S(1)} %add.157), channel_id=1, source_target_pairs={{0,8},{4,12},{8,0},{12,4},{16,24},{20,28},{24,16},{28,20},{1,9},{5... | collective-permute-start | bytes 3080 | tf_op jit(solution)/shard_map/ppermute | solution.py:28
  549.2 4.5 collective-permute-start.23
  553.7 4.6 collective-permute-start.18
  (22 other events, 278.5 us)
Sparse Core Ops, SparseCore 0:
  10.2 106.4 all-gather.6
  118.3 118.8 all-gather.4
  316.1 103.5 all-gather.10
  421.1 81.3 all-gather.8

commit v2 on v1

--- a/solution.py
+++ b/solution.py
@@ -49,16 +49,16 @@
     return lax.dynamic_index_in_dim(blocks, lax.axis_index("fsdp"), 2, keepdims=False)
 
 
-def start_columns(blocks):
-    chips = blocks.shape[0]
+def pick_columns(blocks):
     chip = lax.axis_index("ctx") // 2
-    pieces = []
-    for m in range(chips):
-        piece = lax.dynamic_index_in_dim(blocks, chip ^ m, 0, keepdims=False)
-        if m:
-            piece = swap(piece, "ctx", 2 * m)
-        pieces.append(piece)
-    return pieces
+    return [
+        lax.dynamic_index_in_dim(blocks, chip ^ m, 0, keepdims=False)
+        for m in range(blocks.shape[0])
+    ]
+
+
+def start_columns(pieces):
+    return pieces[:1] + [swap(piece, "ctx", 2 + 2 * m) for m, piece in enumerate(pieces[1:])]
 
 
 def finish_columns(pieces, gate):
@@ -243,23 +243,35 @@
             ref[1] = dv_ref[pl.ds(at * tokens, tokens), :].astype(ref.dtype)
 
 
-def attention(start, ends, q_raw, go, own, near, far, mult, kv_heads, head_dim):
+def attention_rest(start, ends, q, go, own, near, far, mult, *refs, **sizes):
+    attention_body(start, ends, q, go, own, near, far, mult, *refs[3:], **sizes)
+
+
+def attention(start, ends, q_raw, go, own, near, far, mult, kv_heads, head_dim, skip, carry):
     tokens, q_cols = q_raw.shape
     heads = q_cols // (kv_heads * head_dim)
     rows = min(256, tokens)
     steps = tokens // rows
     span = WIN + rows
-    stacked = pl.BlockSpec((2, tokens, head_dim), lambda g, s, *_: (0, 0, g))
+    stacked = pl.BlockSpec((2, tokens, head_dim), lambda g, s, *_: (0, 0, skip + g))
     by_query = pl.BlockSpec((rows, heads * head_dim), lambda g, s, *_: (s, g))
+    by_skipped = pl.BlockSpec((rows, heads * head_dim), lambda g, s, *_: (s, skip + g))
+    whole = pl.BlockSpec(memory_space=pl.ANY)
     row = pl.BlockSpec((1, head_dim), lambda g, s, *_: (0, 0))
     half = jax.ShapeDtypeStruct(own.shape, jnp.bfloat16)
     keys = WIN + tokens
     return pl.pallas_call(
-        functools.partial(attention_body, rows=rows, heads=heads, segments=ends.shape[0]),
+        functools.partial(
+            attention_rest if carry else attention_body,
+            rows=rows,
+            heads=heads,
+            segments=ends.shape[0],
+        ),
         grid_spec=pltpu.PrefetchScalarGridSpec(
             num_scalar_prefetch=2,
             grid=(kv_heads, steps),
-            in_specs=[by_query, by_query, stacked, stacked, stacked, row],
+            in_specs=[by_query, by_skipped, stacked, stacked, stacked, row]
+            + [whole for _ in carry],
             out_specs=(by_query, stacked, stacked, stacked, row),
             scratch_shapes=[
                 pltpu.VMEM((steps, span, rows), jnp.float32),
@@ -281,8 +293,9 @@
         compiler_params=pltpu.CompilerParams(
             dimension_semantics=("arbitrary", "arbitrary"), vmem_limit_bytes=48 << 20
         ),
+        input_output_aliases={8 + i: 1 + i for i in range(len(carry))},
         name="attention",
-    )(start, ends, q_raw, go, own, near, far, mult)
+    )(start, ends, q_raw, go, own, near, far, mult, *carry)
 
 
 def layer(
@@ -311,7 +324,9 @@
 
     key_value = jnp.concatenate([key_projection, value_projection], axis=1)
     wide_kv = lax.all_gather(key_value, "ctx", axis=0, tiled=True)
-    wide_q = lax.all_gather(w_query, "ctx", axis=0, tiled=True)
+    half = w_query.shape[1] // 2
+    wide_qa = lax.all_gather(w_query[:, :half], "ctx", axis=0, tiled=True)
+    wide_qb = lax.all_gather(w_query[:, half:], "ctx", axis=0, tiled=True)
 
     widened = inputs.astype(jnp.float32)
     turned = jnp.transpose(inputs)
@@ -330,30 +345,39 @@
     picked = jnp.where(on_first_core, own, far)
     near = swap(picked, "ctx", 1)
 
-    blocks, _ = lax.optimization_barrier((blocks, wide_q))
-    pieces = start_columns(blocks)
-    q_raw = dot(normed, wide_q)
     query_multiplier = (q_gain * query_scale)[None, :]
-    dq16, d_own, d_near, d_far, q_sum = attention(
-        jnp.full((1,), ctx_index * tokens, jnp.int32),
-        jnp.cumsum(half_lengths).astype(jnp.int32),
-        q_raw,
-        output_cotangent,
-        own,
-        near,
-        far,
-        query_multiplier,
-        kv_heads,
-        head_dim,
-    )
+
+    def attend(q_raw, skip, carry):
+        return attention(
+            jnp.full((1,), ctx_index * tokens, jnp.int32),
+            jnp.cumsum(half_lengths).astype(jnp.int32),
+            q_raw,
+            output_cotangent,
+            own,
+            near,
+            far,
+            query_multiplier,
+            kv_heads // 2,
+            head_dim,
+            skip,
+            carry,
+        )
+
+    dqa, *carry, qa_sum = attend(dot(normed, wide_qa), 0, ())
+    all_dqa = lax.all_gather(dqa, "ctx", axis=0, tiled=True)
+    blocks, _ = lax.optimization_barrier((blocks, dqa))
+    pieces = pick_columns(blocks)
+    pieces = start_columns(pieces)
+    dqb, d_own, d_near, d_far, qb_sum = attend(dot(normed, wide_qb), kv_heads // 2, carry)
+    q_sum = qa_sum + qb_sum
 
     crossed = swap(d_near, "ctx", 1)
     nothing = jnp.zeros_like(crossed)
     outgoing = d_far + jnp.where(on_first_core, nothing, crossed)
     returned = shift(outgoing, "ctx", -REACH)
-    gated, returned = lax.optimization_barrier((dq16, returned))
-    all_dq = lax.all_gather(gated, "ctx", axis=0, tiled=True)
-    query_part = dot(wide_q, dq16, NT)
+    gated, returned = lax.optimization_barrier((dqb, returned))
+    all_dqb = lax.all_gather(gated, "ctx", axis=0, tiled=True)
+    query_part = dot(wide_qa, dqa, NT) + dot(wide_qb, dqb, NT)
     query_part = lax.optimization_barrier(query_part)
     dk16, dv16, k_sum = key_grads_of(
         d_own,
@@ -367,7 +391,7 @@
     dkv16 = jnp.concatenate([dk16, dv16], axis=1)
     all_dkv = lax.all_gather(dkv16, "ctx", axis=0, tiled=True)
 
-    columns = finish_columns(pieces, dq16)
+    columns = finish_columns(pieces, dqb)
 
     head_part = (query_part + dot(wide_kv, dkv16, NT)).astype(jnp.bfloat16)
     row_dot = everywhere(
@@ -402,7 +426,13 @@
         0,
     )
 
-    q_weights = (grad_scale * dot(columns, all_dq)).astype(jnp.bfloat16)
+    q_weights = jnp.concatenate(
+        [
+            (grad_scale * dot(columns, part)).astype(jnp.bfloat16)
+            for part in (all_dqa, all_dqb)
+        ],
+        axis=1,
+    )
     k_weights = (grad_scale * dot(columns, all_dkv[:, :kv_cols])).astype(jnp.bfloat16)
     v_weights = (grad_scale * dot(columns, all_dkv[:, kv_cols:])).astype(jnp.bfloat16)
 

time: 597 us -> 616 us (1.032)
  waiting for transfers between devices: 335 us -> 315 us
  starting transfers between devices: 49.6 us -> 69.2 us
  matrix products: 74.3 us -> 81.7 us
    ppermute x22, waiting for transfers between devices: 124 us -> 101 us  [swap(): lax.ppermute(value, axis, [(s, s ^ flip) for s in range(lax.axis_size(axi...]
    ppermute x22, starting transfers between devices: 46.4 us -> 65.6 us  [swap(): lax.ppermute(value, axis, [(s, s ^ flip) for s in range(lax.axis_size(axi...]
    ppermute x2, waiting for transfers between devices: 73.7 us -> 85.6 us  [shift(): lax.ppermute(value, axis, [(s, s + steps) for s in range(initial, last)])]
    dot_general x7 -> x10, matrix products: 74.3 us -> 81.7 us  [dot(): return lax.dot_general(a, b, dims, preferred_element_type=jnp.float32)]
    all_gather x2 -> x4, waiting for transfers between devices: 54.7 us -> 48.8 us  [the longest x1 38.1 us: layer(): wide_qb = lax.all_gather(w_query[:, half:], 'ctx', axis=0, tiled=True)]
    pallas_call x1 -> x2, Pallas kernels: 25.3 us -> 29 us  [attention(): pl.pallas_call(functools.partial(attention_rest if carry else attention_b...]
  transfers between devices with their start and end apart: 28 -> 30, of which waited for: 12 -> 14; matrix products, arithmetic and copies ran while one was open for 23% -> 25% of each run, Pallas kernels for 1% -> 6%
where the time goes in v2:
time: 616 us; the launch traced here: 609 us
  waiting for transfers between devices  315 us (51%)
  matrix products  81.7 us (13%)
  starting transfers between devices  69.2 us (11%)
  local copies, waits for them, and re-layouts  50.5 us (8%)
  other arithmetic  39.6 us (6%)
  Pallas kernels  37.7 us (6%)
  between operations  15 us (2%)
    ppermute x22, waiting for transfers between devices, swap(): lax.ppermute(value, axis, [(s, s ^ flip) for s in range(lax.axis_size(axi...  101 us
    ppermute x2, waiting for transfers between devices, shift(): lax.ppermute(value, axis, [(s, s + steps) for s in range(initial, last)])  85.6 us
    dot_general x10, matrix products, dot(): return lax.dot_general(a, b, dims, preferred_element_type=jnp.float32)  81.7 us
    all_gather x1, waiting for transfers between devices, layer(): wide_kv = lax.all_gather(key_value, 'ctx', axis=0, tiled=True)  78.9 us
    ppermute x22, starting transfers between devices, swap(): lax.ppermute(value, axis, [(s, s ^ flip) for s in range(lax.axis_size(axi...  65.6 us
    all_gather x1, waiting for transfers between devices, layer(): wide_qb = lax.all_gather(w_query[:, half:], 'ctx', axis=0, tiled=True)  38.1 us
    pallas_call x2, Pallas kernels, attention(): pl.pallas_call(functools.partial(attention_rest if carry else attention_b...  29 us
  transfers between devices with their start and end apart: 30, of which 14 were waited for; matrix products, arithmetic and copies ran while one was open for 25% of the time, Pallas kernels for 6%

profile of v2, /device:TPU:0, one launch (start us, length us, event | category | flops | bytes accessed | tf_op | source)
XLA Modules:
  0.0 609.0 jit_solution(6530909851778668354)
XLA Ops:
  20.4 8.0 %copy.31 = bf16[5376,512]{1,0:T(8,128)(2,1)} copy(bf16[5376,512]{0,1:T(8,128)(2,1)} %fusion.59) | data formatting | bytes 11010048 | tf_op jit(solution)/shard_map/convert_element_type | solution.py:340
  28.4 6.8 %fusion.2 = bf16[512,5376]{1,0:T(8,128)(2,1)} fusion(bf16[512,5376]{1,0:T(8,128)(2,1)} %param.9, f32[5376]{0:T(1024)S(1)} %copy-done.18, f32[512]{0:T(512)S(1)} %add_rsqrt_fusion), kind=kLoop, calls=%fused_computation.5 | loop fusion | flops 11010048 | bytes 11033600 | tf_op jit(solution)/shard_map/convert_element_type | solution.py:335
  37.8 78.9 %all-gather.9.cloned.1.call-done = bf16[5376,1024]{1,0:T(8,128)(2,1)} async-done(((bf16[672,1024]{1,0:T(8,128)(2,1)}), bf16[5376,1024]{1,0:T(8,128)(2,1)}) %all-gather.9.cloned.1.call-update) | async-done | bytes 11010064 | tf_op jit(solution)/shard_map/all_gather | solution.py:326
  116.7 11.2 %fusion.36.k_ref.v_ref = f32[512,1024]{1,0:T(8,128)} fusion(bf16[512,5376]{1,0:T(8,128)(2,1)} %fusion.2, bf16[5376,1024]{1,0:T(8,128)(2,1)} %all-gather.9.cloned.1.call-done), kind=kOutput, calls=%fused_computation.75 | convolution fusion | flops 5637144576 | bytes 18612224 | tf_op jit(solution)/shard_map/dot_general | solution.py:32
  133.8 45.4 %collective-permute-done.far_ref.far = bf16[2,512,512]{2,1,0:T(8,128)(2,1)S(1)} collective-permute-done((bf16[2,512,512]{2,1,0:T(8,128)(2,1)}, bf16[2,512,512]{2,1,0:T(8,128)(2,1)S(1)}, u32[]{:S(2)}, u32[]{:S(2)}) %collective-permute-start) | collective-permute-done | bytes 1048608 | tf_op jit(solution)/shard_map/ppermute | solution.py:24
  182.0 10.7 %all-gather.7.cloned.1.call-done = bf16[5376,512]{1,0:T(8,128)(2,1)} async-done(((bf16[672,512]{1,0:T(8,128)(2,1)}), bf16[5376,512]{1,0:T(8,128)(2,1)}) %all-gather.7.cloned.1.call-update) | async-done | bytes 5505040 | tf_op jit(solution)/shard_map/all_gather | solution.py:328
  200.3 14.5 %attention.2 = (bf16[512,512]{1,0:T(8,128)(2,1)S(1)}, f32[2,512,512]{2,1,0:T(8,128)}, bf16[2,512,512]{2,1,0:T(8,128)(2,1)S(1)}, bf16[2,512,512]{2,1,0:T(8,128)(2,1)S(1)}, f32[1,128]{1,0:T(1,128)S(1)}) custom-call(s32[1]{0:T(128)} %bitcast.start_ref.start, s32[4]{0:T(128)S(1)} %bitcast.90, f32[512,512]{1,0:T(8,128)S(1)} %fusion.35.q_ref, ...), custom_call_target="tpu_custom_call" | custom-call | tf_op jit(solution)/shard_map/attention/pallas_call | solution.py:263
  216.6 38.1 %all-gather.11.cloned.1.call-done = bf16[5376,512]{1,0:T(8,128)(2,1)} async-done(((bf16[672,512]{1,0:T(8,128)(2,1)}), bf16[5376,512]{1,0:T(8,128)(2,1)}) %all-gather.11.cloned.1.call-update) | async-done | bytes 5505040 | tf_op jit(solution)/shard_map/all_gather | solution.py:329
  254.8 6.8 %fusion.37.q = f32[512,512]{1,0:T(8,128)S(1)} fusion(bf16[512,5376]{1,0:T(8,128)(2,1)} %fusion.2, bf16[5376,512]{1,0:T(8,128)(2,1)} %all-gather.11.cloned.1.call-done), kind=kOutput, calls=%fused_computation.76 | convolution fusion | flops 2818572288 | bytes 12058624 | tf_op jit(solution)/shard_map/dot_general | solution.py:32
  261.6 14.6 %attention.3 = (bf16[512,512]{1,0:T(8,128)(2,1)S(1)}, f32[2,512,512]{2,1,0:T(8,128)}, bf16[2,512,512]{2,1,0:T(8,128)(2,1)S(1)}, bf16[2,512,512]{2,1,0:T(8,128)(2,1)S(1)}, f32[1,128]{1,0:T(1,128)S(1)}) custom-call(s32[1]{0:T(128)} %bitcast.start_ref.start, s32[4]{0:T(128)S(1)} %bitcast.91, ...), custom_call_target="tpu_custom_call", output_to_operand_aliasing={{1}: (8, {}), {2}: (9, {}), {3}: (10, {})} | custom-call | tf_op jit(solution)/shard_map/attention/pallas_call | solution.py:263
  281.4 40.2 %collective-permute-done.3.far_ref = bf16[2,512,512]{2,1,0:T(8,128)(2,1)S(1)} collective-permute-done((bf16[2,512,512]{2,1,0:T(8,128)(2,1)S(1)}, bf16[2,512,512]{2,1,0:T(8,128)(2,1)S(1)}, u32[]{:S(2)}, u32[]{:S(2)}) %collective-permute-start.3) | collective-permute-done | bytes 1048608 | tf_op jit(solution)/shard_map/ppermute | solution.py:24
  335.5 8.3 %fusion.38 = f32[512,5376]{1,0:T(8,128)} fusion(bf16[512,512]{1,0:T(8,128)(2,1)S(1)} %copy-done.5, bf16[5376,512]{1,0:T(8,128)(2,1)} %all-gather.11.cloned.1.call-done), kind=kOutput, calls=%fused_computation.77 | convolution fusion | flops 2818572288 | bytes 17039360 | tf_op jit(solution)/shard_map/dot_general | solution.py:32
  343.8 20.3 %collective-permute-done.9 = bf16[2,168,512]{2,1,0:T(8,128)(2,1)S(1)} collective-permute-done((bf16[2,168,512]{2,1,0:T(8,128)(2,1)S(1)}, bf16[2,168,512]{2,1,0:T(8,128)(2,1)S(1)}, u32[]{:S(2)}, u32[]{:S(2)}) %collective-permute-start.9) | collective-permute-done | bytes 344096 | tf_op jit(solution)/shard_map/ppermute | solution.py:28
  370.4 10.0 %collective-permute-done.11 = bf16[2,168,512]{2,1,0:T(8,128)(2,1)S(1)} collective-permute-done((bf16[2,168,512]{2,1,0:T(8,128)(2,1)S(1)}, bf16[2,168,512]{2,1,0:T(8,128)(2,1)S(1)}, u32[]{:S(2)}, u32[]{:S(2)}) %collective-permute-start.11) | collective-permute-done | bytes 344096 | tf_op jit(solution)/shard_map/ppermute | solution.py:28
  380.8 8.0 %add_bitcast_fusion = f32[5376,512]{0,1:T(8,128)S(1)} fusion(f32[512,5376]{1,0:T(8,128)} %fusion.38, bf16[512,512]{1,0:T(8,128)(2,1)S(1)} %copy-done.3, bf16[5376,512]{1,0:T(8,128)(2,1)} %all-gather.7.cloned.1.call-done), kind=kOutput, calls=%fused_computation.10 | convolution fusion | flops 2821324800 | bytes 28049408 | tf_op jit(solution)/shard_map/dot_general | solution.py:32
  392.0 12.9 %fusion.39 = f32[5376,512]{0,1:T(8,128)} fusion(bf16[5376,1024]{1,0:T(8,128)(2,1)} %all-gather.9.cloned.1.call-done, bf16[512,1024]{1,0:T(8,128)(2,1)S(1)} %copy-done.15), kind=kOutput, calls=%fused_computation.78 | convolution fusion | flops 5637144576 | bytes 23068672 | tf_op jit(solution)/shard_map/dot_general | solution.py:32
  427.1 16.9 %collective-permute-start.22 = (f32[2,128]{1,0:T(2,128)S(1)}, f32[2,128]{1,0:T(2,128)S(1)}, u32[]{:S(2)}, u32[]{:S(2)}) collective-permute-start(f32[2,128]{1,0:T(2,128)S(1)} %add.169), channel_id=1, source_target_pairs={{0,8},{4,12},{8,0},{12,4},{16,24},{20,28},{24,16},{28,20},{1,9},{5... | collective-permute-start | bytes 3080 | tf_op jit(solution)/shard_map/ppermute | solution.py:28
  450.8 30.3 %collective-permute-done.7 = f32[1,512]{1,0:T(1,128)S(1)} collective-permute-done((f32[1,512]{1,0:T(1,128)S(1)}, f32[1,512]{1,0:T(1,128)S(1)}, u32[]{:S(2)}, u32[]{:S(2)}) %collective-permute-start.7) | collective-permute-done | bytes 2080 | tf_op jit(solution)/shard_map/ppermute | solution.py:28
  485.5 16.6 %collective-permute-start.23 = (f32[2,128]{1,0:T(2,128)S(1)}, f32[2,128]{1,0:T(2,128)S(1)}, u32[]{:S(2)}, u32[]{:S(2)}) collective-permute-start(f32[2,128]{1,0:T(2,128)S(1)} %add.170), channel_id=1, source_target_pairs={{0,16},{4,20},{8,24},{12,28},{16,0},{20,4},{24,8},{28,12},{1,17},{... | collective-permute-start | bytes 3080 | tf_op jit(solution)/shard_map/ppermute | solution.py:28
  521.8 12.3 %collective-permute-start.17 = (f32[1344]{0:T(1024)S(1)}, f32[1344]{0:T(1024)S(1)}, u32[]{:S(2)}, u32[]{:S(2)}) collective-permute-start(f32[1344]{0:T(1024)S(1)} %fusion.31), channel_id=1, source_target_pairs={{0,8},{4,12},{8,0},{12,4},{16,24},{20,28},{24,16},{28,20},{1,9},{5... | collective-permute-start | bytes 16136 | tf_op jit(solution)/shard_map/ppermute | solution.py:28
  534.1 28.5 %collective-permute-done.14 = bf16[168,4096]{1,0:T(8,128)(2,1)} collective-permute-done((bf16[168,4096]{1,0:T(8,128)(2,1)}, bf16[168,4096]{1,0:T(8,128)(2,1)}, u32[]{:S(2)}, u32[]{:S(2)}) %collective-permute-start.14) | collective-permute-done | bytes 1376288 | tf_op jit(solution)/shard_map/ppermute | solution.py:28
  572.8 6.8 %fusion.23 = bf16[672,512]{1,0:T(8,128)(2,1)S(1)} fusion(bf16[672,4096]{1,0:T(8,128)(2,1)} %bitcast.95, bf16[4096,512]{1,0:T(8,128)(2,1)} %all-gather.13.cloned.1.call-done), kind=kOutput, calls=%fused_computation.40 | convolution fusion | flops 2819260416 | bytes 10387456 | tf_op jit(solution)/shard_map/dot_general | solution.py:32
  579.6 6.8 %fusion.24 = bf16[672,512]{1,0:T(8,128)(2,1)S(1)} fusion(bf16[672,4096]{1,0:T(8,128)(2,1)} %bitcast.96, bf16[4096,512]{1,0:T(8,128)(2,1)} %all-gather.15.cloned.1.call-done), kind=kOutput, calls=%fused_computation.41 | convolution fusion | flops 2819260416 | bytes 10387456 | tf_op jit(solution)/shard_map/dot_general | solution.py:32
  587.7 7.8 %fusion.25 = bf16[672,512]{1,0:T(8,128)(2,1)} fusion(bf16[672,4096]{1,0:T(8,128)(2,1)} %bitcast.97, bf16[4096,1024]{1,0:T(8,128)(2,1)} %all-gather.17.cloned.1.call-done), kind=kOutput, calls=%fused_computation.42 | convolution fusion | flops 2819260416 | bytes 10387456 | tf_op jit(solution)/shard_map/dot_general | solution.py:32
  (165 shorter events, 133.3 us)
Async XLA Ops:
  7.2 109.5 %all-gather.9.cloned.1.call-start = ((), (), s32[]{:S(2)}) async-start(), calls=%async_computation.1 | async-start | bytes 12386304 | tf_op jit(solution)/shard_map/all_gather | solution.py:326
  9.9 182.7 %all-gather.7.cloned.1.call-start = ((), (), s32[]{:S(2)}) async-start(), calls=%async_computation | async-start | bytes 6193152 | tf_op jit(solution)/shard_map/all_gather | solution.py:328
  11.2 243.6 %all-gather.11.cloned.1.call-start = ((), (), s32[]{:S(2)}) async-start(), calls=%async_computation.2 | async-start | bytes 6193152 | tf_op jit(solution)/shard_map/all_gather | solution.py:329
  11.9 560.8 %all-gather.13.cloned.1.call-start = ((), (), s32[]{:S(2)}) async-start(), calls=%async_computation.3 | async-start | bytes 4718592 | tf_op jit(solution)/shard_map/all_gather | solution.py:367
  131.7 47.5 %collective-permute-start = (bf16[2,512,512]{2,1,0:T(8,128)(2,1)}, bf16[2,512,512]{2,1,0:T(8,128)(2,1)S(1)}, u32[]{:S(2)}, u32[]{:S(2)}) collective-permute-start(bf16[2,512,512]{2,1,0:T(8,128)(2,1)} %key_rows.1.own_ref.own), channel_id=1, source_target_pairs={{0,8},{4,12},{8,16},{12,20},{16,24},{20,28},{1,9},{5,13},{9,17},{1... | collective-permute-start | bytes 3145736 | tf_op jit(solution)/shard_map/ppermute | solution.py:24
  181.9 17.4 %collective-permute-start.1 = (bf16[2,512,512]{2,1,0:T(8,128)(2,1)}, bf16[2,512,512]{2,1,0:T(8,128)(2,1)S(1)}, u32[]{:S(2)}, u32[]{:S(2)}) collective-permute-start(bf16[2,512,512]{2,1,0:T(8,128)(2,1)} %broadcast_select_fusion.1), channel_id=1, source_target_pairs={{0,4},{4,0},{8,12},{12,8},{16,20},{20,16},{24,28},{28,24},{1,5},{5... | collective-permute-start | bytes 3145736 | tf_op jit(solution)/shard_map/ppermute | solution.py:28
  216.6 363.0 %all-gather.15.cloned.1.call-start = ((), (), s32[]{:S(2)}) async-start(), calls=%async_computation.4 | async-start | bytes 4718592 | tf_op jit(solution)/shard_map/all_gather | solution.py:379
  280.1 41.5 %collective-permute-start.3 = (bf16[2,512,512]{2,1,0:T(8,128)(2,1)S(1)}, bf16[2,512,512]{2,1,0:T(8,128)(2,1)S(1)}, u32[]{:S(2)}, u32[]{:S(2)}) collective-permute-start(bf16[2,512,512]{2,1,0:T(8,128)(2,1)S(1)} %get-tuple-element.85), channel_id=1, source_target_pairs={{8,0},{12,4},{16,8},{20,12},{24,16},{28,20},{9,1},{13,5},{17,9},{2... | collective-permute-start | bytes 3145736 | tf_op jit(solution)/shard_map/ppermute | solution.py:24
  321.6 266.1 %all-gather.17.cloned.1.call-start = ((), (), s32[]{:S(2)}) async-start(), calls=%async_computation.5 | async-start | bytes 9437184 | tf_op jit(solution)/shard_map/all_gather | solution.py:392
  331.1 33.1 %collective-permute-start.9 = (bf16[2,168,512]{2,1,0:T(8,128)(2,1)S(1)}, bf16[2,168,512]{2,1,0:T(8,128)(2,1)S(1)}, u32[]{:S(2)}, u32[]{:S(2)}) collective-permute-start(bf16[2,168,512]{2,1,0:T(8,128)(2,1)S(1)} %get-tuple-element.82), channel_id=1, source_target_pairs={{0,8},{4,12},{8,0},{12,4},{16,24},{20,28},{24,16},{28,20},{1,9},{5... | collective-permute-start | bytes 1032200 | tf_op jit(solution)/shard_map/ppermute | solution.py:28
  332.9 37.5 %collective-permute-start.10 = (bf16[2,168,512]{2,1,0:T(8,128)(2,1)S(1)}, bf16[2,168,512]{2,1,0:T(8,128)(2,1)S(1)}, u32[]{:S(2)}, u32[]{:S(2)}) collective-permute-start(bf16[2,168,512]{2,1,0:T(8,128)(2,1)S(1)} %get-tuple-element.81), channel_id=1, source_target_pairs={{0,16},{4,20},{8,24},{12,28},{16,0},{20,4},{24,8},{28,12},{1,17},{... | collective-permute-start | bytes 1032200 | tf_op jit(solution)/shard_map/ppermute | solution.py:28
  333.7 46.8 %collective-permute-start.11 = (bf16[2,168,512]{2,1,0:T(8,128)(2,1)S(1)}, bf16[2,168,512]{2,1,0:T(8,128)(2,1)S(1)}, u32[]{:S(2)}, u32[]{:S(2)}) collective-permute-start(bf16[2,168,512]{2,1,0:T(8,128)(2,1)S(1)} %get-tuple-element.80), channel_id=1, source_target_pairs={{0,24},{4,28},{8,16},{12,20},{16,8},{20,12},{24,0},{28,4},{1,25},{... | collective-permute-start | bytes 1032200 | tf_op jit(solution)/shard_map/ppermute | solution.py:28
  390.5 21.2 %collective-permute-start.19 = (f32[2,128]{1,0:T(2,128)S(1)}, f32[2,128]{1,0:T(2,128)S(1)}, u32[]{:S(2)}, u32[]{:S(2)}) collective-permute-start(f32[2,128]{1,0:T(2,128)S(1)} %pad_maximum_fusion.4), channel_id=1, source_target_pairs={{0,1},{1,0},{2,3},{3,2},{4,5},{5,4},{6,7},{7,6},{8,9},{9,8},{10,11... | collective-permute-start | bytes 3080 | tf_op jit(solution)/shard_map/ppermute | solution.py:28
  411.7 14.1 %collective-permute-start.20 = (f32[2,128]{1,0:T(2,128)S(1)}, f32[2,128]{1,0:T(2,128)S(1)}, u32[]{:S(2)}, u32[]{:S(2)}) collective-permute-start(f32[2,128]{1,0:T(2,128)S(1)} %fusion.32), channel_id=1, source_target_pairs={{0,2},{1,3},{2,0},{3,1},{4,6},{5,7},{6,4},{7,5},{8,10},{9,11},{10,... | collective-permute-start | bytes 3080 | tf_op jit(solution)/shard_map/ppermute | solution.py:28
  419.1 85.5 %collective-permute-start.4 = (bf16[1344,512]{1,0:T(8,128)(2,1)}, bf16[1344,512]{1,0:T(8,128)(2,1)}, u32[]{:S(2)}, u32[]{:S(2)}) collective-permute-start(bf16[1344,512]{1,0:T(8,128)(2,1)} %copy.33), channel_id=1, source_target_pairs={{0,1},{1,0},{2,3},{3,2},{4,5},{5,4},{6,7},{7,6},{8,9},{9,8},{10,11... | collective-permute-start | bytes 4128776 | tf_op jit(solution)/shard_map/ppermute | solution.py:28
  421.6 87.5 %collective-permute-start.5 = (bf16[1344,512]{1,0:T(8,128)(2,1)}, bf16[1344,512]{1,0:T(8,128)(2,1)}, u32[]{:S(2)}, u32[]{:S(2)}) collective-permute-start(bf16[1344,512]{1,0:T(8,128)(2,1)} %copy.35), channel_id=1, source_target_pairs={{0,2},{1,3},{2,0},{3,1},{4,6},{5,7},{6,4},{7,5},{8,10},{9,11},{10,... | collective-permute-start | bytes 4128776 | tf_op jit(solution)/shard_map/ppermute | solution.py:28
  423.9 87.9 %collective-permute-start.6 = (bf16[1344,512]{1,0:T(8,128)(2,1)}, bf16[1344,512]{1,0:T(8,128)(2,1)}, u32[]{:S(2)}, u32[]{:S(2)}) collective-permute-start(bf16[1344,512]{1,0:T(8,128)(2,1)} %copy.37), channel_id=1, source_target_pairs={{0,3},{1,2},{2,1},{3,0},{4,7},{5,6},{6,5},{7,4},{8,11},{9,10},{10,... | collective-permute-start | bytes 4128776 | tf_op jit(solution)/shard_map/ppermute | solution.py:28
  426.0 55.2 %collective-permute-start.7 = (f32[1,512]{1,0:T(1,128)S(1)}, f32[1,512]{1,0:T(1,128)S(1)}, u32[]{:S(2)}, u32[]{:S(2)}) collective-permute-start(f32[1,512]{1,0:T(1,128)S(1)} %bitcast.107), channel_id=1, source_target_pairs={{0,1},{1,0},{2,3},{3,2},{4,5},{5,4},{6,7},{7,6},{8,9},{9,8},{10,11... | collective-permute-start | bytes 6152 | tf_op jit(solution)/shard_map/ppermute | solution.py:28
  427.1 54.8 %collective-permute-start.22 = (f32[2,128]{1,0:T(2,128)S(1)}, f32[2,128]{1,0:T(2,128)S(1)}, u32[]{:S(2)}, u32[]{:S(2)}) collective-permute-start(f32[2,128]{1,0:T(2,128)S(1)} %add.169), channel_id=1, source_target_pairs={{0,8},{4,12},{8,0},{12,4},{16,24},{20,28},{24,16},{28,20},{1,9},{5... | collective-permute-start | bytes 3080 | tf_op jit(solution)/shard_map/ppermute | solution.py:28
  481.1 38.0 %collective-permute-start.13 = (bf16[168,4096]{1,0:T(8,128)(2,1)}, bf16[168,4096]{1,0:T(8,128)(2,1)}, u32[]{:S(2)}, u32[]{:S(2)}) collective-permute-start(bf16[168,4096]{1,0:T(8,128)(2,1)} %reshape.105), channel_id=1, source_target_pairs={{0,1},{1,0},{2,3},{3,2},{4,5},{5,4},{6,7},{7,6},{8,9},{9,8},{10,11... | collective-permute-start | bytes 4128776 | tf_op jit(solution)/shard_map/ppermute | solution.py:28
  485.5 18.1 %collective-permute-start.23 = (f32[2,128]{1,0:T(2,128)S(1)}, f32[2,128]{1,0:T(2,128)S(1)}, u32[]{:S(2)}, u32[]{:S(2)}) collective-permute-start(f32[2,128]{1,0:T(2,128)S(1)} %add.170), channel_id=1, source_target_pairs={{0,16},{4,20},{8,24},{12,28},{16,0},{20,4},{24,8},{28,12},{1,17},{... | collective-permute-start | bytes 3080 | tf_op jit(solution)/shard_map/ppermute | solution.py:28
  503.7 58.9 %collective-permute-start.14 = (bf16[168,4096]{1,0:T(8,128)(2,1)}, bf16[168,4096]{1,0:T(8,128)(2,1)}, u32[]{:S(2)}, u32[]{:S(2)}) collective-permute-start(bf16[168,4096]{1,0:T(8,128)(2,1)} %reshape.105), channel_id=1, source_target_pairs={{0,2},{1,3},{2,0},{3,1},{4,6},{5,7},{6,4},{7,5},{8,10},{9,11},{10,... | collective-permute-start | bytes 4128776 | tf_op jit(solution)/shard_map/ppermute | solution.py:28
  504.6 63.2 %collective-permute-start.15 = (bf16[168,4096]{1,0:T(8,128)(2,1)}, bf16[168,4096]{1,0:T(8,128)(2,1)}, u32[]{:S(2)}, u32[]{:S(2)}) collective-permute-start(bf16[168,4096]{1,0:T(8,128)(2,1)} %reshape.105), channel_id=1, source_target_pairs={{0,3},{1,2},{2,1},{3,0},{4,7},{5,6},{6,5},{7,4},{8,11},{9,10},{10,... | collective-permute-start | bytes 4128776 | tf_op jit(solution)/shard_map/ppermute | solution.py:28
  521.8 43.4 %collective-permute-start.17 = (f32[1344]{0:T(1024)S(1)}, f32[1344]{0:T(1024)S(1)}, u32[]{:S(2)}, u32[]{:S(2)}) collective-permute-start(f32[1344]{0:T(1024)S(1)} %fusion.31), channel_id=1, source_target_pairs={{0,8},{4,12},{8,0},{12,4},{16,24},{20,28},{24,16},{28,20},{1,9},{5... | collective-permute-start | bytes 16136 | tf_op jit(solution)/shard_map/ppermute | solution.py:28
  (31 other events, 274.3 us)
Sparse Core Ops, SparseCore 0:
  10.2 106.4 all-gather.8
  118.9 73.7 all-gather.6
  194.9 59.8 all-gather.10
  256.2 51.3 all-gather.12
  321.7 76.3 all-gather.14
  399.6 80.6 all-gather.16

commit v3 on v2

--- a/solution.py
+++ b/solution.py
@@ -244,7 +244,7 @@
 
 
 def attention_rest(start, ends, q, go, own, near, far, mult, *refs, **sizes):
-    attention_body(start, ends, q, go, own, near, far, mult, *refs[3:], **sizes)
+    attention_body(start, ends, q, go, own, near, far, mult, *refs[4:], **sizes)
 
 
 def attention(start, ends, q_raw, go, own, near, far, mult, kv_heads, head_dim, skip, carry):
@@ -272,7 +272,7 @@
             grid=(kv_heads, steps),
             in_specs=[by_query, by_skipped, stacked, stacked, stacked, row]
             + [whole for _ in carry],
-            out_specs=(by_query, stacked, stacked, stacked, row),
+            out_specs=(by_skipped, stacked, stacked, stacked, row),
             scratch_shapes=[
                 pltpu.VMEM((steps, span, rows), jnp.float32),
                 pltpu.VMEM((keys, head_dim), jnp.bfloat16),
@@ -284,7 +284,7 @@
             ],
         ),
         out_shape=(
-            jax.ShapeDtypeStruct((tokens, q_cols), jnp.bfloat16),
+            jax.ShapeDtypeStruct(go.shape, jnp.bfloat16),
             jax.ShapeDtypeStruct(own.shape, jnp.float32),
             half,
             half,
@@ -293,7 +293,7 @@
         compiler_params=pltpu.CompilerParams(
             dimension_semantics=("arbitrary", "arbitrary"), vmem_limit_bytes=48 << 20
         ),
-        input_output_aliases={8 + i: 1 + i for i in range(len(carry))},
+        input_output_aliases={8 + i: i for i in range(len(carry))},
         name="attention",
     )(start, ends, q_raw, go, own, near, far, mult, *carry)
 
@@ -322,10 +322,14 @@
     shard_rows = w_query.shape[0]
     features = model_width // fsdp_count
 
-    key_value = jnp.concatenate([key_projection, value_projection], axis=1)
-    wide_kv = lax.all_gather(key_value, "ctx", axis=0, tiled=True)
     half = w_query.shape[1] // 2
-    wide_qa = lax.all_gather(w_query[:, :half], "ctx", axis=0, tiled=True)
+    wide = lax.all_gather(
+        jnp.concatenate([key_projection, value_projection, w_query[:, :half]], axis=1),
+        "ctx",
+        axis=0,
+        tiled=True,
+    )
+    wide_kv, wide_qa = wide[:, : 2 * kv_cols], wide[:, 2 * kv_cols :]
     wide_qb = lax.all_gather(w_query[:, half:], "ctx", axis=0, tiled=True)
 
     widened = inputs.astype(jnp.float32)
@@ -342,8 +346,11 @@
     )
     blocks, own = lax.optimization_barrier((share_of_columns(normed_turned, shard_rows), own))
     far = shift(own, "ctx", REACH)
+    blocks, far = lax.optimization_barrier((blocks, far))
     picked = jnp.where(on_first_core, own, far)
     near = swap(picked, "ctx", 1)
+    pieces = pick_columns(blocks)
+    pieces = start_columns(pieces)
 
     query_multiplier = (q_gain * query_scale)[None, :]
 
@@ -363,21 +370,17 @@
             carry,
         )
 
-    dqa, *carry, qa_sum = attend(dot(normed, wide_qa), 0, ())
-    all_dqa = lax.all_gather(dqa, "ctx", axis=0, tiled=True)
-    blocks, _ = lax.optimization_barrier((blocks, dqa))
-    pieces = pick_columns(blocks)
-    pieces = start_columns(pieces)
-    dqb, d_own, d_near, d_far, qb_sum = attend(dot(normed, wide_qb), kv_heads // 2, carry)
+    *carry, qa_sum = attend(dot(normed, wide_qa), 0, ())
+    dq16, d_own, d_near, d_far, qb_sum = attend(dot(normed, wide_qb), kv_heads // 2, carry)
     q_sum = qa_sum + qb_sum
 
     crossed = swap(d_near, "ctx", 1)
     nothing = jnp.zeros_like(crossed)
     outgoing = d_far + jnp.where(on_first_core, nothing, crossed)
     returned = shift(outgoing, "ctx", -REACH)
-    gated, returned = lax.optimization_barrier((dqb, returned))
-    all_dqb = lax.all_gather(gated, "ctx", axis=0, tiled=True)
-    query_part = dot(wide_qa, dqa, NT) + dot(wide_qb, dqb, NT)
+    gated, returned = lax.optimization_barrier((dq16, returned))
+    all_dq = lax.all_gather(gated, "ctx", axis=0, tiled=True)
+    query_part = dot(wide_qa, dq16[:, :half], NT) + dot(wide_qb, dq16[:, half:], NT)
     query_part = lax.optimization_barrier(query_part)
     dk16, dv16, k_sum = key_grads_of(
         d_own,
@@ -391,7 +394,7 @@
     dkv16 = jnp.concatenate([dk16, dv16], axis=1)
     all_dkv = lax.all_gather(dkv16, "ctx", axis=0, tiled=True)
 
-    columns = finish_columns(pieces, dqb)
+    columns = finish_columns(pieces, dq16)
 
     head_part = (query_part + dot(wide_kv, dkv16, NT)).astype(jnp.bfloat16)
     row_dot = everywhere(
@@ -426,13 +429,7 @@
         0,
     )
 
-    q_weights = jnp.concatenate(
-        [
-            (grad_scale * dot(columns, part)).astype(jnp.bfloat16)
-            for part in (all_dqa, all_dqb)
-        ],
-        axis=1,
-    )
+    q_weights = (grad_scale * dot(columns, all_dq)).astype(jnp.bfloat16)
     k_weights = (grad_scale * dot(columns, all_dkv[:, :kv_cols])).astype(jnp.bfloat16)
     v_weights = (grad_scale * dot(columns, all_dkv[:, kv_cols:])).astype(jnp.bfloat16)
 

time: 616 us -> 622 us (level)
  waiting for transfers between devices: 315 us -> 402 us
  starting transfers between devices: 69.2 us -> 24.4 us
  other arithmetic: 39.6 us -> 23.8 us
  local copies, waits for them, and re-layouts: 50.5 us -> 36.5 us
    ppermute x22, waiting for transfers between devices: 101 us -> 183 us  [swap(): lax.ppermute(value, axis, [(s, s ^ flip) for s in range(lax.axis_size(axi...]
    ppermute x2, waiting for transfers between devices: 85.6 us -> 28.1 us  [shift(): lax.ppermute(value, axis, [(s, s + steps) for s in range(initial, last)])]
    ppermute x22, starting transfers between devices: 65.6 us -> 20.9 us  [swap(): lax.ppermute(value, axis, [(s, s ^ flip) for s in range(lax.axis_size(axi...]
    all_gather x4 -> x2, waiting for transfers between devices: 89.6 us -> 131 us  [the longest x1 131 us: layer(): lax.all_gather(jnp.concatenate([key_projection, value_projection, w_query...]
    all_gather x1, waiting for transfers between devices: 38.1 us -> 58.8 us  [layer(): wide_qb = lax.all_gather(w_query[:, half:], 'ctx', axis=0, tiled=True)]
    dynamic_slice x5 -> x2, local copies, waits for them, and re-layouts: 9.11 us -> 0.36 us  [part_of(): return lax.dynamic_slice_in_dim(array, index * features, features, 0)]
    convert_element_type x1 -> x0, local copies, waits for them, and re-layouts: 8 us -> none  [layer(): (turned.astype(jnp.float32) * inv_row * norm_gain[:, None]).astype(jnp.bf...]
    unnamed x52 -> x42, local copies, waits for them, and re-layouts: 7.77 us -> 15.6 us
  transfers between devices with their start and end apart: 30 -> 28, of which waited for: 14 -> 14; matrix products, arithmetic and copies ran while one was open for 25% -> 18% of each run, Pallas kernels for 6% -> 1%
where the time goes in v3:
time: 622 us; the launch traced here: 617 us
  waiting for transfers between devices  402 us (65%)
  matrix products  78.3 us (13%)
  Pallas kernels  37.5 us (6%)
  local copies, waits for them, and re-layouts  36.5 us (6%)
  starting transfers between devices  24.4 us (4%)
  other arithmetic  23.8 us (4%)
  between operations  14.5 us (2%)
    ppermute x22, waiting for transfers between devices, swap(): lax.ppermute(value, axis, [(s, s ^ flip) for s in range(lax.axis_size(axi...  183 us
    all_gather x1, waiting for transfers between devices, layer(): lax.all_gather(jnp.concatenate([key_projection, value_projection, w_query...  131 us
    dot_general x9, matrix products, dot(): return lax.dot_general(a, b, dims, preferred_element_type=jnp.float32)  78.3 us
    all_gather x1, waiting for transfers between devices, layer(): wide_qb = lax.all_gather(w_query[:, half:], 'ctx', axis=0, tiled=True)  58.8 us
    pallas_call x2, Pallas kernels, attention(): pl.pallas_call(functools.partial(attention_rest if carry else attention_b...  29 us
    ppermute x2, waiting for transfers between devices, shift(): lax.ppermute(value, axis, [(s, s + steps) for s in range(initial, last)])  28.1 us
    ppermute x22, starting transfers between devices, swap(): lax.ppermute(value, axis, [(s, s ^ flip) for s in range(lax.axis_size(axi...  20.9 us
    unnamed x42, local copies, waits for them, and re-layouts  15.6 us
  transfers between devices with their start and end apart: 28, of which 14 were waited for; matrix products, arithmetic and copies ran while one was open for 18% of the time, Pallas kernels for 1%

profile of v3, /device:TPU:0, one launch (start us, length us, event | category | flops | bytes accessed | tf_op | source)
XLA Modules:
  0.0 616.7 jit_solution(17316739309644539615)
XLA Ops:
  13.2 8.3 %copy.27 = bf16[512,5376]{0,1:T(8,128)(2,1)} copy(bf16[512,5376]{1,0:T(8,128)(2,1)} %param.9) | data formatting | bytes 11010048 | tf_op args[0]
  21.7 4.7 fusion
  27.5 4.0 fusion.2
  33.0 131.2 %all-gather.5.cloned.1.call-done = bf16[5376,1536]{1,0:T(8,128)(2,1)} async-done(((bf16[672,1536]{1,0:T(8,128)(2,1)}), bf16[5376,1536]{1,0:T(8,128)(2,1)}) %all-gather.5.cloned.1.call-update) | async-done | bytes 16515088 | tf_op jit(solution)/shard_map/all_gather | solution.py:326
  164.2 11.4 %fusion.8.k_ref.v_ref = f32[512,1024]{1,0:T(8,128)} fusion(bf16[512,5376]{0,1:T(8,128)(2,1)} %fusion.2, bf16[5376,1536]{1,0:T(8,128)(2,1)} %all-gather.5.cloned.1.call-done), kind=kOutput, calls=%fused_computation.13 | convolution fusion | flops 5637144576 | bytes 18612224 | tf_op jit(solution)/shard_map/dot_general | solution.py:32
  181.3 58.8 %all-gather.7.cloned.1.call-done = bf16[5376,512]{1,0:T(8,128)(2,1)} async-done(((bf16[672,512]{1,0:T(8,128)(2,1)}), bf16[5376,512]{1,0:T(8,128)(2,1)}) %all-gather.7.cloned.1.call-update) | async-done | bytes 5505040 | tf_op jit(solution)/shard_map/all_gather | solution.py:333
  240.1 6.9 %fusion.43.q = f32[512,512]{1,0:T(8,128)S(1)} fusion(bf16[512,5376]{0,1:T(8,128)(2,1)} %fusion.2, bf16[5376,512]{1,0:T(8,128)(2,1)} %all-gather.7.cloned.1.call-done), kind=kOutput, calls=%fused_computation.82 | convolution fusion | flops 2818572288 | bytes 12058624 | tf_op jit(solution)/shard_map/dot_general | solution.py:32
  249.3 5.0 fusion.11.q_ref
  255.3 14.5 %attention.2 = (bf16[512,1024]{1,0:T(8,128)(2,1)}, f32[2,512,512]{2,1,0:T(8,128)}, bf16[2,512,512]{2,1,0:T(8,128)(2,1)S(1)}, bf16[2,512,512]{2,1,0:T(8,128)(2,1)S(1)}, f32[1,128]{1,0:T(1,128)S(1)}) custom-call(s32[1]{0:T(128)} %bitcast.start_ref.start, s32[4]{0:T(128)S(1)} %bitcast.81, f32[512,512]{1,0:T(8,128)S(1)} %fusion.11.q_ref, ...), custom_call_target="tpu_custom_call" | custom-call | tf_op jit(solution)/shard_map/attention/pallas_call | solution.py:263
  269.8 14.5 %attention.3 = (bf16[512,1024]{1,0:T(8,128)(2,1)}, f32[2,512,512]{2,1,0:T(8,128)}, bf16[2,512,512]{2,1,0:T(8,128)(2,1)S(1)}, bf16[2,512,512]{2,1,0:T(8,128)(2,1)S(1)}, f32[1,128]{1,0:T(1,128)S(1)}) custom-call(s32[1]{0:T(128)} %bitcast.start_ref.start, s32[4]{0:T(128)S(1)} %bitcast.82, ...), custom_call_target="tpu_custom_call", output_to_operand_aliasing={{0}: (8, {}), {1}: (9, {}), {2}: (10, {}), {3}: (11, {})} | custom-call | tf_op jit(solution)/shard_map/attention/pallas_call | solution.py:263
  289.4 28.1 %collective-permute-done.3.far_ref = bf16[2,512,512]{2,1,0:T(8,128)(2,1)S(1)} collective-permute-done((bf16[2,512,512]{2,1,0:T(8,128)(2,1)S(1)}, bf16[2,512,512]{2,1,0:T(8,128)(2,1)S(1)}, u32[]{:S(2)}, u32[]{:S(2)}) %collective-permute-start.3) | collective-permute-done | bytes 1048608 | tf_op jit(solution)/shard_map/ppermute | solution.py:24
  318.4 4.7 key_grads.1
  331.3 9.0 %collective-permute-done.11 = bf16[2,168,512]{2,1,0:T(8,128)(2,1)S(1)} collective-permute-done((bf16[2,168,512]{2,1,0:T(8,128)(2,1)S(1)}, bf16[2,168,512]{2,1,0:T(8,128)(2,1)S(1)}, u32[]{:S(2)}, u32[]{:S(2)}) %collective-permute-start.11) | collective-permute-done | bytes 344096 | tf_op jit(solution)/shard_map/ppermute | solution.py:28
  340.4 56.5 %collective-permute-done.10 = bf16[2,168,512]{2,1,0:T(8,128)(2,1)S(1)} collective-permute-done((bf16[2,168,512]{2,1,0:T(8,128)(2,1)S(1)}, bf16[2,168,512]{2,1,0:T(8,128)(2,1)S(1)}, u32[]{:S(2)}, u32[]{:S(2)}) %collective-permute-start.10) | collective-permute-done | bytes 344096 | tf_op jit(solution)/shard_map/ppermute | solution.py:28
  397.2 5.4 fusion.36
  402.6 10.4 %bitcast_add_fusion = f32[5376,512]{1,0:T(8,128)} fusion(f32[512,5376]{0,1:T(8,128)S(1)} %fusion.36, bf16[5376,1536]{1,0:T(8,128)(2,1)} %all-gather.5.cloned.1.call-done, bf16[512,1024]{1,0:T(8,128)(2,1)} %get-tuple-element.44), kind=kOutput, calls=%fused_computation.9 | convolution fusion | flops 2821324800 | bytes 28049408 | tf_op jit(solution)/shard_map/dot_general | solution.py:32
  426.4 13.9 %fusion.6 = f32[5376,512]{1,0:T(8,128)} fusion(bf16[512,1024]{1,0:T(8,128)(2,1)S(1)} %copy-done.7, bf16[5376,1536]{1,0:T(8,128)(2,1)} %all-gather.5.cloned.1.call-done), kind=kOutput, calls=%fused_computation.11 | convolution fusion | flops 5637144576 | bytes 23068672 | tf_op jit(solution)/shard_map/dot_general | solution.py:32
  440.4 5.9 fusion.5
  453.5 58.0 %collective-permute-done.20 = f32[2,128]{1,0:T(2,128)S(1)} collective-permute-done((f32[2,128]{1,0:T(2,128)S(1)}, f32[2,128]{1,0:T(2,128)S(1)}, u32[]{:S(2)}, u32[]{:S(2)}) %collective-permute-start.20) | collective-permute-done | bytes 1056 | tf_op jit(solution)/shard_map/ppermute | solution.py:28
  522.9 22.2 %collective-permute-done.4 = bf16[1344,512]{1,0:T(8,128)(2,1)S(1)} collective-permute-done((bf16[1344,512]{1,0:T(8,128)(2,1)S(1)}, bf16[1344,512]{1,0:T(8,128)(2,1)S(1)}, u32[]{:S(2)}, u32[]{:S(2)}) %collective-permute-start.4) | collective-permute-done | bytes 1376288 | tf_op jit(solution)/shard_map/ppermute | solution.py:28
  547.7 26.0 %collective-permute-done.15 = bf16[168,4096]{1,0:T(8,128)(2,1)S(1)} collective-permute-done((bf16[168,4096]{1,0:T(8,128)(2,1)S(1)}, bf16[168,4096]{1,0:T(8,128)(2,1)S(1)}, u32[]{:S(2)}, u32[]{:S(2)}) %collective-permute-start.15) | collective-permute-done | bytes 1376288 | tf_op jit(solution)/shard_map/ppermute | solution.py:28
  584.6 7.8 %fusion.33 = bf16[672,512]{1,0:T(8,128)(2,1)} fusion(bf16[672,4096]{1,0:T(8,128)(2,1)} %bitcast.30, bf16[4096,1024]{1,0:T(8,128)(2,1)} %all-gather.11.cloned.1.call-done), kind=kOutput, calls=%fused_computation.47 | convolution fusion | flops 2819260416 | bytes 10387456 | tf_op jit(solution)/shard_map/dot_general | solution.py:32
  592.5 6.4 %fusion.30 = bf16[672,512]{1,0:T(8,128)(2,1)} fusion(bf16[672,4096]{1,0:T(8,128)(2,1)} %bitcast.30, bf16[4096,1024]{1,0:T(8,128)(2,1)S(1)} %copy-done.11), kind=kOutput, calls=%fused_computation.46 | convolution fusion | flops 2819260416 | bytes 10387456 | tf_op jit(solution)/shard_map/dot_general | solution.py:32
  598.9 11.1 %multiply_convert_fusion = bf16[672,1024]{1,0:T(8,128)(2,1)} fusion(bf16[672,4096]{1,0:T(8,128)(2,1)} %bitcast.30, bf16[4096,1024]{1,0:T(8,128)(2,1)} %all-gather.9.cloned.1.call-done), kind=kOutput, calls=%fused_computation.29 | convolution fusion | flops 5638520832 | bytes 15269888 | tf_op jit(solution)/shard_map/dot_general | solution.py:32
  (140 shorter events, 77.5 us)
Async XLA Ops:
  7.2 157.0 %all-gather.5.cloned.1.call-start = ((), (), s32[]{:S(2)}) async-start(), calls=%async_computation | async-start | bytes 18579456 | tf_op jit(solution)/shard_map/all_gather | solution.py:326
  12.3 227.7 %all-gather.7.cloned.1.call-start = ((), (), s32[]{:S(2)}) async-start(), calls=%async_computation.1 | async-start | bytes 6193152 | tf_op jit(solution)/shard_map/all_gather | solution.py:333
  13.1 571.5 %all-gather.11.cloned.1.call-start = ((), (), s32[]{:S(2)}) async-start(), calls=%async_computation.3 | async-start | bytes 9437184 | tf_op jit(solution)/shard_map/all_gather | solution.py:395
  179.3 67.7 %collective-permute-start = (bf16[2,512,512]{2,1,0:T(8,128)(2,1)}, bf16[2,512,512]{2,1,0:T(8,128)(2,1)S(1)}, u32[]{:S(2)}, u32[]{:S(2)}) collective-permute-start(bf16[2,512,512]{2,1,0:T(8,128)(2,1)} %key_rows.1.own_ref.own), channel_id=1, source_target_pairs={{0,8},{4,12},{8,16},{12,20},{16,24},{20,28},{1,9},{5,13},{9,17},{1... | collective-permute-start | bytes 3145736 | tf_op jit(solution)/shard_map/ppermute | solution.py:24
  247.2 7.2 %collective-permute-start.1 = (bf16[2,512,512]{2,1,0:T(8,128)(2,1)S(1)}, bf16[2,512,512]{2,1,0:T(8,128)(2,1)S(1)}, u32[]{:S(2)}, u32[]{:S(2)}) collective-permute-start(bf16[2,512,512]{2,1,0:T(8,128)(2,1)S(1)} %broadcast_select_fusion.1), channel_id=1, source_target_pairs={{0,4},{4,0},{8,12},{12,8},{16,20},{20,16},{24,28},{28,24},{1,5},{5... | collective-permute-start | bytes 3145736 | tf_op jit(solution)/shard_map/ppermute | solution.py:28
  288.1 29.4 %collective-permute-start.3 = (bf16[2,512,512]{2,1,0:T(8,128)(2,1)S(1)}, bf16[2,512,512]{2,1,0:T(8,128)(2,1)S(1)}, u32[]{:S(2)}, u32[]{:S(2)}) collective-permute-start(bf16[2,512,512]{2,1,0:T(8,128)(2,1)S(1)} %get-tuple-element.63), channel_id=1, source_target_pairs={{8,0},{12,4},{16,8},{20,12},{24,16},{28,20},{9,1},{13,5},{17,9},{2... | collective-permute-start | bytes 3145736 | tf_op jit(solution)/shard_map/ppermute | solution.py:24
  326.3 272.5 %all-gather.9.cloned.1.call-start = ((), (), s32[]{:S(2)}) async-start(), calls=%async_computation.2 | async-start | bytes 9437184 | tf_op jit(solution)/shard_map/all_gather | solution.py:382
  326.7 13.6 %collective-permute-start.11 = (bf16[2,168,512]{2,1,0:T(8,128)(2,1)S(1)}, bf16[2,168,512]{2,1,0:T(8,128)(2,1)S(1)}, u32[]{:S(2)}, u32[]{:S(2)}) collective-permute-start(bf16[2,168,512]{2,1,0:T(8,128)(2,1)S(1)} %get-tuple-element.58), channel_id=1, source_target_pairs={{0,24},{4,28},{8,16},{12,20},{16,8},{20,12},{24,0},{28,4},{1,25},{... | collective-permute-start | bytes 1032200 | tf_op jit(solution)/shard_map/ppermute | solution.py:28
  326.8 70.0 %collective-permute-start.10 = (bf16[2,168,512]{2,1,0:T(8,128)(2,1)S(1)}, bf16[2,168,512]{2,1,0:T(8,128)(2,1)S(1)}, u32[]{:S(2)}, u32[]{:S(2)}) collective-permute-start(bf16[2,168,512]{2,1,0:T(8,128)(2,1)S(1)} %get-tuple-element.59), channel_id=1, source_target_pairs={{0,16},{4,20},{8,24},{12,28},{16,0},{20,4},{24,8},{28,12},{1,17},{... | collective-permute-start | bytes 1032200 | tf_op jit(solution)/shard_map/ppermute | solution.py:28
  330.0 66.9 %collective-permute-start.9 = (bf16[2,168,512]{2,1,0:T(8,128)(2,1)S(1)}, bf16[2,168,512]{2,1,0:T(8,128)(2,1)S(1)}, u32[]{:S(2)}, u32[]{:S(2)}) collective-permute-start(bf16[2,168,512]{2,1,0:T(8,128)(2,1)S(1)} %get-tuple-element.60), channel_id=1, source_target_pairs={{0,8},{4,12},{8,0},{12,4},{16,24},{20,28},{24,16},{28,20},{1,9},{5... | collective-permute-start | bytes 1032200 | tf_op jit(solution)/shard_map/ppermute | solution.py:28
  397.1 15.9 %collective-permute-start.12 = (bf16[4,168,512]{2,1,0:T(8,128)(2,1)S(1)}, bf16[4,168,512]{2,1,0:T(8,128)(2,1)S(1)}, u32[]{:S(2)}, u32[]{:S(2)}) collective-permute-start(bf16[4,168,512]{2,1,0:T(8,128)(2,1)S(1)} %dynamic-slice_bitcast_fusion), channel_id=1, source_target_pairs={{0,4},{4,0},{8,12},{12,8},{16,20},{20,16},{24,28},{28,24},{1,5},{5... | collective-permute-start | bytes 2064392 | tf_op jit(solution)/shard_map/ppermute | solution.py:28
  418.4 93.5 %collective-permute-start.13 = (bf16[168,4096]{1,0:T(8,128)(2,1)}, bf16[168,4096]{1,0:T(8,128)(2,1)}, u32[]{:S(2)}, u32[]{:S(2)}) collective-permute-start(bf16[168,4096]{1,0:T(8,128)(2,1)} %reshape.105), channel_id=1, source_target_pairs={{0,1},{1,0},{2,3},{3,2},{4,5},{5,4},{6,7},{7,6},{8,9},{9,8},{10,11... | collective-permute-start | bytes 4128776 | tf_op jit(solution)/shard_map/ppermute | solution.py:28
  420.1 97.7 %collective-permute-start.14 = (bf16[168,4096]{1,0:T(8,128)(2,1)}, bf16[168,4096]{1,0:T(8,128)(2,1)}, u32[]{:S(2)}, u32[]{:S(2)}) collective-permute-start(bf16[168,4096]{1,0:T(8,128)(2,1)} %reshape.105), channel_id=1, source_target_pairs={{0,2},{1,3},{2,0},{3,1},{4,6},{5,7},{6,4},{7,5},{8,10},{9,11},{10,... | collective-permute-start | bytes 4128776 | tf_op jit(solution)/shard_map/ppermute | solution.py:28
  425.8 26.0 %collective-permute-start.19 = (f32[2,128]{1,0:T(2,128)S(1)}, f32[2,128]{1,0:T(2,128)S(1)}, u32[]{:S(2)}, u32[]{:S(2)}) collective-permute-start(f32[2,128]{1,0:T(2,128)S(1)} %pad_maximum_fusion.3), channel_id=1, source_target_pairs={{0,1},{1,0},{2,3},{3,2},{4,5},{5,4},{6,7},{7,6},{8,9},{9,8},{10,11... | collective-permute-start | bytes 3080 | tf_op jit(solution)/shard_map/ppermute | solution.py:28
  446.6 76.3 %collective-permute-start.6 = (bf16[1344,512]{1,0:T(8,128)(2,1)S(1)}, bf16[1344,512]{1,0:T(8,128)(2,1)S(1)}, u32[]{:S(2)}, u32[]{:S(2)}) collective-permute-start(bf16[1344,512]{1,0:T(8,128)(2,1)S(1)} %get-tuple-element.53), channel_id=1, source_target_pairs={{0,3},{1,2},{2,1},{3,0},{4,7},{5,6},{6,5},{7,4},{8,11},{9,10},{10,... | collective-permute-start | bytes 4128776 | tf_op jit(solution)/shard_map/ppermute | solution.py:28
  448.2 74.6 %collective-permute-start.5 = (bf16[1344,512]{1,0:T(8,128)(2,1)S(1)}, bf16[1344,512]{1,0:T(8,128)(2,1)S(1)}, u32[]{:S(2)}, u32[]{:S(2)}) collective-permute-start(bf16[1344,512]{1,0:T(8,128)(2,1)S(1)} %get-tuple-element.54), channel_id=1, source_target_pairs={{0,2},{1,3},{2,0},{3,1},{4,6},{5,7},{6,4},{7,5},{8,10},{9,11},{10,... | collective-permute-start | bytes 4128776 | tf_op jit(solution)/shard_map/ppermute | solution.py:28
  451.8 59.7 %collective-permute-start.20 = (f32[2,128]{1,0:T(2,128)S(1)}, f32[2,128]{1,0:T(2,128)S(1)}, u32[]{:S(2)}, u32[]{:S(2)}) collective-permute-start(f32[2,128]{1,0:T(2,128)S(1)} %fusion.40), channel_id=1, source_target_pairs={{0,2},{1,3},{2,0},{3,1},{4,6},{5,7},{6,4},{7,5},{8,10},{9,11},{10,... | collective-permute-start | bytes 3080 | tf_op jit(solution)/shard_map/ppermute | solution.py:28
  512.0 33.1 %collective-permute-start.4 = (bf16[1344,512]{1,0:T(8,128)(2,1)S(1)}, bf16[1344,512]{1,0:T(8,128)(2,1)S(1)}, u32[]{:S(2)}, u32[]{:S(2)}) collective-permute-start(bf16[1344,512]{1,0:T(8,128)(2,1)S(1)} %get-tuple-element.52), channel_id=1, source_target_pairs={{0,1},{1,0},{2,3},{3,2},{4,5},{5,4},{6,7},{7,6},{8,9},{9,8},{10,11... | collective-permute-start | bytes 4128776 | tf_op jit(solution)/shard_map/ppermute | solution.py:28
  517.8 55.9 %collective-permute-start.15 = (bf16[168,4096]{1,0:T(8,128)(2,1)S(1)}, bf16[168,4096]{1,0:T(8,128)(2,1)S(1)}, u32[]{:S(2)}, u32[]{:S(2)}) collective-permute-start(bf16[168,4096]{1,0:T(8,128)(2,1)S(1)} %copy-done.8), channel_id=1, source_target_pairs={{0,3},{1,2},{2,1},{3,0},{4,7},{5,6},{6,5},{7,4},{8,11},{9,10},{10,... | collective-permute-start | bytes 4128776 | tf_op jit(solution)/shard_map/ppermute | solution.py:28
  522.9 52.0 %collective-permute-start.22 = (f32[2,128]{1,0:T(2,128)S(1)}, f32[2,128]{1,0:T(2,128)S(1)}, u32[]{:S(2)}, u32[]{:S(2)}) collective-permute-start(f32[2,128]{1,0:T(2,128)S(1)} %add.165), channel_id=1, source_target_pairs={{0,8},{4,12},{8,0},{12,4},{16,24},{20,28},{24,16},{28,20},{1,9},{5... | collective-permute-start | bytes 3080 | tf_op jit(solution)/shard_map/ppermute | solution.py:28
  547.7 27.2 %collective-permute-start.16 = (f32[1344]{0:T(1024)S(1)}, f32[1344]{0:T(1024)S(1)}, u32[]{:S(2)}, u32[]{:S(2)}) collective-permute-start(f32[1344]{0:T(1024)S(1)} %broadcast_multiply_fusion), channel_id=1, source_target_pairs={{0,4},{4,0},{8,12},{12,8},{16,20},{20,16},{24,28},{28,24},{1,5},{5... | collective-permute-start | bytes 16136 | tf_op jit(solution)/shard_map/ppermute | solution.py:28
  574.9 4.5 collective-permute-start.23
  574.9 4.4 collective-permute-start.17
  579.4 4.6 collective-permute-start.18
  (24 other events, 310.8 us)
Sparse Core Ops, SparseCore 0:
  12.5 151.6 all-gather.4
  166.4 73.6 all-gather.6
  326.5 102.2 all-gather.10
  430.2 80.9 all-gather.8

commit v4 on v1

--- a/solution.py
+++ b/solution.py
@@ -111,39 +111,129 @@
     )(projected, projected, gain[None, :])
 
 
-def key_grad_body(own_ref, near_ref, far_ref, k_ref, gain_ref, dk_ref, dv_ref, sum_ref):
-    total = own_ref[...] + near_ref[...].astype(jnp.float32) + far_ref[...].astype(jnp.float32)
-    k = k_ref[...]
-    inv = lax.rsqrt(jnp.mean(k * k, axis=1, keepdims=True) + epsilon)
-    k_hat = k * inv
-    d = total[0]
-    u = d * gain_ref[...]
-    dk_ref[...] = (inv * (u - k_hat * jnp.mean(u * k_hat, axis=1, keepdims=True))).astype(
-        jnp.bfloat16
-    )
-    dv_ref[...] = total[1].astype(jnp.bfloat16)
+def key_grad_body(own_ref, near_ref, far_ref, k_ref, gain_ref, out_ref, sum_ref):
+    total = own_ref[0] + near_ref[0].astype(jnp.float32) + far_ref[0].astype(jnp.float32)
+
+    @pl.when((pl.program_id(0) == 0) & (pl.program_id(1) == 0))
+    def _():
+        sum_ref[...] = jnp.zeros_like(sum_ref)
 
     @pl.when(pl.program_id(0) == 0)
     def _():
-        sum_ref[...] = jnp.zeros_like(sum_ref)
-
-    sum_ref[...] += jnp.sum(d * k_hat, axis=0, keepdims=True)
+        k = k_ref[...]
+        inv = lax.rsqrt(jnp.mean(k * k, axis=1, keepdims=True) + epsilon)
+        k_hat = k * inv
+        u = total * gain_ref[...]
+        out_ref[...] = (
+            inv * (u - k_hat * jnp.mean(u * k_hat, axis=1, keepdims=True))
+        ).astype(jnp.bfloat16)
+        sum_ref[...] += jnp.sum(total * k_hat, axis=0, keepdims=True)
+
+    @pl.when(pl.program_id(0) == 1)
+    def _():
+        out_ref[...] = total.astype(jnp.bfloat16)
 
 
 def key_grads_of(own, near, far, projected, gain, kv_heads, head_dim):
     tokens = projected.shape[0]
-    stacked = pl.BlockSpec((2, tokens, head_dim), lambda g: (0, 0, g))
-    flat = pl.BlockSpec((tokens, head_dim), lambda g: (0, g))
-    row = pl.BlockSpec((1, head_dim), lambda g: (0, 0))
-    half = jax.ShapeDtypeStruct((tokens, kv_heads * head_dim), jnp.bfloat16)
+    stacked = pl.BlockSpec((1, tokens, head_dim), lambda t, g: (t, 0, g))
+    row = pl.BlockSpec((1, head_dim), lambda t, g: (0, 0))
     return pl.pallas_call(
         key_grad_body,
-        grid=(kv_heads,),
-        in_specs=[stacked, stacked, stacked, flat, row],
-        out_specs=(flat, flat, row),
-        out_shape=(half, half, jax.ShapeDtypeStruct((1, head_dim), jnp.float32)),
+        grid=(2, kv_heads),
+        in_specs=[
+            stacked,
+            stacked,
+            stacked,
+            pl.BlockSpec((tokens, head_dim), lambda t, g: (0, g)),
+            row,
+        ],
+        out_specs=(
+            pl.BlockSpec((tokens, head_dim), lambda t, g: (0, t * kv_heads + g)),
+            row,
+        ),
+        out_shape=(
+            jax.ShapeDtypeStruct((tokens, 2 * kv_heads * head_dim), jnp.bfloat16),
+            jax.ShapeDtypeStruct((1, head_dim), jnp.float32),
+        ),
         name="key_grads",
     )(own, near, far, projected, gain[None, :])
+
+
+def normed_grad_body(part_ref, wide_ref, d_ref, x_ref, gain_ref, out_ref, dots_ref):
+    rounded = (part_ref[...] + dot(wide_ref[...], d_ref[...], NT)).astype(jnp.bfloat16)
+    out_ref[...] = rounded
+
+    @pl.when(pl.program_id(0) == 0)
+    def _():
+        dots_ref[...] = jnp.zeros_like(dots_ref)
+
+    gained = x_ref[...].astype(jnp.float32) * gain_ref[...]
+    dots_ref[...] += jnp.sum(rounded.astype(jnp.float32) * gained, axis=0, keepdims=True)
+
+
+def normed_grad(part, wide, d, turned, gain):
+    width, tokens = part.shape
+    cols = wide.shape[1]
+    rows = max(r for r in range(128, 513, 128) if width % r == 0)
+    by_row = pl.BlockSpec((rows, tokens), lambda i: (i, 0))
+    return pl.pallas_call(
+        normed_grad_body,
+        grid=(width // rows,),
+        in_specs=[
+            by_row,
+            pl.BlockSpec((rows, cols), lambda i: (i, 0)),
+            pl.BlockSpec((tokens, cols), lambda i: (0, 0)),
+            by_row,
+            pl.BlockSpec((rows, 1), lambda i: (i, 0)),
+        ],
+        out_specs=(by_row, pl.BlockSpec((1, tokens), lambda i: (0, 0))),
+        out_shape=(
+            jax.ShapeDtypeStruct((width, tokens), jnp.bfloat16),
+            jax.ShapeDtypeStruct((1, tokens), jnp.float32),
+        ),
+        name="normed_grad",
+    )(part, wide, d, turned, gain[:, None])
+
+
+def weight_grad_body(columns_ref, d_ref, k_ref, v_ref, sum_ref, *, scale):
+    step = pl.program_id(0)
+    product = dot(columns_ref[...], d_ref[...])
+
+    @pl.when(step == 0)
+    def _():
+        sum_ref[...] = product
+
+    @pl.when(step > 0)
+    def _():
+        sum_ref[...] += product
+
+    @pl.when(step == pl.num_programs(0) - 1)
+    def _():
+        cut = k_ref.shape[1]
+        k_ref[...] = (scale * sum_ref[:, :cut]).astype(k_ref.dtype)
+        v_ref[...] = (scale * sum_ref[:, cut:]).astype(v_ref.dtype)
+
+
+def weight_grads(columns, d, scale):
+    rows, tokens = columns.shape
+    cols = d.shape[1]
+    chunk = tokens // 4
+    out = pl.BlockSpec((rows, cols // 2), lambda i: (0, 0))
+    shape = jax.ShapeDtypeStruct((rows, cols // 2), jnp.bfloat16)
+    return pl.pallas_call(
+        functools.partial(weight_grad_body, scale=scale),
+        grid=(4,),
+        in_specs=[
+            pl.BlockSpec((rows, chunk), lambda i: (0, i)),
+            pl.BlockSpec((chunk, cols), lambda i: (i, 0)),
+        ],
+        out_specs=(out, out),
+        out_shape=(shape, shape),
+        scratch_shapes=[pltpu.VMEM((rows, cols), jnp.float32)],
+        compiler_params=pltpu.CompilerParams(vmem_limit_bytes=40 << 20),
+        name="weight_grads",
+    )(columns, d)
 
 
 def attention_body(
@@ -351,11 +441,10 @@
     nothing = jnp.zeros_like(crossed)
     outgoing = d_far + jnp.where(on_first_core, nothing, crossed)
     returned = shift(outgoing, "ctx", -REACH)
-    gated, returned = lax.optimization_barrier((dq16, returned))
-    all_dq = lax.all_gather(gated, "ctx", axis=0, tiled=True)
+    all_dq = lax.all_gather(dq16, "ctx", axis=0, tiled=True)
     query_part = dot(wide_q, dq16, NT)
     query_part = lax.optimization_barrier(query_part)
-    dk16, dv16, k_sum = key_grads_of(
+    dkv16, k_sum = key_grads_of(
         d_own,
         jnp.where(on_first_core, crossed, nothing),
         returned,
@@ -364,21 +453,12 @@
         kv_heads,
         head_dim,
     )
-    dkv16 = jnp.concatenate([dk16, dv16], axis=1)
     all_dkv = lax.all_gather(dkv16, "ctx", axis=0, tiled=True)
 
     columns = finish_columns(pieces, dq16)
 
-    head_part = (query_part + dot(wide_kv, dkv16, NT)).astype(jnp.bfloat16)
-    row_dot = everywhere(
-        jnp.sum(
-            head_part.astype(jnp.float32) * (turned.astype(jnp.float32) * norm_gain[:, None]),
-            axis=0,
-            keepdims=True,
-        )
-        * inv_row,
-        ("fsdp",),
-    )
+    head_part, row_dot = normed_grad(query_part, wide_kv, dkv16, turned, norm_gain)
+    row_dot = everywhere(row_dot * inv_row, ("fsdp",))
 
     def part_of(array, index):
         return lax.dynamic_slice_in_dim(array, index * features, features, 0)
@@ -403,8 +483,7 @@
     )
 
     q_weights = (grad_scale * dot(columns, all_dq)).astype(jnp.bfloat16)
-    k_weights = (grad_scale * dot(columns, all_dkv[:, :kv_cols])).astype(jnp.bfloat16)
-    v_weights = (grad_scale * dot(columns, all_dkv[:, kv_cols:])).astype(jnp.bfloat16)
+    k_weights, v_weights = weight_grads(columns, all_dkv, grad_scale)
 
     gains = jnp.concatenate([q_sum * (grad_scale * query_scale), k_sum * grad_scale], axis=0)
     gains = everywhere(gains, ("fsdp",))

time: 597 us -> 601 us (level)
  waiting for transfers between devices: 335 us -> 385 us
  Pallas kernels: 33.9 us -> 65.9 us
  matrix products: 74.3 us -> 44.9 us
  starting transfers between devices: 49.6 us -> 24.9 us
  local copies, waits for them, and re-layouts: 49.3 us -> 35.3 us
    ppermute x2, waiting for transfers between devices: 73.7 us -> 111 us  [shift(): lax.ppermute(value, axis, [(s, s + steps) for s in range(initial, last)])]
    pallas_call x1 -> x3, Pallas kernels: 4.69 us -> 36.7 us  [the longest x1 19.6 us: normed_grad(): pl.pallas_call(normed_grad_body, grid=(width // rows,), in_specs=[by_row,...]
    dot_general x7 -> x4, matrix products: 74.3 us -> 44.9 us  [dot(): return lax.dot_general(a, b, dims, preferred_element_type=jnp.float32)]
    ppermute x22, starting transfers between devices: 46.4 us -> 21.9 us  [swap(): lax.ppermute(value, axis, [(s, s ^ flip) for s in range(lax.axis_size(axi...]
    ppermute x22, waiting for transfers between devices: 124 us -> 138 us  [swap(): lax.ppermute(value, axis, [(s, s ^ flip) for s in range(lax.axis_size(axi...]
    convert_element_type x1 -> x0, local copies, waits for them, and re-layouts: 8.5 us -> none  [layer(): (turned.astype(jnp.float32) * inv_row * norm_gain[:, None]).astype(jnp.bf...]
    unnamed x38 -> x25, local copies, waits for them, and re-layouts: 5.85 us -> 13.7 us
    reduce_sum x1 -> x0, other arithmetic: 6.53 us -> none  [layer(): jnp.sum(head_part.astype(jnp.float32) * (turned.astype(jnp.float32) * nor...]
  transfers between devices with their start and end apart: 28 -> 28, of which waited for: 12 -> 11; matrix products, arithmetic and copies ran while one was open for 23% -> 17% of each run, Pallas kernels for 1% -> 5%
where the time goes in v4:
time: 601 us; the launch traced here: 600 us
  waiting for transfers between devices  385 us (64%)
  Pallas kernels  65.9 us (11%)
  matrix products  44.9 us (7%)
  local copies, waits for them, and re-layouts  35.3 us (6%)
  other arithmetic  29.8 us (5%)
  starting transfers between devices  24.9 us (4%)
  between operations  14.1 us (2%)
    ppermute x22, waiting for transfers between devices, swap(): lax.ppermute(value, axis, [(s, s ^ flip) for s in range(lax.axis_size(axi...  138 us
    ppermute x2, waiting for transfers between devices, shift(): lax.ppermute(value, axis, [(s, s + steps) for s in range(initial, last)])  111 us
    all_gather x1, waiting for transfers between devices, layer(): wide_kv = lax.all_gather(key_value, 'ctx', axis=0, tiled=True)  80.5 us
    all_gather x1, waiting for transfers between devices, layer(): wide_q = lax.all_gather(w_query, 'ctx', axis=0, tiled=True)  55.3 us
    dot_general x4, matrix products, dot(): return lax.dot_general(a, b, dims, preferred_element_type=jnp.float32)  44.9 us
    pallas_call x1, Pallas kernels, attention(): pl.pallas_call(functools.partial(attention_body, rows=rows, heads=heads,...  25.4 us
    ppermute x22, starting transfers between devices, swap(): lax.ppermute(value, axis, [(s, s ^ flip) for s in range(lax.axis_size(axi...  21.9 us
    pallas_call x1, Pallas kernels, normed_grad(): pl.pallas_call(normed_grad_body, grid=(width // rows,), in_specs=[by_row,...  19.6 us
  transfers between devices with their start and end apart: 28, of which 11 were waited for; matrix products, arithmetic and copies ran while one was open for 17% of the time, Pallas kernels for 5%

profile of v4, /device:TPU:0, one launch (start us, length us, event | category | flops | bytes accessed | tf_op | source)
XLA Modules:
  0.0 600.3 jit_solution(8652777170039843113)
XLA Ops:
  10.6 8.3 %copy.20 = bf16[512,5376]{0,1:T(8,128)(2,1)} copy(bf16[512,5376]{1,0:T(8,128)(2,1)} %param.9) | data formatting | bytes 11010048 | tf_op args[0]
  18.9 4.4 fusion
  23.3 7.0 %fusion.2 = bf16[512,5376]{1,0:T(8,128)(2,1)} fusion(bf16[512,5376]{1,0:T(8,128)(2,1)} %param.9, f32[5376]{0:T(1024)S(1)} %copy-done.8, f32[512]{0:T(512)S(1)} %add_rsqrt_fusion), kind=kLoop, calls=%fused_computation.4 | loop fusion | flops 11010048 | bytes 11033600 | tf_op jit(solution)/shard_map/convert_element_type | solution.py:410
  30.3 4.6 multiply_convert_fusion
  36.1 80.5 %all-gather.7.cloned.1.call-done.wide_ref = bf16[5376,1024]{1,0:T(8,128)(2,1)} async-done(((bf16[672,1024]{1,0:T(8,128)(2,1)}), bf16[5376,1024]{1,0:T(8,128)(2,1)}) %all-gather.7.cloned.1.call-update) | async-done | bytes 11010064 | tf_op jit(solution)/shard_map/all_gather | solution.py:403
  116.7 11.2 %fusion.13.k_ref.v_ref = f32[512,1024]{1,0:T(8,128)} fusion(bf16[512,5376]{1,0:T(8,128)(2,1)} %fusion.2, bf16[5376,1024]{1,0:T(8,128)(2,1)} %all-gather.7.cloned.1.call-done.wide_ref), kind=kOutput, calls=%fused_computation.56 | convolution fusion | flops 5637144576 | bytes 18612224 | tf_op jit(solution)/shard_map/dot_general | solution.py:32
  127.9 3.8 key_rows.1.own_ref
  133.3 45.9 %collective-permute-done.far_ref = bf16[2,512,512]{2,1,0:T(8,128)(2,1)S(1)} collective-permute-done((bf16[2,512,512]{2,1,0:T(8,128)(2,1)}, bf16[2,512,512]{2,1,0:T(8,128)(2,1)S(1)}, u32[]{:S(2)}, u32[]{:S(2)}) %collective-permute-start) | collective-permute-done | bytes 1048608 | tf_op jit(solution)/shard_map/ppermute | solution.py:24
  181.9 55.3 %all-gather.5.cloned.1.call-done = bf16[5376,1024]{1,0:T(8,128)(2,1)} async-done(((bf16[672,1024]{1,0:T(8,128)(2,1)}), bf16[5376,1024]{1,0:T(8,128)(2,1)}) %all-gather.5.cloned.1.call-update) | async-done | bytes 11010064 | tf_op jit(solution)/shard_map/all_gather | solution.py:404
  237.2 11.2 %fusion.12.q_ref = f32[512,1024]{1,0:T(8,128)} fusion(bf16[512,5376]{1,0:T(8,128)(2,1)} %fusion.2, bf16[5376,1024]{1,0:T(8,128)(2,1)} %all-gather.5.cloned.1.call-done), kind=kOutput, calls=%fused_computation.55 | convolution fusion | flops 5637144576 | bytes 18612224 | tf_op jit(solution)/shard_map/dot_general | solution.py:32
  248.5 25.4 %attention.1 = (bf16[512,1024]{1,0:T(8,128)(2,1)}, f32[2,512,512]{2,1,0:T(8,128)}, bf16[2,512,512]{2,1,0:T(8,128)(2,1)S(1)}, bf16[2,512,512]{2,1,0:T(8,128)(2,1)S(1)}, f32[1,128]{1,0:T(1,128)S(1)}) custom-call(s32[1]{0:T(128)} %bitcast.start_ref, s32[4]{0:T(128)S(1)} %bitcast.72, f32[512,1024]{1,0:T(8,128)} %fusion.12.q_ref, ...), custom_call_target="tpu_custom_call" | custom-call | tf_op jit(solution)/shard_map/attention/pallas_call | solution.py:347
  280.4 65.2 %collective-permute-done.3.far_ref = bf16[2,512,512]{2,1,0:T(8,128)(2,1)S(1)} collective-permute-done((bf16[2,512,512]{2,1,0:T(8,128)(2,1)S(1)}, bf16[2,512,512]{2,1,0:T(8,128)(2,1)S(1)}, u32[]{:S(2)}, u32[]{:S(2)}) %collective-permute-start.3) | collective-permute-done | bytes 1048608 | tf_op jit(solution)/shard_map/ppermute | solution.py:24
  346.7 7.1 %key_grads.1 = (bf16[512,1024]{1,0:T(8,128)(2,1)}, f32[1,128]{1,0:T(1,128)}) custom-call(f32[2,512,512]{2,1,0:T(8,128)} %get-tuple-element.25.own_ref, bf16[2,512,512]{2,1,0:T(8,128)(2,1)} %get-tuple-element.50.near_ref, bf16[2,512,512]{2,1,0:T(8,128)(2,1)} %copy-done.7, f32[512,1024]{1,0:T(8,128)} %fusion.13.k_ref.v_ref, f32[1,128]{1,0:T(1,128)} %bitcast.85), custom_call_target="tpu_custom_call" | custom-call | tf_op jit(solution)/shard_map/key_grads/pallas_call | solution.py:141
  354.0 5.0 collective-permute-start.10
  362.4 11.7 %collective-permute-done.11 = bf16[2,168,512]{2,1,0:T(8,128)(2,1)S(1)} collective-permute-done((bf16[2,168,512]{2,1,0:T(8,128)(2,1)S(1)}, bf16[2,168,512]{2,1,0:T(8,128)(2,1)S(1)}, u32[]{:S(2)}, u32[]{:S(2)}) %collective-permute-start.11) | collective-permute-done | bytes 344096 | tf_op jit(solution)/shard_map/ppermute | solution.py:28
  374.1 32.5 %collective-permute-done.10 = bf16[2,168,512]{2,1,0:T(8,128)(2,1)S(1)} collective-permute-done((bf16[2,168,512]{2,1,0:T(8,128)(2,1)S(1)}, bf16[2,168,512]{2,1,0:T(8,128)(2,1)S(1)}, u32[]{:S(2)}, u32[]{:S(2)}) %collective-permute-start.10) | collective-permute-done | bytes 344096 | tf_op jit(solution)/shard_map/ppermute | solution.py:28
  406.9 11.4 %convolution_bitcast_fusion.part_ref = f32[5376,512]{1,0:T(8,128)} fusion(bf16[512,1024]{1,0:T(8,128)(2,1)} %get-tuple-element.24, bf16[5376,1024]{1,0:T(8,128)(2,1)} %all-gather.5.cloned.1.call-done), kind=kOutput, calls=%fused_computation.6 | convolution fusion | flops 5637144576 | bytes 23068672 | tf_op jit(solution)/shard_map/dot_general | solution.py:32
  431.8 19.6 %normed_grad.1 = (bf16[5376,512]{1,0:T(8,128)(2,1)}, f32[1,512]{1,0:T(1,128)}) custom-call(f32[5376,512]{1,0:T(8,128)} %convolution_bitcast_fusion.part_ref, bf16[5376,1024]{1,0:T(8,128)(2,1)} %all-gather.7.cloned.1.call-done.wide_ref, bf16[512,1024]{1,0:T(8,128)(2,1)} %get-tuple-element.28.d_ref, bf16[5376,512]{1,0:T(8,128)(2,1)} %bitcast.73, ...), custom_call_target="tpu_custom_call" | custom-call | tf_op jit(solution)/shard_map/normed_grad/pallas_call | solution.py:180
  453.6 4.5 collective-permute-done.19
  471.6 82.3 %collective-permute-done.8 = f32[1,512]{1,0:T(1,128)S(1)} collective-permute-done((f32[1,512]{1,0:T(1,128)S(1)}, f32[1,512]{1,0:T(1,128)S(1)}, u32[]{:S(2)}, u32[]{:S(2)}) %collective-permute-start.8) | collective-permute-done | bytes 2080 | tf_op jit(solution)/shard_map/ppermute | solution.py:28
  554.0 4.3 fusion.7
  569.4 11.1 %multiply_convert_fusion.1 = bf16[672,1024]{1,0:T(8,128)(2,1)} fusion(bf16[672,4096]{1,0:T(8,128)(2,1)} %bitcast.30.columns_ref, bf16[4096,1024]{1,0:T(8,128)(2,1)} %all-gather.9.cloned.1.call-done), kind=kOutput, calls=%fused_computation.14 | convolution fusion | flops 5638520832 | bytes 15269888 | tf_op jit(solution)/shard_map/dot_general | solution.py:32
  580.4 3.4 copy-done.1
  583.8 9.9 %weight_grads.1 = (bf16[672,512]{1,0:T(8,128)(2,1)}, bf16[672,512]{1,0:T(8,128)(2,1)}) custom-call(bf16[672,4096]{1,0:T(8,128)(2,1)} %bitcast.30.columns_ref, bf16[4096,1024]{1,0:T(8,128)(2,1)S(1)} %copy-done.1), custom_call_target="tpu_custom_call" | custom-call | tf_op jit(solution)/shard_map/weight_grads/pallas_call | solution.py:224
  (116 shorter events, 60.4 us)
Async XLA Ops:
  7.2 109.5 %all-gather.7.cloned.1.call-start = ((), (), s32[]{:S(2)}) async-start(), calls=%async_computation.1 | async-start | bytes 12386304 | tf_op jit(solution)/shard_map/all_gather | solution.py:403
  9.8 227.5 %all-gather.5.cloned.1.call-start = ((), (), s32[]{:S(2)}) async-start(), calls=%async_computation | async-start | bytes 12386304 | tf_op jit(solution)/shard_map/all_gather | solution.py:404
  10.5 558.8 %all-gather.9.cloned.1.call-start = ((), (), s32[]{:S(2)}) async-start(), calls=%async_computation.2 | async-start | bytes 9437184 | tf_op jit(solution)/shard_map/all_gather | solution.py:444
  131.7 47.5 %collective-permute-start = (bf16[2,512,512]{2,1,0:T(8,128)(2,1)}, bf16[2,512,512]{2,1,0:T(8,128)(2,1)S(1)}, u32[]{:S(2)}, u32[]{:S(2)}) collective-permute-start(bf16[2,512,512]{2,1,0:T(8,128)(2,1)} %key_rows.1.own_ref), channel_id=1, source_target_pairs={{0,8},{4,12},{8,16},{12,20},{16,24},{20,28},{1,9},{5,13},{9,17},{1... | collective-permute-start | bytes 3145736 | tf_op jit(solution)/shard_map/ppermute | solution.py:24
  181.9 66.5 %collective-permute-start.1 = (bf16[2,512,512]{2,1,0:T(8,128)(2,1)}, bf16[2,512,512]{2,1,0:T(8,128)(2,1)}, u32[]{:S(2)}, u32[]{:S(2)}) collective-permute-start(bf16[2,512,512]{2,1,0:T(8,128)(2,1)} %broadcast_select_fusion.1), channel_id=1, source_target_pairs={{0,4},{4,0},{8,12},{12,8},{16,20},{20,16},{24,28},{28,24},{1,5},{5... | collective-permute-start | bytes 3145736 | tf_op jit(solution)/shard_map/ppermute | solution.py:28
  274.9 305.6 %all-gather.11.cloned.1.call-start = ((), (), s32[]{:S(2)}) async-start(), calls=%async_computation.3 | async-start | bytes 9437184 | tf_op jit(solution)/shard_map/all_gather | solution.py:456
  279.0 66.7 %collective-permute-start.3 = (bf16[2,512,512]{2,1,0:T(8,128)(2,1)S(1)}, bf16[2,512,512]{2,1,0:T(8,128)(2,1)S(1)}, u32[]{:S(2)}, u32[]{:S(2)}) collective-permute-start(bf16[2,512,512]{2,1,0:T(8,128)(2,1)S(1)} %get-tuple-element.49), channel_id=1, source_target_pairs={{8,0},{12,4},{16,8},{20,12},{24,16},{28,20},{9,1},{13,5},{17,9},{2... | collective-permute-start | bytes 3145736 | tf_op jit(solution)/shard_map/ppermute | solution.py:24
  353.9 20.2 %collective-permute-start.11 = (bf16[2,168,512]{2,1,0:T(8,128)(2,1)S(1)}, bf16[2,168,512]{2,1,0:T(8,128)(2,1)S(1)}, u32[]{:S(2)}, u32[]{:S(2)}) collective-permute-start(bf16[2,168,512]{2,1,0:T(8,128)(2,1)S(1)} %get-tuple-element.46), channel_id=1, source_target_pairs={{0,24},{4,28},{8,16},{12,20},{16,8},{20,12},{24,0},{28,4},{1,25},{... | collective-permute-start | bytes 1032200 | tf_op jit(solution)/shard_map/ppermute | solution.py:28
  354.0 52.6 %collective-permute-start.10 = (bf16[2,168,512]{2,1,0:T(8,128)(2,1)S(1)}, bf16[2,168,512]{2,1,0:T(8,128)(2,1)S(1)}, u32[]{:S(2)}, u32[]{:S(2)}) collective-permute-start(bf16[2,168,512]{2,1,0:T(8,128)(2,1)S(1)} %get-tuple-element.47), channel_id=1, source_target_pairs={{0,16},{4,20},{8,24},{12,28},{16,0},{20,4},{24,8},{28,12},{1,17},{... | collective-permute-start | bytes 1032200 | tf_op jit(solution)/shard_map/ppermute | solution.py:28
  359.0 47.6 %collective-permute-start.9 = (bf16[2,168,512]{2,1,0:T(8,128)(2,1)S(1)}, bf16[2,168,512]{2,1,0:T(8,128)(2,1)S(1)}, u32[]{:S(2)}, u32[]{:S(2)}) collective-permute-start(bf16[2,168,512]{2,1,0:T(8,128)(2,1)S(1)} %get-tuple-element.48), channel_id=1, source_target_pairs={{0,8},{4,12},{8,0},{12,4},{16,24},{20,28},{24,16},{28,20},{1,9},{5... | collective-permute-start | bytes 1032200 | tf_op jit(solution)/shard_map/ppermute | solution.py:28
  406.8 11.5 %collective-permute-start.12 = (bf16[4,168,512]{2,1,0:T(8,128)(2,1)S(1)}, bf16[4,168,512]{2,1,0:T(8,128)(2,1)S(1)}, u32[]{:S(2)}, u32[]{:S(2)}) collective-permute-start(bf16[4,168,512]{2,1,0:T(8,128)(2,1)S(1)} %dynamic-slice_bitcast_fusion), channel_id=1, source_target_pairs={{0,4},{4,0},{8,12},{12,8},{16,20},{20,16},{24,28},{28,24},{1,5},{5... | collective-permute-start | bytes 2064392 | tf_op jit(solution)/shard_map/ppermute | solution.py:28
  423.7 43.7 %collective-permute-start.14 = (bf16[168,4096]{1,0:T(8,128)(2,1)}, bf16[168,4096]{1,0:T(8,128)(2,1)S(1)}, u32[]{:S(2)}, u32[]{:S(2)}) collective-permute-start(bf16[168,4096]{1,0:T(8,128)(2,1)} %reshape.93), channel_id=1, source_target_pairs={{0,2},{1,3},{2,0},{3,1},{4,6},{5,7},{6,4},{7,5},{8,10},{9,11},{10,... | collective-permute-start | bytes 4128776 | tf_op jit(solution)/shard_map/ppermute | solution.py:28
  425.4 38.8 %collective-permute-start.13 = (bf16[168,4096]{1,0:T(8,128)(2,1)}, bf16[168,4096]{1,0:T(8,128)(2,1)}, u32[]{:S(2)}, u32[]{:S(2)}) collective-permute-start(bf16[168,4096]{1,0:T(8,128)(2,1)} %reshape.93), channel_id=1, source_target_pairs={{0,1},{1,0},{2,3},{3,2},{4,5},{5,4},{6,7},{7,6},{8,9},{9,8},{10,11... | collective-permute-start | bytes 4128776 | tf_op jit(solution)/shard_map/ppermute | solution.py:28
  426.9 31.2 %collective-permute-start.19 = (f32[2,128]{1,0:T(2,128)S(1)}, f32[2,128]{1,0:T(2,128)S(1)}, u32[]{:S(2)}, u32[]{:S(2)}) collective-permute-start(f32[2,128]{1,0:T(2,128)S(1)} %pad_maximum_fusion.3), channel_id=1, source_target_pairs={{0,1},{1,0},{2,3},{3,2},{4,5},{5,4},{6,7},{7,6},{8,9},{9,8},{10,11... | collective-permute-start | bytes 3080 | tf_op jit(solution)/shard_map/ppermute | solution.py:28
  452.1 12.6 %collective-permute-start.7 = (f32[1,512]{1,0:T(1,128)S(1)}, f32[1,512]{1,0:T(1,128)S(1)}, u32[]{:S(2)}, u32[]{:S(2)}) collective-permute-start(f32[1,512]{1,0:T(1,128)S(1)} %mul.156), channel_id=1, source_target_pairs={{0,1},{1,0},{2,3},{3,2},{4,5},{5,4},{6,7},{7,6},{8,9},{9,8},{10,11... | collective-permute-start | bytes 6152 | tf_op jit(solution)/shard_map/ppermute | solution.py:28
  458.1 4.6 collective-permute-start.20
  461.0 92.9 %collective-permute-start.4 = (bf16[1344,512]{1,0:T(8,128)(2,1)S(1)}, bf16[1344,512]{1,0:T(8,128)(2,1)S(1)}, u32[]{:S(2)}, u32[]{:S(2)}) collective-permute-start(bf16[1344,512]{1,0:T(8,128)(2,1)S(1)} %get-tuple-element.40), channel_id=1, source_target_pairs={{0,1},{1,0},{2,3},{3,2},{4,5},{5,4},{6,7},{7,6},{8,9},{9,8},{10,11... | collective-permute-start | bytes 4128776 | tf_op jit(solution)/shard_map/ppermute | solution.py:28
  462.7 91.2 %collective-permute-start.6 = (bf16[1344,512]{1,0:T(8,128)(2,1)S(1)}, bf16[1344,512]{1,0:T(8,128)(2,1)S(1)}, u32[]{:S(2)}, u32[]{:S(2)}) collective-permute-start(bf16[1344,512]{1,0:T(8,128)(2,1)S(1)} %get-tuple-element.41), channel_id=1, source_target_pairs={{0,3},{1,2},{2,1},{3,0},{4,7},{5,6},{6,5},{7,4},{8,11},{9,10},{10,... | collective-permute-start | bytes 4128776 | tf_op jit(solution)/shard_map/ppermute | solution.py:28
  464.2 89.7 %collective-permute-start.5 = (bf16[1344,512]{1,0:T(8,128)(2,1)S(1)}, bf16[1344,512]{1,0:T(8,128)(2,1)S(1)}, u32[]{:S(2)}, u32[]{:S(2)}) collective-permute-start(bf16[1344,512]{1,0:T(8,128)(2,1)S(1)} %get-tuple-element.42), channel_id=1, source_target_pairs={{0,2},{1,3},{2,0},{3,1},{4,6},{5,7},{6,4},{7,5},{8,10},{9,11},{10,... | collective-permute-start | bytes 4128776 | tf_op jit(solution)/shard_map/ppermute | solution.py:28
  464.8 5.1 collective-permute-start.21
  467.4 90.9 %collective-permute-start.15 = (bf16[168,4096]{1,0:T(8,128)(2,1)S(1)}, bf16[168,4096]{1,0:T(8,128)(2,1)S(1)}, u32[]{:S(2)}, u32[]{:S(2)}) collective-permute-start(bf16[168,4096]{1,0:T(8,128)(2,1)S(1)} %copy-done.6), channel_id=1, source_target_pairs={{0,3},{1,2},{2,1},{3,0},{4,7},{5,6},{6,5},{7,4},{8,11},{9,10},{10,... | collective-permute-start | bytes 4128776 | tf_op jit(solution)/shard_map/ppermute | solution.py:28
  469.9 84.0 %collective-permute-start.8 = (f32[1,512]{1,0:T(1,128)S(1)}, f32[1,512]{1,0:T(1,128)S(1)}, u32[]{:S(2)}, u32[]{:S(2)}) collective-permute-start(f32[1,512]{1,0:T(1,128)S(1)} %add.133), channel_id=1, source_target_pairs={{0,2},{1,3},{2,0},{3,1},{4,6},{5,7},{6,4},{7,5},{8,10},{9,11},{10,... | collective-permute-start | bytes 6152 | tf_op jit(solution)/shard_map/ppermute | solution.py:28
  553.9 5.7 collective-permute-start.22
  564.1 4.6 collective-permute-start.18
  (16 other events, 255.8 us)
Sparse Core Ops, SparseCore 0:
  10.2 106.4 all-gather.6
  118.3 118.8 all-gather.4
  275.0 128.8 all-gather.8
  405.4 80.1 all-gather.10

commit v5 on v4

--- a/solution.py
+++ b/solution.py
@@ -160,22 +160,22 @@
     )(own, near, far, projected, gain[None, :])
 
 
-def normed_grad_body(part_ref, wide_ref, d_ref, x_ref, gain_ref, out_ref, dots_ref):
-    rounded = (part_ref[...] + dot(wide_ref[...], d_ref[...], NT)).astype(jnp.bfloat16)
+def normed_grad_body(part_ref, wide_ref, d_ref, x_ref, gain_ref, out_ref, dots_ref, dt_ref):
+    @pl.when(pl.program_id(0) == 0)
+    def _():
+        dots_ref[...] = jnp.zeros_like(dots_ref)
+        dt_ref[...] = jnp.transpose(d_ref[...])
+
+    rounded = (part_ref[...] + dot(wide_ref[...], dt_ref[...])).astype(jnp.bfloat16)
     out_ref[...] = rounded
-
-    @pl.when(pl.program_id(0) == 0)
-    def _():
-        dots_ref[...] = jnp.zeros_like(dots_ref)
-
     gained = x_ref[...].astype(jnp.float32) * gain_ref[...]
     dots_ref[...] += jnp.sum(rounded.astype(jnp.float32) * gained, axis=0, keepdims=True)
 
 
-def normed_grad(part, wide, d, turned, gain):
+def normed_grad(part, wide, d, turned, gain_column):
     width, tokens = part.shape
     cols = wide.shape[1]
-    rows = max(r for r in range(128, 513, 128) if width % r == 0)
+    rows = max(r for r in range(128, 897, 128) if width % r == 0)
     by_row = pl.BlockSpec((rows, tokens), lambda i: (i, 0))
     return pl.pallas_call(
         normed_grad_body,
@@ -192,8 +192,10 @@
             jax.ShapeDtypeStruct((width, tokens), jnp.bfloat16),
             jax.ShapeDtypeStruct((1, tokens), jnp.float32),
         ),
+        scratch_shapes=[pltpu.VMEM((cols, tokens), jnp.bfloat16)],
+        compiler_params=pltpu.CompilerParams(vmem_limit_bytes=40 << 20),
         name="normed_grad",
-    )(part, wide, d, turned, gain[:, None])
+    )(part, wide, d, turned, gain_column)
 
 
 def weight_grad_body(columns_ref, d_ref, k_ref, v_ref, sum_ref, *, scale):
@@ -415,7 +417,9 @@
     normed_turned = (turned.astype(jnp.float32) * inv_row * norm_gain[:, None]).astype(
         jnp.bfloat16
     )
-    blocks, own = lax.optimization_barrier((share_of_columns(normed_turned, shard_rows), own))
+    blocks, gain_column, own = lax.optimization_barrier(
+        (share_of_columns(normed_turned, shard_rows), norm_gain[:, None], own)
+    )
     far = shift(own, "ctx", REACH)
     picked = jnp.where(on_first_core, own, far)
     near = swap(picked, "ctx", 1)
@@ -457,7 +461,7 @@
 
     columns = finish_columns(pieces, dq16)
 
-    head_part, row_dot = normed_grad(query_part, wide_kv, dkv16, turned, norm_gain)
+    head_part, row_dot = normed_grad(query_part, wide_kv, dkv16, turned, gain_column)
     row_dot = everywhere(row_dot * inv_row, ("fsdp",))
 
     def part_of(array, index):

time: 601 us -> 607 us (level)
  starting transfers between devices: 24.9 us -> 33.2 us
  Pallas kernels: 65.9 us -> 59.2 us
    ppermute x22, starting transfers between devices: 21.9 us -> 30.2 us  [swap(): lax.ppermute(value, axis, [(s, s ^ flip) for s in range(lax.axis_size(axi...]
    pallas_call x1, Pallas kernels: 19.6 us -> 13 us  [normed_grad(): pl.pallas_call(normed_grad_body, grid=(width // rows,), in_specs=[by_row,...]
    unnamed x25 -> x29, local copies, waits for them, and re-layouts: 13.7 us -> 14.2 us
  transfers between devices with their start and end apart: 28 -> 28, of which waited for: 11 -> 11; matrix products, arithmetic and copies ran while one was open for 17% -> 17% of each run, Pallas kernels for 5% -> 4%
where the time goes in v5:
time: 607 us; the launch traced here: 606 us
  waiting for transfers between devices  387 us (64%)
  Pallas kernels  59.2 us (10%)
  matrix products  44.9 us (7%)
  local copies, waits for them, and re-layouts  37.6 us (6%)
  starting transfers between devices  33.2 us (5%)
  other arithmetic  29.9 us (5%)
  between operations  14.1 us (2%)
    ppermute x22, waiting for transfers between devices, swap(): lax.ppermute(value, axis, [(s, s ^ flip) for s in range(lax.axis_size(axi...  139 us
    ppermute x2, waiting for transfers between devices, shift(): lax.ppermute(value, axis, [(s, s + steps) for s in range(initial, last)])  111 us
    all_gather x1, waiting for transfers between devices, layer(): wide_kv = lax.all_gather(key_value, 'ctx', axis=0, tiled=True)  80.5 us
    all_gather x1, waiting for transfers between devices, layer(): wide_q = lax.all_gather(w_query, 'ctx', axis=0, tiled=True)  55.3 us
    dot_general x4, matrix products, dot(): return lax.dot_general(a, b, dims, preferred_element_type=jnp.float32)  44.9 us
    ppermute x22, starting transfers between devices, swap(): lax.ppermute(value, axis, [(s, s ^ flip) for s in range(lax.axis_size(axi...  30.2 us
    pallas_call x1, Pallas kernels, attention(): pl.pallas_call(functools.partial(attention_body, rows=rows, heads=heads,...  25.4 us
    unnamed x29, local copies, waits for them, and re-layouts  14.2 us
  transfers between devices with their start and end apart: 28, of which 11 were waited for; matrix products, arithmetic and copies ran while one was open for 17% of the time, Pallas kernels for 4%

profile of v5, /device:TPU:0, one launch (start us, length us, event | category | flops | bytes accessed | tf_op | source)
XLA Modules:
  0.0 606.0 jit_solution(12400743981281813966)
XLA Ops:
  10.6 8.3 %copy.20 = bf16[512,5376]{0,1:T(8,128)(2,1)} copy(bf16[512,5376]{1,0:T(8,128)(2,1)} %param.9) | data formatting | bytes 11010048 | tf_op args[0]
  18.9 4.4 fusion
  23.3 7.0 %fusion.2 = bf16[512,5376]{1,0:T(8,128)(2,1)} fusion(bf16[512,5376]{1,0:T(8,128)(2,1)} %param.9, f32[5376]{0:T(1024)S(1)} %copy-done.10, f32[512]{0:T(512)S(1)} %add_rsqrt_fusion), kind=kLoop, calls=%fused_computation.4 | loop fusion | flops 11010048 | bytes 11033600 | tf_op jit(solution)/shard_map/convert_element_type | solution.py:412
  30.3 4.6 multiply_convert_fusion
  36.1 80.5 %all-gather.7.cloned.1.call-done.wide_ref = bf16[5376,1024]{1,0:T(8,128)(2,1)} async-done(((bf16[672,1024]{1,0:T(8,128)(2,1)}), bf16[5376,1024]{1,0:T(8,128)(2,1)}) %all-gather.7.cloned.1.call-update) | async-done | bytes 11010064 | tf_op jit(solution)/shard_map/all_gather | solution.py:405
  116.7 11.2 %fusion.13.k_ref.v_ref = f32[512,1024]{1,0:T(8,128)} fusion(bf16[512,5376]{1,0:T(8,128)(2,1)} %fusion.2, bf16[5376,1024]{1,0:T(8,128)(2,1)} %all-gather.7.cloned.1.call-done.wide_ref), kind=kOutput, calls=%fused_computation.56 | convolution fusion | flops 5637144576 | bytes 18612224 | tf_op jit(solution)/shard_map/dot_general | solution.py:32
  133.3 45.9 %collective-permute-done.far_ref = bf16[2,512,512]{2,1,0:T(8,128)(2,1)S(1)} collective-permute-done((bf16[2,512,512]{2,1,0:T(8,128)(2,1)}, bf16[2,512,512]{2,1,0:T(8,128)(2,1)S(1)}, u32[]{:S(2)}, u32[]{:S(2)}) %collective-permute-start) | collective-permute-done | bytes 1048608 | tf_op jit(solution)/shard_map/ppermute | solution.py:24
  181.9 55.3 %all-gather.5.cloned.1.call-done = bf16[5376,1024]{1,0:T(8,128)(2,1)} async-done(((bf16[672,1024]{1,0:T(8,128)(2,1)}), bf16[5376,1024]{1,0:T(8,128)(2,1)}) %all-gather.5.cloned.1.call-update) | async-done | bytes 11010064 | tf_op jit(solution)/shard_map/all_gather | solution.py:406
  237.2 11.2 %fusion.12.q_ref = f32[512,1024]{1,0:T(8,128)} fusion(bf16[512,5376]{1,0:T(8,128)(2,1)} %fusion.2, bf16[5376,1024]{1,0:T(8,128)(2,1)} %all-gather.5.cloned.1.call-done), kind=kOutput, calls=%fused_computation.55 | convolution fusion | flops 5637144576 | bytes 18612224 | tf_op jit(solution)/shard_map/dot_general | solution.py:32
  248.5 25.4 %attention.1 = (bf16[512,1024]{1,0:T(8,128)(2,1)}, f32[2,512,512]{2,1,0:T(8,128)}, bf16[2,512,512]{2,1,0:T(8,128)(2,1)S(1)}, bf16[2,512,512]{2,1,0:T(8,128)(2,1)S(1)}, f32[1,128]{1,0:T(1,128)S(1)}) custom-call(s32[1]{0:T(128)} %bitcast.start_ref, s32[4]{0:T(128)S(1)} %bitcast.72, f32[512,1024]{1,0:T(8,128)} %fusion.12.q_ref, ...), custom_call_target="tpu_custom_call" | custom-call | tf_op jit(solution)/shard_map/attention/pallas_call | solution.py:349
  280.4 65.2 %collective-permute-done.3.far_ref = bf16[2,512,512]{2,1,0:T(8,128)(2,1)S(1)} collective-permute-done((bf16[2,512,512]{2,1,0:T(8,128)(2,1)S(1)}, bf16[2,512,512]{2,1,0:T(8,128)(2,1)S(1)}, u32[]{:S(2)}, u32[]{:S(2)}) %collective-permute-start.3) | collective-permute-done | bytes 1048608 | tf_op jit(solution)/shard_map/ppermute | solution.py:24
  346.6 7.1 %key_grads.1 = (bf16[512,1024]{1,0:T(8,128)(2,1)}, f32[1,128]{1,0:T(1,128)}) custom-call(f32[2,512,512]{2,1,0:T(8,128)} %get-tuple-element.26.own_ref, bf16[2,512,512]{2,1,0:T(8,128)(2,1)} %get-tuple-element.52.near_ref, bf16[2,512,512]{2,1,0:T(8,128)(2,1)} %copy-done.9, f32[512,1024]{1,0:T(8,128)} %fusion.13.k_ref.v_ref, f32[1,128]{1,0:T(1,128)} %bitcast.82), custom_call_target="tpu_custom_call" | custom-call | tf_op jit(solution)/shard_map/key_grads/pallas_call | solution.py:141
  361.5 28.1 %collective-permute-done.9 = bf16[2,168,512]{2,1,0:T(8,128)(2,1)} collective-permute-done((bf16[2,168,512]{2,1,0:T(8,128)(2,1)}, bf16[2,168,512]{2,1,0:T(8,128)(2,1)}, u32[]{:S(2)}, u32[]{:S(2)}) %collective-permute-start.9) | collective-permute-done | bytes 344096 | tf_op jit(solution)/shard_map/ppermute | solution.py:28
  389.6 10.7 %collective-permute-done.10 = bf16[2,168,512]{2,1,0:T(8,128)(2,1)} collective-permute-done((bf16[2,168,512]{2,1,0:T(8,128)(2,1)}, bf16[2,168,512]{2,1,0:T(8,128)(2,1)}, u32[]{:S(2)}, u32[]{:S(2)}) %collective-permute-start.10) | collective-permute-done | bytes 344096 | tf_op jit(solution)/shard_map/ppermute | solution.py:28
  401.8 11.4 %convolution_bitcast_fusion.part_ref = f32[5376,512]{1,0:T(8,128)} fusion(bf16[512,1024]{1,0:T(8,128)(2,1)} %get-tuple-element.25, bf16[5376,1024]{1,0:T(8,128)(2,1)} %all-gather.5.cloned.1.call-done), kind=kOutput, calls=%fused_computation.6 | convolution fusion | flops 5637144576 | bytes 23068672 | tf_op jit(solution)/shard_map/dot_general | solution.py:32
  416.5 4.5 broadcast_in_dim.42
  421.1 4.5 reshape.93
  434.2 13.0 %normed_grad.1 = (bf16[5376,512]{1,0:T(8,128)(2,1)S(1)}, f32[1,512]{1,0:T(1,128)S(1)}) custom-call(f32[5376,512]{1,0:T(8,128)} %convolution_bitcast_fusion.part_ref, bf16[5376,1024]{1,0:T(8,128)(2,1)} %all-gather.7.cloned.1.call-done.wide_ref, bf16[512,1024]{1,0:T(8,128)(2,1)S(1)} %copy-done.2, bf16[5376,512]{1,0:T(8,128)(2,1)} %bitcast.73, ...), custom_call_target="tpu_custom_call" | custom-call | tf_op jit(solution)/shard_map/normed_grad/pallas_call | solution.py:180
  448.7 9.7 %collective-permute-done.19 = f32[2,128]{1,0:T(2,128)S(1)} collective-permute-done((f32[2,128]{1,0:T(2,128)S(1)}, f32[2,128]{1,0:T(2,128)S(1)}, u32[]{:S(2)}, u32[]{:S(2)}) %collective-permute-start.19) | collective-permute-done | bytes 1056 | tf_op jit(solution)/shard_map/ppermute | solution.py:28
  469.7 82.5 %collective-permute-done.8 = f32[1,512]{1,0:T(1,128)S(1)} collective-permute-done((f32[1,512]{1,0:T(1,128)S(1)}, f32[1,512]{1,0:T(1,128)S(1)}, u32[]{:S(2)}, u32[]{:S(2)}) %collective-permute-start.8) | collective-permute-done | bytes 2080 | tf_op jit(solution)/shard_map/ppermute | solution.py:28
  552.2 7.9 %collective-permute-start.22 = (f32[2,128]{1,0:T(2,128)S(1)}, f32[2,128]{1,0:T(2,128)S(1)}, u32[]{:S(2)}, u32[]{:S(2)}) collective-permute-start(f32[2,128]{1,0:T(2,128)S(1)} %add.150), channel_id=1, source_target_pairs={{0,8},{4,12},{8,0},{12,4},{16,24},{20,28},{24,16},{28,20},{1,9},{5... | collective-permute-start | bytes 3080 | tf_op jit(solution)/shard_map/ppermute | solution.py:28
  560.2 3.9 fusion.7
  575.1 11.1 %multiply_convert_fusion.1 = bf16[672,1024]{1,0:T(8,128)(2,1)} fusion(bf16[672,4096]{1,0:T(8,128)(2,1)} %bitcast.30.columns_ref, bf16[4096,1024]{1,0:T(8,128)(2,1)} %all-gather.9.cloned.1.call-done), kind=kOutput, calls=%fused_computation.14 | convolution fusion | flops 5638520832 | bytes 15269888 | tf_op jit(solution)/shard_map/dot_general | solution.py:32
  589.6 9.9 %weight_grads.1 = (bf16[672,512]{1,0:T(8,128)(2,1)}, bf16[672,512]{1,0:T(8,128)(2,1)}) custom-call(bf16[672,4096]{1,0:T(8,128)(2,1)} %bitcast.30.columns_ref, bf16[4096,1024]{1,0:T(8,128)(2,1)S(1)} %copy-done.1), custom_call_target="tpu_custom_call" | custom-call | tf_op jit(solution)/shard_map/weight_grads/pallas_call | solution.py:226
  (121 shorter events, 68.5 us)
Async XLA Ops:
  7.2 109.5 %all-gather.7.cloned.1.call-start = ((), (), s32[]{:S(2)}) async-start(), calls=%async_computation.1 | async-start | bytes 12386304 | tf_op jit(solution)/shard_map/all_gather | solution.py:405
  9.8 227.5 %all-gather.5.cloned.1.call-start = ((), (), s32[]{:S(2)}) async-start(), calls=%async_computation | async-start | bytes 12386304 | tf_op jit(solution)/shard_map/all_gather | solution.py:406
  10.5 564.6 %all-gather.9.cloned.1.call-start = ((), (), s32[]{:S(2)}) async-start(), calls=%async_computation.2 | async-start | bytes 9437184 | tf_op jit(solution)/shard_map/all_gather | solution.py:448
  131.7 47.5 %collective-permute-start = (bf16[2,512,512]{2,1,0:T(8,128)(2,1)}, bf16[2,512,512]{2,1,0:T(8,128)(2,1)S(1)}, u32[]{:S(2)}, u32[]{:S(2)}) collective-permute-start(bf16[2,512,512]{2,1,0:T(8,128)(2,1)} %key_rows.1.own_ref), channel_id=1, source_target_pairs={{0,8},{4,12},{8,16},{12,20},{16,24},{20,28},{1,9},{5,13},{9,17},{1... | collective-permute-start | bytes 3145736 | tf_op jit(solution)/shard_map/ppermute | solution.py:24
  181.9 66.5 %collective-permute-start.1 = (bf16[2,512,512]{2,1,0:T(8,128)(2,1)}, bf16[2,512,512]{2,1,0:T(8,128)(2,1)}, u32[]{:S(2)}, u32[]{:S(2)}) collective-permute-start(bf16[2,512,512]{2,1,0:T(8,128)(2,1)} %broadcast_select_fusion.1), channel_id=1, source_target_pairs={{0,4},{4,0},{8,12},{12,8},{16,20},{20,16},{24,28},{28,24},{1,5},{5... | collective-permute-start | bytes 3145736 | tf_op jit(solution)/shard_map/ppermute | solution.py:28
  274.8 311.3 %all-gather.11.cloned.1.call-start = ((), (), s32[]{:S(2)}) async-start(), calls=%async_computation.3 | async-start | bytes 9437184 | tf_op jit(solution)/shard_map/all_gather | solution.py:460
  278.9 66.7 %collective-permute-start.3 = (bf16[2,512,512]{2,1,0:T(8,128)(2,1)S(1)}, bf16[2,512,512]{2,1,0:T(8,128)(2,1)S(1)}, u32[]{:S(2)}, u32[]{:S(2)}) collective-permute-start(bf16[2,512,512]{2,1,0:T(8,128)(2,1)S(1)} %get-tuple-element.51), channel_id=1, source_target_pairs={{8,0},{12,4},{16,8},{20,12},{24,16},{28,20},{9,1},{13,5},{17,9},{2... | collective-permute-start | bytes 3145736 | tf_op jit(solution)/shard_map/ppermute | solution.py:24
  354.8 34.9 %collective-permute-start.9 = (bf16[2,168,512]{2,1,0:T(8,128)(2,1)}, bf16[2,168,512]{2,1,0:T(8,128)(2,1)}, u32[]{:S(2)}, u32[]{:S(2)}) collective-permute-start(bf16[2,168,512]{2,1,0:T(8,128)(2,1)} %get-tuple-element.50), channel_id=1, source_target_pairs={{0,8},{4,12},{8,0},{12,4},{16,24},{20,28},{24,16},{28,20},{1,9},{5... | collective-permute-start | bytes 1032200 | tf_op jit(solution)/shard_map/ppermute | solution.py:28
  358.3 42.0 %collective-permute-start.10 = (bf16[2,168,512]{2,1,0:T(8,128)(2,1)}, bf16[2,168,512]{2,1,0:T(8,128)(2,1)}, u32[]{:S(2)}, u32[]{:S(2)}) collective-permute-start(bf16[2,168,512]{2,1,0:T(8,128)(2,1)} %get-tuple-element.49), channel_id=1, source_target_pairs={{0,16},{4,20},{8,24},{12,28},{16,0},{20,4},{24,8},{28,12},{1,17},{... | collective-permute-start | bytes 1032200 | tf_op jit(solution)/shard_map/ppermute | solution.py:28
  358.3 42.0 %collective-permute-start.11 = (bf16[2,168,512]{2,1,0:T(8,128)(2,1)S(1)}, bf16[2,168,512]{2,1,0:T(8,128)(2,1)}, u32[]{:S(2)}, u32[]{:S(2)}) collective-permute-start(bf16[2,168,512]{2,1,0:T(8,128)(2,1)S(1)} %get-tuple-element.48), channel_id=1, source_target_pairs={{0,24},{4,28},{8,16},{12,20},{16,8},{20,12},{24,0},{28,4},{1,25},{... | collective-permute-start | bytes 1032200 | tf_op jit(solution)/shard_map/ppermute | solution.py:28
  401.7 11.5 %collective-permute-start.12 = (bf16[4,168,512]{2,1,0:T(8,128)(2,1)S(1)}, bf16[4,168,512]{2,1,0:T(8,128)(2,1)S(1)}, u32[]{:S(2)}, u32[]{:S(2)}) collective-permute-start(bf16[4,168,512]{2,1,0:T(8,128)(2,1)S(1)} %dynamic-slice_bitcast_fusion), channel_id=1, source_target_pairs={{0,4},{4,0},{8,12},{12,8},{16,20},{20,16},{24,28},{28,24},{1,5},{5... | collective-permute-start | bytes 2064392 | tf_op jit(solution)/shard_map/ppermute | solution.py:28
  425.6 38.2 %collective-permute-start.13 = (bf16[168,4096]{1,0:T(8,128)(2,1)}, bf16[168,4096]{1,0:T(8,128)(2,1)S(1)}, u32[]{:S(2)}, u32[]{:S(2)}) collective-permute-start(bf16[168,4096]{1,0:T(8,128)(2,1)} %reshape.93), channel_id=1, source_target_pairs={{0,1},{1,0},{2,3},{3,2},{4,5},{5,4},{6,7},{7,6},{8,9},{9,8},{10,11... | collective-permute-start | bytes 4128776 | tf_op jit(solution)/shard_map/ppermute | solution.py:28
  427.3 39.2 %collective-permute-start.14 = (bf16[168,4096]{1,0:T(8,128)(2,1)}, bf16[168,4096]{1,0:T(8,128)(2,1)S(1)}, u32[]{:S(2)}, u32[]{:S(2)}) collective-permute-start(bf16[168,4096]{1,0:T(8,128)(2,1)} %reshape.93), channel_id=1, source_target_pairs={{0,2},{1,3},{2,0},{3,1},{4,6},{5,7},{6,4},{7,5},{8,10},{9,11},{10,... | collective-permute-start | bytes 4128776 | tf_op jit(solution)/shard_map/ppermute | solution.py:28
  428.8 29.6 %collective-permute-start.19 = (f32[2,128]{1,0:T(2,128)S(1)}, f32[2,128]{1,0:T(2,128)S(1)}, u32[]{:S(2)}, u32[]{:S(2)}) collective-permute-start(f32[2,128]{1,0:T(2,128)S(1)} %pad_maximum_fusion.3), channel_id=1, source_target_pairs={{0,1},{1,0},{2,3},{3,2},{4,5},{5,4},{6,7},{7,6},{8,9},{9,8},{10,11... | collective-permute-start | bytes 3080 | tf_op jit(solution)/shard_map/ppermute | solution.py:28
  447.2 18.1 %collective-permute-start.7 = (f32[1,512]{1,0:T(1,128)S(1)}, f32[1,512]{1,0:T(1,128)S(1)}, u32[]{:S(2)}, u32[]{:S(2)}) collective-permute-start(f32[1,512]{1,0:T(1,128)S(1)} %mul.156), channel_id=1, source_target_pairs={{0,1},{1,0},{2,3},{3,2},{4,5},{5,4},{6,7},{7,6},{8,9},{9,8},{10,11... | collective-permute-start | bytes 6152 | tf_op jit(solution)/shard_map/ppermute | solution.py:28
  460.5 99.6 %collective-permute-start.4 = (bf16[1344,512]{1,0:T(8,128)(2,1)S(1)}, bf16[1344,512]{1,0:T(8,128)(2,1)S(1)}, u32[]{:S(2)}, u32[]{:S(2)}) collective-permute-start(bf16[1344,512]{1,0:T(8,128)(2,1)S(1)} %get-tuple-element.42), channel_id=1, source_target_pairs={{0,1},{1,0},{2,3},{3,2},{4,5},{5,4},{6,7},{7,6},{8,9},{9,8},{10,11... | collective-permute-start | bytes 4128776 | tf_op jit(solution)/shard_map/ppermute | solution.py:28
  462.1 98.1 %collective-permute-start.5 = (bf16[1344,512]{1,0:T(8,128)(2,1)S(1)}, bf16[1344,512]{1,0:T(8,128)(2,1)S(1)}, u32[]{:S(2)}, u32[]{:S(2)}) collective-permute-start(bf16[1344,512]{1,0:T(8,128)(2,1)S(1)} %get-tuple-element.44), channel_id=1, source_target_pairs={{0,2},{1,3},{2,0},{3,1},{4,6},{5,7},{6,4},{7,5},{8,10},{9,11},{10,... | collective-permute-start | bytes 4128776 | tf_op jit(solution)/shard_map/ppermute | solution.py:28
  463.8 96.3 %collective-permute-start.6 = (bf16[1344,512]{1,0:T(8,128)(2,1)S(1)}, bf16[1344,512]{1,0:T(8,128)(2,1)S(1)}, u32[]{:S(2)}, u32[]{:S(2)}) collective-permute-start(bf16[1344,512]{1,0:T(8,128)(2,1)S(1)} %get-tuple-element.43), channel_id=1, source_target_pairs={{0,3},{1,2},{2,1},{3,0},{4,7},{5,6},{6,5},{7,4},{8,11},{9,10},{10,... | collective-permute-start | bytes 4128776 | tf_op jit(solution)/shard_map/ppermute | solution.py:28
  466.6 97.5 %collective-permute-start.15 = (bf16[168,4096]{1,0:T(8,128)(2,1)S(1)}, bf16[168,4096]{1,0:T(8,128)(2,1)S(1)}, u32[]{:S(2)}, u32[]{:S(2)}) collective-permute-start(bf16[168,4096]{1,0:T(8,128)(2,1)S(1)} %copy-done.8), channel_id=1, source_target_pairs={{0,3},{1,2},{2,1},{3,0},{4,7},{5,6},{6,5},{7,4},{8,11},{9,10},{10,... | collective-permute-start | bytes 4128776 | tf_op jit(solution)/shard_map/ppermute | solution.py:28
  468.1 84.1 %collective-permute-start.8 = (f32[1,512]{1,0:T(1,128)S(1)}, f32[1,512]{1,0:T(1,128)S(1)}, u32[]{:S(2)}, u32[]{:S(2)}) collective-permute-start(f32[1,512]{1,0:T(1,128)S(1)} %add.133), channel_id=1, source_target_pairs={{0,2},{1,3},{2,0},{3,1},{4,6},{5,7},{6,4},{7,5},{8,10},{9,11},{10,... | collective-permute-start | bytes 6152 | tf_op jit(solution)/shard_map/ppermute | solution.py:28
  552.2 13.1 %collective-permute-start.22 = (f32[2,128]{1,0:T(2,128)S(1)}, f32[2,128]{1,0:T(2,128)S(1)}, u32[]{:S(2)}, u32[]{:S(2)}) collective-permute-start(f32[2,128]{1,0:T(2,128)S(1)} %add.150), channel_id=1, source_target_pairs={{0,8},{4,12},{8,0},{12,4},{16,24},{20,28},{24,16},{28,20},{1,9},{5... | collective-permute-start | bytes 3080 | tf_op jit(solution)/shard_map/ppermute | solution.py:28
  565.3 4.5 collective-permute-start.23
  565.4 4.4 collective-permute-start.17
  569.8 4.6 collective-permute-start.18
  (18 other events, 268.1 us)
Sparse Core Ops, SparseCore 0:
  10.2 106.4 all-gather.6
  118.3 118.8 all-gather.4
  275.0 126.2 all-gather.8
  402.7 80.1 all-gather.10

commit v6 on v5

--- a/solution.py
+++ b/solution.py
@@ -198,42 +198,57 @@
     )(part, wide, d, turned, gain_column)
 
 
-def weight_grad_body(columns_ref, d_ref, k_ref, v_ref, sum_ref, *, scale):
-    step = pl.program_id(0)
-    product = dot(columns_ref[...], d_ref[...])
-
-    @pl.when(step == 0)
-    def _():
-        sum_ref[...] = product
-
-    @pl.when(step > 0)
-    def _():
-        sum_ref[...] += product
-
-    @pl.when(step == pl.num_programs(0) - 1)
-    def _():
-        cut = k_ref.shape[1]
-        k_ref[...] = (scale * sum_ref[:, :cut]).astype(k_ref.dtype)
-        v_ref[...] = (scale * sum_ref[:, cut:]).astype(v_ref.dtype)
+CHUNKS = 4
+
+
+def weight_grad_body(
+    columns_ref, d_ref, k_ref, v_ref, left_ref, right_ref, sum_ref, left_sems, right_sems, *, scale
+):
+    chunk = right_ref.shape[1]
+
+    def fetch(i):
+        at = pl.ds(pl.multiple_of(i * chunk, chunk), chunk)
+        return (
+            pltpu.make_async_copy(columns_ref.at[:, at], left_ref.at[i], left_sems.at[i]),
+            pltpu.make_async_copy(d_ref.at[at, :], right_ref.at[i], right_sems.at[i]),
+        )
+
+    for i in range(CHUNKS):
+        for copy in fetch(i):
+            copy.start()
+    sum_ref[...] = jnp.zeros_like(sum_ref)
+
+    @pl.loop(0, CHUNKS)
+    def _(i):
+        for copy in fetch(i):
+            copy.wait()
+        sum_ref[...] += dot(left_ref[i], right_ref[i])
+
+    cut = k_ref.shape[1]
+    k_ref[...] = (scale * sum_ref[:, :cut]).astype(k_ref.dtype)
+    v_ref[...] = (scale * sum_ref[:, cut:]).astype(v_ref.dtype)
 
 
 def weight_grads(columns, d, scale):
     rows, tokens = columns.shape
     cols = d.shape[1]
-    chunk = tokens // 4
-    out = pl.BlockSpec((rows, cols // 2), lambda i: (0, 0))
+    chunk = tokens // CHUNKS
+    vmem = pl.BlockSpec(memory_space=pltpu.MemorySpace.VMEM)
+    hbm = pl.BlockSpec(memory_space=pltpu.MemorySpace.HBM)
     shape = jax.ShapeDtypeStruct((rows, cols // 2), jnp.bfloat16)
     return pl.pallas_call(
         functools.partial(weight_grad_body, scale=scale),
-        grid=(4,),
-        in_specs=[
-            pl.BlockSpec((rows, chunk), lambda i: (0, i)),
-            pl.BlockSpec((chunk, cols), lambda i: (i, 0)),
+        in_specs=[hbm, hbm],
+        out_specs=(vmem, vmem),
+        out_shape=(shape, shape),
+        scratch_shapes=[
+            pltpu.VMEM((CHUNKS, rows, chunk), jnp.bfloat16),
+            pltpu.VMEM((CHUNKS, chunk, cols), jnp.bfloat16),
+            pltpu.VMEM((rows, cols), jnp.float32),
+            pltpu.SemaphoreType.DMA((CHUNKS,)),
+            pltpu.SemaphoreType.DMA((CHUNKS,)),
         ],
-        out_specs=(out, out),
-        out_shape=(shape, shape),
-        scratch_shapes=[pltpu.VMEM((rows, cols), jnp.float32)],
-        compiler_params=pltpu.CompilerParams(vmem_limit_bytes=40 << 20),
+        compiler_params=pltpu.CompilerParams(vmem_limit_bytes=58 << 20),
         name="weight_grads",
     )(columns, d)
 

time: 607 us -> 603 us (level)
    unnamed x29 -> x27, local copies, waits for them, and re-layouts: 14.2 us -> 10.8 us
where the time goes in v6:
time: 603 us; the launch traced here: 602 us
  waiting for transfers between devices  387 us (64%)
  Pallas kernels  58.9 us (10%)
  matrix products  44.9 us (7%)
  local copies, waits for them, and re-layouts  34.1 us (6%)
  starting transfers between devices  33.1 us (5%)
  other arithmetic  29.9 us (5%)
  between operations  14.1 us (2%)
    ppermute x22, waiting for transfers between devices, swap(): lax.ppermute(value, axis, [(s, s ^ flip) for s in range(lax.axis_size(axi...  140 us
    ppermute x2, waiting for transfers between devices, shift(): lax.ppermute(value, axis, [(s, s + steps) for s in range(initial, last)])  111 us
    all_gather x1, waiting for transfers between devices, layer(): wide_kv = lax.all_gather(key_value, 'ctx', axis=0, tiled=True)  80.5 us
    all_gather x1, waiting for transfers between devices, layer(): wide_q = lax.all_gather(w_query, 'ctx', axis=0, tiled=True)  55.3 us
    dot_general x4, matrix products, dot(): return lax.dot_general(a, b, dims, preferred_element_type=jnp.float32)  44.9 us
    ppermute x22, starting transfers between devices, swap(): lax.ppermute(value, axis, [(s, s ^ flip) for s in range(lax.axis_size(axi...  30.2 us
    pallas_call x1, Pallas kernels, attention(): pl.pallas_call(functools.partial(attention_body, rows=rows, heads=heads,...  25.4 us
    pallas_call x1, Pallas kernels, normed_grad(): pl.pallas_call(normed_grad_body, grid=(width // rows,), in_specs=[by_row,...  13 us
  transfers between devices with their start and end apart: 28, of which 11 were waited for; matrix products, arithmetic and copies ran while one was open for 17% of the time, Pallas kernels for 4%

profile of v6, /device:TPU:0, one launch (start us, length us, event | category | flops | bytes accessed | tf_op | source)
XLA Modules:
  0.0 602.4 jit_solution(13288832413286853011)
XLA Ops:
  10.6 8.3 %copy.20 = bf16[512,5376]{0,1:T(8,128)(2,1)} copy(bf16[512,5376]{1,0:T(8,128)(2,1)} %param.9) | data formatting | bytes 11010048 | tf_op args[0]
  18.9 4.4 fusion
  23.3 7.0 %fusion.2 = bf16[512,5376]{1,0:T(8,128)(2,1)} fusion(bf16[512,5376]{1,0:T(8,128)(2,1)} %param.9, f32[5376]{0:T(1024)S(1)} %copy-done.9, f32[512]{0:T(512)S(1)} %add_rsqrt_fusion), kind=kLoop, calls=%fused_computation.4 | loop fusion | flops 11010048 | bytes 11033600 | tf_op jit(solution)/shard_map/convert_element_type | solution.py:427
  30.3 4.6 multiply_convert_fusion
  36.1 80.5 %all-gather.7.cloned.1.call-done.wide_ref = bf16[5376,1024]{1,0:T(8,128)(2,1)} async-done(((bf16[672,1024]{1,0:T(8,128)(2,1)}), bf16[5376,1024]{1,0:T(8,128)(2,1)}) %all-gather.7.cloned.1.call-update) | async-done | bytes 11010064 | tf_op jit(solution)/shard_map/all_gather | solution.py:420
  116.7 11.3 %fusion.13.k_ref.v_ref = f32[512,1024]{1,0:T(8,128)} fusion(bf16[512,5376]{1,0:T(8,128)(2,1)} %fusion.2, bf16[5376,1024]{1,0:T(8,128)(2,1)} %all-gather.7.cloned.1.call-done.wide_ref), kind=kOutput, calls=%fused_computation.56 | convolution fusion | flops 5637144576 | bytes 18612224 | tf_op jit(solution)/shard_map/dot_general | solution.py:32
  133.3 45.9 %collective-permute-done.far_ref = bf16[2,512,512]{2,1,0:T(8,128)(2,1)S(1)} collective-permute-done((bf16[2,512,512]{2,1,0:T(8,128)(2,1)}, bf16[2,512,512]{2,1,0:T(8,128)(2,1)S(1)}, u32[]{:S(2)}, u32[]{:S(2)}) %collective-permute-start) | collective-permute-done | bytes 1048608 | tf_op jit(solution)/shard_map/ppermute | solution.py:24
  182.0 55.3 %all-gather.5.cloned.1.call-done = bf16[5376,1024]{1,0:T(8,128)(2,1)} async-done(((bf16[672,1024]{1,0:T(8,128)(2,1)}), bf16[5376,1024]{1,0:T(8,128)(2,1)}) %all-gather.5.cloned.1.call-update) | async-done | bytes 11010064 | tf_op jit(solution)/shard_map/all_gather | solution.py:421
  237.2 11.2 %fusion.12.q_ref = f32[512,1024]{1,0:T(8,128)} fusion(bf16[512,5376]{1,0:T(8,128)(2,1)} %fusion.2, bf16[5376,1024]{1,0:T(8,128)(2,1)} %all-gather.5.cloned.1.call-done), kind=kOutput, calls=%fused_computation.55 | convolution fusion | flops 5637144576 | bytes 18612224 | tf_op jit(solution)/shard_map/dot_general | solution.py:32
  248.4 25.4 %attention.1 = (bf16[512,1024]{1,0:T(8,128)(2,1)}, f32[2,512,512]{2,1,0:T(8,128)}, bf16[2,512,512]{2,1,0:T(8,128)(2,1)S(1)}, bf16[2,512,512]{2,1,0:T(8,128)(2,1)S(1)}, f32[1,128]{1,0:T(1,128)S(1)}) custom-call(s32[1]{0:T(128)} %bitcast.start_ref, s32[4]{0:T(128)S(1)} %bitcast.72, f32[512,1024]{1,0:T(8,128)} %fusion.12.q_ref, ...), custom_call_target="tpu_custom_call" | custom-call | tf_op jit(solution)/shard_map/attention/pallas_call | solution.py:364
  280.4 65.2 %collective-permute-done.3.far_ref = bf16[2,512,512]{2,1,0:T(8,128)(2,1)S(1)} collective-permute-done((bf16[2,512,512]{2,1,0:T(8,128)(2,1)S(1)}, bf16[2,512,512]{2,1,0:T(8,128)(2,1)S(1)}, u32[]{:S(2)}, u32[]{:S(2)}) %collective-permute-start.3) | collective-permute-done | bytes 1048608 | tf_op jit(solution)/shard_map/ppermute | solution.py:24
  346.6 7.1 %key_grads.1 = (bf16[512,1024]{1,0:T(8,128)(2,1)}, f32[1,128]{1,0:T(1,128)}) custom-call(f32[2,512,512]{2,1,0:T(8,128)} %get-tuple-element.26.own_ref, bf16[2,512,512]{2,1,0:T(8,128)(2,1)} %get-tuple-element.52.near_ref, bf16[2,512,512]{2,1,0:T(8,128)(2,1)} %copy-done.8, f32[512,1024]{1,0:T(8,128)} %fusion.13.k_ref.v_ref, f32[1,128]{1,0:T(1,128)} %bitcast.82), custom_call_target="tpu_custom_call" | custom-call | tf_op jit(solution)/shard_map/key_grads/pallas_call | solution.py:141
  361.5 28.1 %collective-permute-done.9 = bf16[2,168,512]{2,1,0:T(8,128)(2,1)} collective-permute-done((bf16[2,168,512]{2,1,0:T(8,128)(2,1)}, bf16[2,168,512]{2,1,0:T(8,128)(2,1)}, u32[]{:S(2)}, u32[]{:S(2)}) %collective-permute-start.9) | collective-permute-done | bytes 344096 | tf_op jit(solution)/shard_map/ppermute | solution.py:28
  389.6 10.7 %collective-permute-done.10 = bf16[2,168,512]{2,1,0:T(8,128)(2,1)} collective-permute-done((bf16[2,168,512]{2,1,0:T(8,128)(2,1)}, bf16[2,168,512]{2,1,0:T(8,128)(2,1)}, u32[]{:S(2)}, u32[]{:S(2)}) %collective-permute-start.10) | collective-permute-done | bytes 344096 | tf_op jit(solution)/shard_map/ppermute | solution.py:28
  401.8 11.4 %convolution_bitcast_fusion.part_ref = f32[5376,512]{1,0:T(8,128)} fusion(bf16[512,1024]{1,0:T(8,128)(2,1)} %get-tuple-element.25, bf16[5376,1024]{1,0:T(8,128)(2,1)} %all-gather.5.cloned.1.call-done), kind=kOutput, calls=%fused_computation.6 | convolution fusion | flops 5637144576 | bytes 23068672 | tf_op jit(solution)/shard_map/dot_general | solution.py:32
  416.5 4.5 broadcast_in_dim.42
  421.0 4.5 reshape.93
  434.2 13.0 %normed_grad.1 = (bf16[5376,512]{1,0:T(8,128)(2,1)S(1)}, f32[1,512]{1,0:T(1,128)S(1)}) custom-call(f32[5376,512]{1,0:T(8,128)} %convolution_bitcast_fusion.part_ref, bf16[5376,1024]{1,0:T(8,128)(2,1)} %all-gather.7.cloned.1.call-done.wide_ref, bf16[512,1024]{1,0:T(8,128)(2,1)S(1)} %copy-done.1, bf16[5376,512]{1,0:T(8,128)(2,1)} %bitcast.73, ...), custom_call_target="tpu_custom_call" | custom-call | tf_op jit(solution)/shard_map/normed_grad/pallas_call | solution.py:180
  448.7 9.7 %collective-permute-done.19 = f32[2,128]{1,0:T(2,128)S(1)} collective-permute-done((f32[2,128]{1,0:T(2,128)S(1)}, f32[2,128]{1,0:T(2,128)S(1)}, u32[]{:S(2)}, u32[]{:S(2)}) %collective-permute-start.19) | collective-permute-done | bytes 1056 | tf_op jit(solution)/shard_map/ppermute | solution.py:28
  469.7 82.5 %collective-permute-done.8 = f32[1,512]{1,0:T(1,128)S(1)} collective-permute-done((f32[1,512]{1,0:T(1,128)S(1)}, f32[1,512]{1,0:T(1,128)S(1)}, u32[]{:S(2)}, u32[]{:S(2)}) %collective-permute-start.8) | collective-permute-done | bytes 2080 | tf_op jit(solution)/shard_map/ppermute | solution.py:28
  552.2 7.9 %collective-permute-start.22 = (f32[2,128]{1,0:T(2,128)S(1)}, f32[2,128]{1,0:T(2,128)S(1)}, u32[]{:S(2)}, u32[]{:S(2)}) collective-permute-start(f32[2,128]{1,0:T(2,128)S(1)} %add.150), channel_id=1, source_target_pairs={{0,8},{4,12},{8,0},{12,4},{16,24},{20,28},{24,16},{28,20},{1,9},{5... | collective-permute-start | bytes 3080 | tf_op jit(solution)/shard_map/ppermute | solution.py:28
  560.2 3.9 fusion.7
  575.1 11.1 %multiply_convert_fusion.1 = bf16[672,1024]{1,0:T(8,128)(2,1)} fusion(bf16[672,4096]{1,0:T(8,128)(2,1)} %bitcast.30.columns_ref, bf16[4096,1024]{1,0:T(8,128)(2,1)} %all-gather.9.cloned.1.call-done), kind=kOutput, calls=%fused_computation.14 | convolution fusion | flops 5638520832 | bytes 15269888 | tf_op jit(solution)/shard_map/dot_general | solution.py:32
  586.2 9.7 %weight_grads.1 = (bf16[672,512]{1,0:T(8,128)(2,1)}, bf16[672,512]{1,0:T(8,128)(2,1)}) custom-call(bf16[672,4096]{1,0:T(8,128)(2,1)} %bitcast.30.columns_ref, bf16[4096,1024]{1,0:T(8,128)(2,1)} %all-gather.11.cloned.1.call-done.d_ref), custom_call_target="tpu_custom_call" | custom-call | tf_op jit(solution)/shard_map/weight_grads/pallas_call | solution.py:239
  (119 shorter events, 65.1 us)
Async XLA Ops:
  7.2 109.5 %all-gather.7.cloned.1.call-start = ((), (), s32[]{:S(2)}) async-start(), calls=%async_computation.1 | async-start | bytes 12386304 | tf_op jit(solution)/shard_map/all_gather | solution.py:420
  9.8 227.5 %all-gather.5.cloned.1.call-start = ((), (), s32[]{:S(2)}) async-start(), calls=%async_computation | async-start | bytes 12386304 | tf_op jit(solution)/shard_map/all_gather | solution.py:421
  10.5 564.5 %all-gather.9.cloned.1.call-start = ((), (), s32[]{:S(2)}) async-start(), calls=%async_computation.2 | async-start | bytes 9437184 | tf_op jit(solution)/shard_map/all_gather | solution.py:463
  131.8 47.5 %collective-permute-start = (bf16[2,512,512]{2,1,0:T(8,128)(2,1)}, bf16[2,512,512]{2,1,0:T(8,128)(2,1)S(1)}, u32[]{:S(2)}, u32[]{:S(2)}) collective-permute-start(bf16[2,512,512]{2,1,0:T(8,128)(2,1)} %key_rows.1.own_ref), channel_id=1, source_target_pairs={{0,8},{4,12},{8,16},{12,20},{16,24},{20,28},{1,9},{5,13},{9,17},{1... | collective-permute-start | bytes 3145736 | tf_op jit(solution)/shard_map/ppermute | solution.py:24
  182.0 66.5 %collective-permute-start.1 = (bf16[2,512,512]{2,1,0:T(8,128)(2,1)}, bf16[2,512,512]{2,1,0:T(8,128)(2,1)}, u32[]{:S(2)}, u32[]{:S(2)}) collective-permute-start(bf16[2,512,512]{2,1,0:T(8,128)(2,1)} %broadcast_select_fusion.1), channel_id=1, source_target_pairs={{0,4},{4,0},{8,12},{12,8},{16,20},{20,16},{24,28},{28,24},{1,5},{5... | collective-permute-start | bytes 3145736 | tf_op jit(solution)/shard_map/ppermute | solution.py:28
  274.8 311.4 %all-gather.11.cloned.1.call-start = ((), (), s32[]{:S(2)}) async-start(), calls=%async_computation.3 | async-start | bytes 9437184 | tf_op jit(solution)/shard_map/all_gather | solution.py:475
  278.9 66.7 %collective-permute-start.3 = (bf16[2,512,512]{2,1,0:T(8,128)(2,1)S(1)}, bf16[2,512,512]{2,1,0:T(8,128)(2,1)S(1)}, u32[]{:S(2)}, u32[]{:S(2)}) collective-permute-start(bf16[2,512,512]{2,1,0:T(8,128)(2,1)S(1)} %get-tuple-element.51), channel_id=1, source_target_pairs={{8,0},{12,4},{16,8},{20,12},{24,16},{28,20},{9,1},{13,5},{17,9},{2... | collective-permute-start | bytes 3145736 | tf_op jit(solution)/shard_map/ppermute | solution.py:24
  354.7 34.9 %collective-permute-start.9 = (bf16[2,168,512]{2,1,0:T(8,128)(2,1)}, bf16[2,168,512]{2,1,0:T(8,128)(2,1)}, u32[]{:S(2)}, u32[]{:S(2)}) collective-permute-start(bf16[2,168,512]{2,1,0:T(8,128)(2,1)} %get-tuple-element.50), channel_id=1, source_target_pairs={{0,8},{4,12},{8,0},{12,4},{16,24},{20,28},{24,16},{28,20},{1,9},{5... | collective-permute-start | bytes 1032200 | tf_op jit(solution)/shard_map/ppermute | solution.py:28
  358.2 42.0 %collective-permute-start.10 = (bf16[2,168,512]{2,1,0:T(8,128)(2,1)}, bf16[2,168,512]{2,1,0:T(8,128)(2,1)}, u32[]{:S(2)}, u32[]{:S(2)}) collective-permute-start(bf16[2,168,512]{2,1,0:T(8,128)(2,1)} %get-tuple-element.49), channel_id=1, source_target_pairs={{0,16},{4,20},{8,24},{12,28},{16,0},{20,4},{24,8},{28,12},{1,17},{... | collective-permute-start | bytes 1032200 | tf_op jit(solution)/shard_map/ppermute | solution.py:28
  358.2 42.0 %collective-permute-start.11 = (bf16[2,168,512]{2,1,0:T(8,128)(2,1)S(1)}, bf16[2,168,512]{2,1,0:T(8,128)(2,1)}, u32[]{:S(2)}, u32[]{:S(2)}) collective-permute-start(bf16[2,168,512]{2,1,0:T(8,128)(2,1)S(1)} %get-tuple-element.48), channel_id=1, source_target_pairs={{0,24},{4,28},{8,16},{12,20},{16,8},{20,12},{24,0},{28,4},{1,25},{... | collective-permute-start | bytes 1032200 | tf_op jit(solution)/shard_map/ppermute | solution.py:28
  401.7 11.5 %collective-permute-start.12 = (bf16[4,168,512]{2,1,0:T(8,128)(2,1)S(1)}, bf16[4,168,512]{2,1,0:T(8,128)(2,1)S(1)}, u32[]{:S(2)}, u32[]{:S(2)}) collective-permute-start(bf16[4,168,512]{2,1,0:T(8,128)(2,1)S(1)} %dynamic-slice_bitcast_fusion), channel_id=1, source_target_pairs={{0,4},{4,0},{8,12},{12,8},{16,20},{20,16},{24,28},{28,24},{1,5},{5... | collective-permute-start | bytes 2064392 | tf_op jit(solution)/shard_map/ppermute | solution.py:28
  425.5 38.3 %collective-permute-start.13 = (bf16[168,4096]{1,0:T(8,128)(2,1)}, bf16[168,4096]{1,0:T(8,128)(2,1)S(1)}, u32[]{:S(2)}, u32[]{:S(2)}) collective-permute-start(bf16[168,4096]{1,0:T(8,128)(2,1)} %reshape.93), channel_id=1, source_target_pairs={{0,1},{1,0},{2,3},{3,2},{4,5},{5,4},{6,7},{7,6},{8,9},{9,8},{10,11... | collective-permute-start | bytes 4128776 | tf_op jit(solution)/shard_map/ppermute | solution.py:28
  427.3 39.3 %collective-permute-start.14 = (bf16[168,4096]{1,0:T(8,128)(2,1)}, bf16[168,4096]{1,0:T(8,128)(2,1)S(1)}, u32[]{:S(2)}, u32[]{:S(2)}) collective-permute-start(bf16[168,4096]{1,0:T(8,128)(2,1)} %reshape.93), channel_id=1, source_target_pairs={{0,2},{1,3},{2,0},{3,1},{4,6},{5,7},{6,4},{7,5},{8,10},{9,11},{10,... | collective-permute-start | bytes 4128776 | tf_op jit(solution)/shard_map/ppermute | solution.py:28
  428.8 29.6 %collective-permute-start.19 = (f32[2,128]{1,0:T(2,128)S(1)}, f32[2,128]{1,0:T(2,128)S(1)}, u32[]{:S(2)}, u32[]{:S(2)}) collective-permute-start(f32[2,128]{1,0:T(2,128)S(1)} %pad_maximum_fusion.3), channel_id=1, source_target_pairs={{0,1},{1,0},{2,3},{3,2},{4,5},{5,4},{6,7},{7,6},{8,9},{9,8},{10,11... | collective-permute-start | bytes 3080 | tf_op jit(solution)/shard_map/ppermute | solution.py:28
  447.2 18.2 %collective-permute-start.7 = (f32[1,512]{1,0:T(1,128)S(1)}, f32[1,512]{1,0:T(1,128)S(1)}, u32[]{:S(2)}, u32[]{:S(2)}) collective-permute-start(f32[1,512]{1,0:T(1,128)S(1)} %mul.156), channel_id=1, source_target_pairs={{0,1},{1,0},{2,3},{3,2},{4,5},{5,4},{6,7},{7,6},{8,9},{9,8},{10,11... | collective-permute-start | bytes 6152 | tf_op jit(solution)/shard_map/ppermute | solution.py:28
  460.5 99.7 %collective-permute-start.4 = (bf16[1344,512]{1,0:T(8,128)(2,1)S(1)}, bf16[1344,512]{1,0:T(8,128)(2,1)S(1)}, u32[]{:S(2)}, u32[]{:S(2)}) collective-permute-start(bf16[1344,512]{1,0:T(8,128)(2,1)S(1)} %get-tuple-element.42), channel_id=1, source_target_pairs={{0,1},{1,0},{2,3},{3,2},{4,5},{5,4},{6,7},{7,6},{8,9},{9,8},{10,11... | collective-permute-start | bytes 4128776 | tf_op jit(solution)/shard_map/ppermute | solution.py:28
  462.1 98.1 %collective-permute-start.5 = (bf16[1344,512]{1,0:T(8,128)(2,1)S(1)}, bf16[1344,512]{1,0:T(8,128)(2,1)S(1)}, u32[]{:S(2)}, u32[]{:S(2)}) collective-permute-start(bf16[1344,512]{1,0:T(8,128)(2,1)S(1)} %get-tuple-element.44), channel_id=1, source_target_pairs={{0,2},{1,3},{2,0},{3,1},{4,6},{5,7},{6,4},{7,5},{8,10},{9,11},{10,... | collective-permute-start | bytes 4128776 | tf_op jit(solution)/shard_map/ppermute | solution.py:28
  463.8 96.3 %collective-permute-start.6 = (bf16[1344,512]{1,0:T(8,128)(2,1)S(1)}, bf16[1344,512]{1,0:T(8,128)(2,1)S(1)}, u32[]{:S(2)}, u32[]{:S(2)}) collective-permute-start(bf16[1344,512]{1,0:T(8,128)(2,1)S(1)} %get-tuple-element.43), channel_id=1, source_target_pairs={{0,3},{1,2},{2,1},{3,0},{4,7},{5,6},{6,5},{7,4},{8,11},{9,10},{10,... | collective-permute-start | bytes 4128776 | tf_op jit(solution)/shard_map/ppermute | solution.py:28
  466.6 97.5 %collective-permute-start.15 = (bf16[168,4096]{1,0:T(8,128)(2,1)S(1)}, bf16[168,4096]{1,0:T(8,128)(2,1)S(1)}, u32[]{:S(2)}, u32[]{:S(2)}) collective-permute-start(bf16[168,4096]{1,0:T(8,128)(2,1)S(1)} %copy-done.7), channel_id=1, source_target_pairs={{0,3},{1,2},{2,1},{3,0},{4,7},{5,6},{6,5},{7,4},{8,11},{9,10},{10,... | collective-permute-start | bytes 4128776 | tf_op jit(solution)/shard_map/ppermute | solution.py:28
  468.1 84.1 %collective-permute-start.8 = (f32[1,512]{1,0:T(1,128)S(1)}, f32[1,512]{1,0:T(1,128)S(1)}, u32[]{:S(2)}, u32[]{:S(2)}) collective-permute-start(f32[1,512]{1,0:T(1,128)S(1)} %add.133), channel_id=1, source_target_pairs={{0,2},{1,3},{2,0},{3,1},{4,6},{5,7},{6,4},{7,5},{8,10},{9,11},{10,... | collective-permute-start | bytes 6152 | tf_op jit(solution)/shard_map/ppermute | solution.py:28
  552.2 13.1 %collective-permute-start.22 = (f32[2,128]{1,0:T(2,128)S(1)}, f32[2,128]{1,0:T(2,128)S(1)}, u32[]{:S(2)}, u32[]{:S(2)}) collective-permute-start(f32[2,128]{1,0:T(2,128)S(1)} %add.150), channel_id=1, source_target_pairs={{0,8},{4,12},{8,0},{12,4},{16,24},{20,28},{24,16},{28,20},{1,9},{5... | collective-permute-start | bytes 3080 | tf_op jit(solution)/shard_map/ppermute | solution.py:28
  565.3 4.5 collective-permute-start.23
  565.4 4.4 collective-permute-start.17
  569.8 4.6 collective-permute-start.18
  (17 other events, 264.5 us)
Sparse Core Ops, SparseCore 0:
  10.2 106.4 all-gather.6
  118.3 118.8 all-gather.4
  274.9 126.2 all-gather.8
  402.6 80.1 all-gather.10

commit v7 on v6

--- a/solution.py
+++ b/solution.py
@@ -111,7 +111,7 @@
     )(projected, projected, gain[None, :])
 
 
-def key_grad_body(own_ref, near_ref, far_ref, k_ref, gain_ref, out_ref, sum_ref):
+def key_grad_body(own_ref, near_ref, far_ref, k_ref, gain_ref, late_ref, out_ref, sum_ref):
     total = own_ref[0] + near_ref[0].astype(jnp.float32) + far_ref[0].astype(jnp.float32)
 
     @pl.when((pl.program_id(0) == 0) & (pl.program_id(1) == 0))
@@ -134,7 +134,7 @@
         out_ref[...] = total.astype(jnp.bfloat16)
 
 
-def key_grads_of(own, near, far, projected, gain, kv_heads, head_dim):
+def key_grads_of(own, near, far, projected, gain, late, kv_heads, head_dim):
     tokens = projected.shape[0]
     stacked = pl.BlockSpec((1, tokens, head_dim), lambda t, g: (t, 0, g))
     row = pl.BlockSpec((1, head_dim), lambda t, g: (0, 0))
@@ -147,17 +147,19 @@
             stacked,
             pl.BlockSpec((tokens, head_dim), lambda t, g: (0, g)),
             row,
+            pl.BlockSpec(memory_space=pl.ANY),
         ],
         out_specs=(
             pl.BlockSpec((tokens, head_dim), lambda t, g: (0, t * kv_heads + g)),
             row,
         ),
         out_shape=(
-            jax.ShapeDtypeStruct((tokens, 2 * kv_heads * head_dim), jnp.bfloat16),
+            jax.ShapeDtypeStruct(late.shape, jnp.bfloat16),
             jax.ShapeDtypeStruct((1, head_dim), jnp.float32),
         ),
+        input_output_aliases={5: 0},
         name="key_grads",
-    )(own, near, far, projected, gain[None, :])
+    )(own, near, far, projected, gain[None, :], late)
 
 
 def normed_grad_body(part_ref, wide_ref, d_ref, x_ref, gain_ref, out_ref, dots_ref, dt_ref):
@@ -202,7 +204,19 @@
 
 
 def weight_grad_body(
-    columns_ref, d_ref, k_ref, v_ref, left_ref, right_ref, sum_ref, left_sems, right_sems, *, scale
+    columns_ref,
+    d_ref,
+    first_ref,
+    q_ref,
+    k_ref,
+    v_ref,
+    left_ref,
+    right_ref,
+    sum_ref,
+    left_sems,
+    right_sems,
+    *,
+    scale,
 ):
     chunk = right_ref.shape[1]
 
@@ -226,21 +240,25 @@
 
     cut = k_ref.shape[1]
     k_ref[...] = (scale * sum_ref[:, :cut]).astype(k_ref.dtype)
-    v_ref[...] = (scale * sum_ref[:, cut:]).astype(v_ref.dtype)
-
-
-def weight_grads(columns, d, scale):
+    v_ref[...] = (scale * sum_ref[:, cut : 2 * cut]).astype(v_ref.dtype)
+    half = first_ref.shape[1]
+    q_ref[:, :half] = first_ref[...]
+    q_ref[:, half:] = (scale * sum_ref[:, 2 * cut :]).astype(q_ref.dtype)
+
+
+def weight_grads(columns, d, first, scale):
     rows, tokens = columns.shape
     cols = d.shape[1]
     chunk = tokens // CHUNKS
     vmem = pl.BlockSpec(memory_space=pltpu.MemorySpace.VMEM)
     hbm = pl.BlockSpec(memory_space=pltpu.MemorySpace.HBM)
-    shape = jax.ShapeDtypeStruct((rows, cols // 2), jnp.bfloat16)
+    half = first.shape[1]
+    shape = jax.ShapeDtypeStruct((rows, (cols - half) // 2), jnp.bfloat16)
     return pl.pallas_call(
         functools.partial(weight_grad_body, scale=scale),
-        in_specs=[hbm, hbm],
-        out_specs=(vmem, vmem),
-        out_shape=(shape, shape),
+        in_specs=[hbm, hbm, vmem],
+        out_specs=(vmem, vmem, vmem),
+        out_shape=(jax.ShapeDtypeStruct((rows, 2 * half), jnp.bfloat16), shape, shape),
         scratch_shapes=[
             pltpu.VMEM((CHUNKS, rows, chunk), jnp.bfloat16),
             pltpu.VMEM((CHUNKS, chunk, cols), jnp.bfloat16),
@@ -250,7 +268,7 @@
         ],
         compiler_params=pltpu.CompilerParams(vmem_limit_bytes=58 << 20),
         name="weight_grads",
-    )(columns, d)
+    )(columns, d, first)
 
 
 def attention_body(
@@ -350,24 +368,40 @@
             ref[1] = dv_ref[pl.ds(at * tokens, tokens), :].astype(ref.dtype)
 
 
-def attention(start, ends, q_raw, go, own, near, far, mult, kv_heads, head_dim):
+def attention_rest(start, ends, q, go, own, near, far, mult, *refs, **sizes):
+    attention_body(start, ends, q, go, own, near, far, mult, *refs[3:], **sizes)
+
+
+def attention(start, ends, q_raw, go, own, near, far, mult, head_dim, part, carry, place):
     tokens, q_cols = q_raw.shape
-    heads = q_cols // (kv_heads * head_dim)
+    all_kv = own.shape[2] // head_dim
+    heads = q_cols // (all_kv * head_dim)
+    kv_heads = all_kv // 2
+    skip = part * kv_heads
+    to = place // (heads * head_dim)
     rows = min(256, tokens)
     steps = tokens // rows
     span = WIN + rows
-    stacked = pl.BlockSpec((2, tokens, head_dim), lambda g, s, *_: (0, 0, g))
-    by_query = pl.BlockSpec((rows, heads * head_dim), lambda g, s, *_: (s, g))
+    stacked = pl.BlockSpec((2, tokens, head_dim), lambda g, s, *_: (0, 0, skip + g))
+    by_query = pl.BlockSpec((rows, heads * head_dim), lambda g, s, *_: (s, skip + g))
+    by_place = pl.BlockSpec((rows, heads * head_dim), lambda g, s, *_: (s, to + g))
+    whole = pl.BlockSpec(memory_space=pl.ANY)
     row = pl.BlockSpec((1, head_dim), lambda g, s, *_: (0, 0))
     half = jax.ShapeDtypeStruct(own.shape, jnp.bfloat16)
     keys = WIN + tokens
     return pl.pallas_call(
-        functools.partial(attention_body, rows=rows, heads=heads, segments=ends.shape[0]),
+        functools.partial(
+            attention_rest if carry else attention_body,
+            rows=rows,
+            heads=heads,
+            segments=ends.shape[0],
+        ),
         grid_spec=pltpu.PrefetchScalarGridSpec(
             num_scalar_prefetch=2,
             grid=(kv_heads, steps),
-            in_specs=[by_query, by_query, stacked, stacked, stacked, row],
-            out_specs=(by_query, stacked, stacked, stacked, row),
+            in_specs=[by_query, by_query, stacked, stacked, stacked, row]
+            + [whole for _ in carry],
+            out_specs=(by_place, stacked, stacked, stacked, row),
             scratch_shapes=[
                 pltpu.VMEM((steps, span, rows), jnp.float32),
                 pltpu.VMEM((keys, head_dim), jnp.bfloat16),
@@ -379,7 +413,7 @@
             ],
         ),
         out_shape=(
-            jax.ShapeDtypeStruct((tokens, q_cols), jnp.bfloat16),
+            jax.ShapeDtypeStruct((tokens, place + q_cols // 2), jnp.bfloat16),
             jax.ShapeDtypeStruct(own.shape, jnp.float32),
             half,
             half,
@@ -388,8 +422,9 @@
         compiler_params=pltpu.CompilerParams(
             dimension_semantics=("arbitrary", "arbitrary"), vmem_limit_bytes=48 << 20
         ),
+        input_output_aliases={8 + i: 1 + i for i in range(len(carry))},
         name="attention",
-    )(start, ends, q_raw, go, own, near, far, mult)
+    )(start, ends, q_raw, go, own, near, far, mult, *carry)
 
 
 def layer(
@@ -443,40 +478,50 @@
     pieces = start_columns(blocks)
     q_raw = dot(normed, wide_q)
     query_multiplier = (q_gain * query_scale)[None, :]
-    dq16, d_own, d_near, d_far, q_sum = attention(
-        jnp.full((1,), ctx_index * tokens, jnp.int32),
-        jnp.cumsum(half_lengths).astype(jnp.int32),
-        q_raw,
-        output_cotangent,
-        own,
-        near,
-        far,
-        query_multiplier,
-        kv_heads,
-        head_dim,
-    )
+
+    def attend(part, carry, place):
+        return attention(
+            jnp.full((1,), ctx_index * tokens, jnp.int32),
+            jnp.cumsum(half_lengths).astype(jnp.int32),
+            q_raw,
+            output_cotangent,
+            own,
+            near,
+            far,
+            query_multiplier,
+            head_dim,
+            part,
+            carry,
+            place,
+        )
+
+    dqa, *carry, qa_sum = attend(0, (), 0)
+    all_dqa = lax.all_gather(dqa, "ctx", axis=0, tiled=True)
+    late, d_own, d_near, d_far, qb_sum = attend(1, carry, 2 * kv_cols)
+    q_sum = qa_sum + qb_sum
+    dqb = late[:, 2 * kv_cols :]
 
     crossed = swap(d_near, "ctx", 1)
     nothing = jnp.zeros_like(crossed)
     outgoing = d_far + jnp.where(on_first_core, nothing, crossed)
     returned = shift(outgoing, "ctx", -REACH)
-    all_dq = lax.all_gather(dq16, "ctx", axis=0, tiled=True)
-    query_part = dot(wide_q, dq16, NT)
+    query_part = dot(wide_q, jnp.concatenate([dqa, dqb], axis=1), NT)
     query_part = lax.optimization_barrier(query_part)
-    dkv16, k_sum = key_grads_of(
+    late, k_sum = key_grads_of(
         d_own,
         jnp.where(on_first_core, crossed, nothing),
         returned,
         kv_raw,
         key_norm_gain,
+        late,
         kv_heads,
         head_dim,
     )
-    all_dkv = lax.all_gather(dkv16, "ctx", axis=0, tiled=True)
-
-    columns = finish_columns(pieces, dq16)
-
-    head_part, row_dot = normed_grad(query_part, wide_kv, dkv16, turned, gain_column)
+    all_late = lax.all_gather(late, "ctx", axis=0, tiled=True)
+
+    columns = finish_columns(pieces, dqb)
+
+    head_part, row_dot = normed_grad(query_part, wide_kv, late, turned, gain_column)
     row_dot = everywhere(row_dot * inv_row, ("fsdp",))
 
     def part_of(array, index):
@@ -501,8 +546,8 @@
         0,
     )
 
-    q_weights = (grad_scale * dot(columns, all_dq)).astype(jnp.bfloat16)
-    k_weights, v_weights = weight_grads(columns, all_dkv, grad_scale)
+    first_weights = (grad_scale * dot(columns, all_dqa)).astype(jnp.bfloat16)
+    q_weights, k_weights, v_weights = weight_grads(columns, all_late, first_weights, grad_scale)
 
     gains = jnp.concatenate([q_sum * (grad_scale * query_scale), k_sum * grad_scale], axis=0)
     gains = everywhere(gains, ("fsdp",))

time: 603 us -> 611 us (1.013)
  waiting for transfers between devices: 387 us -> 363 us
  starting transfers between devices: 33.1 us -> 49.8 us
  local copies, waits for them, and re-layouts: 34.1 us -> 42.8 us
  Pallas kernels: 58.9 us -> 67.2 us
    ppermute x2, waiting for transfers between devices: 111 us -> 91.8 us  [shift(): lax.ppermute(value, axis, [(s, s + steps) for s in range(initial, last)])]
    ppermute x22, starting transfers between devices: 30.2 us -> 46.8 us  [swap(): lax.ppermute(value, axis, [(s, s ^ flip) for s in range(lax.axis_size(axi...]
    unnamed x27 -> x41, local copies, waits for them, and re-layouts: 10.8 us -> 17.3 us
    pallas_call x1 -> x2, Pallas kernels: 25.4 us -> 29 us  [attention(): pl.pallas_call(functools.partial(attention_rest if carry else attention_b...]
  transfers between devices with their start and end apart: 28 -> 28, of which waited for: 11 -> 14; matrix products, arithmetic and copies ran while one was open for 17% -> 17% of each run, Pallas kernels for 4% -> 6%
where the time goes in v7:
time: 611 us; the launch traced here: 609 us
  waiting for transfers between devices  363 us (59%)
  Pallas kernels  67.2 us (11%)
  starting transfers between devices  49.8 us (8%)
  matrix products  43.3 us (7%)
  local copies, waits for them, and re-layouts  42.8 us (7%)
  other arithmetic  29.4 us (5%)
  between operations  14.1 us (2%)
    ppermute x22, waiting for transfers between devices, swap(): lax.ppermute(value, axis, [(s, s ^ flip) for s in range(lax.axis_size(axi...  135 us
    ppermute x2, waiting for transfers between devices, shift(): lax.ppermute(value, axis, [(s, s + steps) for s in range(initial, last)])  91.8 us
    all_gather x1, waiting for transfers between devices, layer(): wide_kv = lax.all_gather(key_value, 'ctx', axis=0, tiled=True)  80.6 us
    all_gather x1, waiting for transfers between devices, layer(): wide_q = lax.all_gather(w_query, 'ctx', axis=0, tiled=True)  54.6 us
    ppermute x22, starting transfers between devices, swap(): lax.ppermute(value, axis, [(s, s ^ flip) for s in range(lax.axis_size(axi...  46.8 us
    dot_general x4, matrix products, dot(): return lax.dot_general(a, b, dims, preferred_element_type=jnp.float32)  43.3 us
    pallas_call x2, Pallas kernels, attention(): pl.pallas_call(functools.partial(attention_rest if carry else attention_b...  29 us
    unnamed x41, local copies, waits for them, and re-layouts  17.3 us
  transfers between devices with their start and end apart: 28, of which 14 were waited for; matrix products, arithmetic and copies ran while one was open for 17% of the time, Pallas kernels for 6%

profile of v7, /device:TPU:0, one launch (start us, length us, event | category | flops | bytes accessed | tf_op | source)
XLA Modules:
  0.0 609.5 jit_solution(6227580462574403674)
XLA Ops:
  10.6 8.3 %copy.24 = bf16[512,5376]{0,1:T(8,128)(2,1)} copy(bf16[512,5376]{1,0:T(8,128)(2,1)} %param.9) | data formatting | bytes 11010048 | tf_op args[0]
  23.3 6.9 %fusion.2 = bf16[512,5376]{1,0:T(8,128)(2,1)} fusion(bf16[512,5376]{1,0:T(8,128)(2,1)} %param.9, f32[5376]{0:T(1024)S(1)} %copy-done.16, f32[512]{0:T(512)S(1)} %add_rsqrt_fusion), kind=kLoop, calls=%fused_computation.4 | loop fusion | flops 11010048 | bytes 11033600 | tf_op jit(solution)/shard_map/convert_element_type | solution.py:462
  30.2 4.6 multiply_convert_fusion
  36.0 80.6 %all-gather.7.cloned.1.call-done.wide_ref = bf16[5376,1024]{1,0:T(8,128)(2,1)} async-done(((bf16[672,1024]{1,0:T(8,128)(2,1)}), bf16[5376,1024]{1,0:T(8,128)(2,1)}) %all-gather.7.cloned.1.call-update) | async-done | bytes 11010064 | tf_op jit(solution)/shard_map/all_gather | solution.py:455
  116.7 11.3 %fusion.18.k_ref.v_ref = f32[512,1024]{1,0:T(8,128)} fusion(bf16[512,5376]{1,0:T(8,128)(2,1)} %fusion.2, bf16[5376,1024]{1,0:T(8,128)(2,1)} %all-gather.7.cloned.1.call-done.wide_ref), kind=kOutput, calls=%fused_computation.61 | convolution fusion | flops 5637144576 | bytes 18612224 | tf_op jit(solution)/shard_map/dot_general | solution.py:32
  133.5 45.7 %collective-permute-done.far_ref.far = bf16[2,512,512]{2,1,0:T(8,128)(2,1)S(1)} collective-permute-done((bf16[2,512,512]{2,1,0:T(8,128)(2,1)}, bf16[2,512,512]{2,1,0:T(8,128)(2,1)S(1)}, u32[]{:S(2)}, u32[]{:S(2)}) %collective-permute-start) | collective-permute-done | bytes 1048608 | tf_op jit(solution)/shard_map/ppermute | solution.py:24
  182.6 54.6 %all-gather.5.cloned.1.call-done = bf16[5376,1024]{1,0:T(8,128)(2,1)} async-done(((bf16[672,1024]{1,0:T(8,128)(2,1)}), bf16[5376,1024]{1,0:T(8,128)(2,1)}) %all-gather.5.cloned.1.call-update) | async-done | bytes 11010064 | tf_op jit(solution)/shard_map/all_gather | solution.py:456
  237.2 11.2 %fusion.17.q_ref.q = f32[512,1024]{1,0:T(8,128)} fusion(bf16[512,5376]{1,0:T(8,128)(2,1)} %fusion.2, bf16[5376,1024]{1,0:T(8,128)(2,1)} %all-gather.5.cloned.1.call-done), kind=kOutput, calls=%fused_computation.60 | convolution fusion | flops 5637144576 | bytes 18612224 | tf_op jit(solution)/shard_map/dot_general | solution.py:32
  250.7 14.5 %attention.2 = (bf16[512,512]{1,0:T(8,128)(2,1)S(1)}, f32[2,512,512]{2,1,0:T(8,128)}, bf16[2,512,512]{2,1,0:T(8,128)(2,1)S(1)}, bf16[2,512,512]{2,1,0:T(8,128)(2,1)S(1)}, f32[1,128]{1,0:T(1,128)S(1)}) custom-call(s32[1]{0:T(128)} %bitcast.start_ref.start, s32[4]{0:T(128)S(1)} %bitcast.71, f32[512,1024]{1,0:T(8,128)} %fusion.17.q_ref.q, ...), custom_call_target="tpu_custom_call" | custom-call | tf_op jit(solution)/shard_map/attention/pallas_call | solution.py:392
  269.4 14.5 %attention.3 = (bf16[512,1536]{1,0:T(8,128)(2,1)}, f32[2,512,512]{2,1,0:T(8,128)}, bf16[2,512,512]{2,1,0:T(8,128)(2,1)S(1)}, bf16[2,512,512]{2,1,0:T(8,128)(2,1)S(1)}, f32[1,128]{1,0:T(1,128)S(1)}) custom-call(s32[1]{0:T(128)} %bitcast.start_ref.start, s32[4]{0:T(128)S(1)} %bitcast.72, ...), custom_call_target="tpu_custom_call", output_to_operand_aliasing={{1}: (8, {}), {2}: (9, {}), {3}: (10, {})} | custom-call | tf_op jit(solution)/shard_map/attention/pallas_call | solution.py:392
  291.0 46.0 %collective-permute-done.3.far_ref = bf16[2,512,512]{2,1,0:T(8,128)(2,1)S(1)} collective-permute-done((bf16[2,512,512]{2,1,0:T(8,128)(2,1)S(1)}, bf16[2,512,512]{2,1,0:T(8,128)(2,1)S(1)}, u32[]{:S(2)}, u32[]{:S(2)}) %collective-permute-start.3) | collective-permute-done | bytes 1048608 | tf_op jit(solution)/shard_map/ppermute | solution.py:24
  338.1 7.0 %key_grads.1 = (bf16[512,1536]{1,0:T(8,128)(2,1)}, f32[1,128]{1,0:T(1,128)}) custom-call(f32[2,512,512]{2,1,0:T(8,128)} %get-tuple-element.36.own_ref, bf16[2,512,512]{2,1,0:T(8,128)(2,1)} %get-tuple-element.64.near_ref, bf16[2,512,512]{2,1,0:T(8,128)(2,1)} %copy-done.14, f32[512,1024]{1,0:T(8,128)} %fusion.18.k_ref.v_ref, ...), custom_call_target="tpu_custom_call", output_to_operand_aliasing={{0}: (5, {})} | custom-call | tf_op jit(solution)/shard_map/key_grads/pallas_call | solution.py:141
  351.4 18.4 %collective-permute-done.9 = bf16[2,168,512]{2,1,0:T(8,128)(2,1)} collective-permute-done((bf16[2,168,512]{2,1,0:T(8,128)(2,1)}, bf16[2,168,512]{2,1,0:T(8,128)(2,1)}, u32[]{:S(2)}, u32[]{:S(2)}) %collective-permute-start.9) | collective-permute-done | bytes 344096 | tf_op jit(solution)/shard_map/ppermute | solution.py:28
  369.8 5.1 collective-permute-done.10
  374.9 13.3 %collective-permute-done.11 = bf16[2,168,512]{2,1,0:T(8,128)(2,1)} collective-permute-done((bf16[2,168,512]{2,1,0:T(8,128)(2,1)S(1)}, bf16[2,168,512]{2,1,0:T(8,128)(2,1)}, u32[]{:S(2)}, u32[]{:S(2)}) %collective-permute-start.11) | collective-permute-done | bytes 344096 | tf_op jit(solution)/shard_map/ppermute | solution.py:28
  389.7 13.1 %convolution_bitcast_fusion.part_ref = f32[5376,512]{1,0:T(8,128)} fusion(bf16[5376,1024]{1,0:T(8,128)(2,1)} %all-gather.5.cloned.1.call-done, bf16[512,512]{1,0:T(8,128)(2,1)S(1)} %copy-done.15, bf16[512,512]{1,0:T(8,128)(2,1)S(1)} %copy-done.9), kind=kOutput, calls=%fused_computation.6 | convolution fusion | flops 5639241728 | bytes 23068672 | tf_op jit(solution)/shard_map/dot_general | solution.py:32
  406.2 4.6 broadcast_in_dim.43
  410.8 4.5 reshape.93
  423.9 13.0 %normed_grad.1 = (bf16[5376,512]{1,0:T(8,128)(2,1)S(1)}, f32[1,512]{1,0:T(1,128)S(1)}) custom-call(f32[5376,512]{1,0:T(8,128)} %convolution_bitcast_fusion.part_ref, bf16[5376,1024]{1,0:T(8,128)(2,1)} %all-gather.7.cloned.1.call-done.wide_ref, bf16[512,1536]{1,0:T(8,128)(2,1)S(1)} %copy-done, bf16[5376,512]{1,0:T(8,128)(2,1)} %bitcast.73, ...), custom_call_target="tpu_custom_call" | custom-call | tf_op jit(solution)/shard_map/normed_grad/pallas_call | solution.py:182
  438.4 9.5 %collective-permute-done.19 = f32[2,128]{1,0:T(2,128)S(1)} collective-permute-done((f32[2,128]{1,0:T(2,128)S(1)}, f32[2,128]{1,0:T(2,128)S(1)}, u32[]{:S(2)}, u32[]{:S(2)}) %collective-permute-start.19) | collective-permute-done | bytes 1056 | tf_op jit(solution)/shard_map/ppermute | solution.py:28
  459.3 82.2 %collective-permute-done.8 = f32[1,512]{1,0:T(1,128)S(1)} collective-permute-done((f32[1,512]{1,0:T(1,128)S(1)}, f32[1,512]{1,0:T(1,128)S(1)}, u32[]{:S(2)}, u32[]{:S(2)}) %collective-permute-start.8) | collective-permute-done | bytes 2080 | tf_op jit(solution)/shard_map/ppermute | solution.py:28
  541.4 24.1 %collective-permute-start.22 = (f32[2,128]{1,0:T(2,128)S(1)}, f32[2,128]{1,0:T(2,128)S(1)}, u32[]{:S(2)}, u32[]{:S(2)}) collective-permute-start(f32[2,128]{1,0:T(2,128)S(1)} %add.154), channel_id=1, source_target_pairs={{0,8},{4,12},{8,0},{12,4},{16,24},{20,28},{24,16},{28,20},{1,9},{5... | collective-permute-start | bytes 3080 | tf_op jit(solution)/shard_map/ppermute | solution.py:28
  580.9 7.7 %fusion.10.first_ref = bf16[672,512]{1,0:T(8,128)(2,1)} fusion(bf16[672,4096]{1,0:T(8,128)(2,1)} %bitcast.30.columns_ref, bf16[4096,512]{1,0:T(8,128)(2,1)} %all-gather.11.cloned.1.call-done), kind=kOutput, calls=%fused_computation.28 | convolution fusion | flops 2819260416 | bytes 10387456 | tf_op jit(solution)/shard_map/dot_general | solution.py:32
  588.6 14.4 %weight_grads.1 = (bf16[672,1024]{1,0:T(8,128)(2,1)}, bf16[672,512]{1,0:T(8,128)(2,1)}, bf16[672,512]{1,0:T(8,128)(2,1)}) custom-call(bf16[672,4096]{1,0:T(8,128)(2,1)} %bitcast.30.columns_ref, bf16[4096,1536]{1,0:T(8,128)(2,1)} %all-gather.9.cloned.1.call-done.d_ref, bf16[672,512]{1,0:T(8,128)(2,1)} %fusion.10.first_ref), custom_call_target="tpu_custom_call" | custom-call | tf_op jit(solution)/shard_map/weight_grads/pallas_call | solution.py:257
  (135 shorter events, 80.3 us)
Async XLA Ops:
  7.2 109.5 %all-gather.7.cloned.1.call-start = ((), (), s32[]{:S(2)}) async-start(), calls=%async_computation.1 | async-start | bytes 12386304 | tf_op jit(solution)/shard_map/all_gather | solution.py:455
  9.8 227.5 %all-gather.5.cloned.1.call-start = ((), (), s32[]{:S(2)}) async-start(), calls=%async_computation | async-start | bytes 12386304 | tf_op jit(solution)/shard_map/all_gather | solution.py:456
  10.5 570.4 %all-gather.11.cloned.1.call-start = ((), (), s32[]{:S(2)}) async-start(), calls=%async_computation.3 | async-start | bytes 4718592 | tf_op jit(solution)/shard_map/all_gather | solution.py:499
  131.8 47.5 %collective-permute-start = (bf16[2,512,512]{2,1,0:T(8,128)(2,1)}, bf16[2,512,512]{2,1,0:T(8,128)(2,1)S(1)}, u32[]{:S(2)}, u32[]{:S(2)}) collective-permute-start(bf16[2,512,512]{2,1,0:T(8,128)(2,1)} %key_rows.1.own_ref.own), channel_id=1, source_target_pairs={{0,8},{4,12},{8,16},{12,20},{16,24},{20,28},{1,9},{5,13},{9,17},{1... | collective-permute-start | bytes 3145736 | tf_op jit(solution)/shard_map/ppermute | solution.py:24
  182.6 65.9 %collective-permute-start.1 = (bf16[2,512,512]{2,1,0:T(8,128)(2,1)}, bf16[2,512,512]{2,1,0:T(8,128)(2,1)S(1)}, u32[]{:S(2)}, u32[]{:S(2)}) collective-permute-start(bf16[2,512,512]{2,1,0:T(8,128)(2,1)} %broadcast_select_fusion.1), channel_id=1, source_target_pairs={{0,4},{4,0},{8,12},{12,8},{16,20},{20,16},{24,28},{28,24},{1,5},{5... | collective-permute-start | bytes 3145736 | tf_op jit(solution)/shard_map/ppermute | solution.py:28
  287.9 49.2 %collective-permute-start.3 = (bf16[2,512,512]{2,1,0:T(8,128)(2,1)S(1)}, bf16[2,512,512]{2,1,0:T(8,128)(2,1)S(1)}, u32[]{:S(2)}, u32[]{:S(2)}) collective-permute-start(bf16[2,512,512]{2,1,0:T(8,128)(2,1)S(1)} %get-tuple-element.63), channel_id=1, source_target_pairs={{8,0},{12,4},{16,8},{20,12},{24,16},{28,20},{9,1},{13,5},{17,9},{2... | collective-permute-start | bytes 3145736 | tf_op jit(solution)/shard_map/ppermute | solution.py:24
  291.0 297.5 %all-gather.9.cloned.1.call-start = ((), (), s32[]{:S(2)}) async-start(), calls=%async_computation.2 | async-start | bytes 14155776 | tf_op jit(solution)/shard_map/all_gather | solution.py:520
  346.1 23.7 %collective-permute-start.9 = (bf16[2,168,512]{2,1,0:T(8,128)(2,1)}, bf16[2,168,512]{2,1,0:T(8,128)(2,1)}, u32[]{:S(2)}, u32[]{:S(2)}) collective-permute-start(bf16[2,168,512]{2,1,0:T(8,128)(2,1)} %get-tuple-element.62), channel_id=1, source_target_pairs={{0,8},{4,12},{8,0},{12,4},{16,24},{20,28},{24,16},{28,20},{1,9},{5... | collective-permute-start | bytes 1032200 | tf_op jit(solution)/shard_map/ppermute | solution.py:28
  347.9 27.0 %collective-permute-start.10 = (bf16[2,168,512]{2,1,0:T(8,128)(2,1)}, bf16[2,168,512]{2,1,0:T(8,128)(2,1)}, u32[]{:S(2)}, u32[]{:S(2)}) collective-permute-start(bf16[2,168,512]{2,1,0:T(8,128)(2,1)} %get-tuple-element.61), channel_id=1, source_target_pairs={{0,16},{4,20},{8,24},{12,28},{16,0},{20,4},{24,8},{28,12},{1,17},{... | collective-permute-start | bytes 1032200 | tf_op jit(solution)/shard_map/ppermute | solution.py:28
  348.6 39.6 %collective-permute-start.11 = (bf16[2,168,512]{2,1,0:T(8,128)(2,1)S(1)}, bf16[2,168,512]{2,1,0:T(8,128)(2,1)}, u32[]{:S(2)}, u32[]{:S(2)}) collective-permute-start(bf16[2,168,512]{2,1,0:T(8,128)(2,1)S(1)} %get-tuple-element.60), channel_id=1, source_target_pairs={{0,24},{4,28},{8,16},{12,20},{16,8},{20,12},{24,0},{28,4},{1,25},{... | collective-permute-start | bytes 1032200 | tf_op jit(solution)/shard_map/ppermute | solution.py:28
  389.6 13.2 %collective-permute-start.12 = (bf16[4,168,512]{2,1,0:T(8,128)(2,1)S(1)}, bf16[4,168,512]{2,1,0:T(8,128)(2,1)S(1)}, u32[]{:S(2)}, u32[]{:S(2)}) collective-permute-start(bf16[4,168,512]{2,1,0:T(8,128)(2,1)S(1)} %dynamic-slice_bitcast_fusion), channel_id=1, source_target_pairs={{0,4},{4,0},{8,12},{12,8},{16,20},{20,16},{24,28},{28,24},{1,5},{5... | collective-permute-start | bytes 2064392 | tf_op jit(solution)/shard_map/ppermute | solution.py:28
  415.3 37.8 %collective-permute-start.13 = (bf16[168,4096]{1,0:T(8,128)(2,1)}, bf16[168,4096]{1,0:T(8,128)(2,1)S(1)}, u32[]{:S(2)}, u32[]{:S(2)}) collective-permute-start(bf16[168,4096]{1,0:T(8,128)(2,1)} %reshape.93), channel_id=1, source_target_pairs={{0,1},{1,0},{2,3},{3,2},{4,5},{5,4},{6,7},{7,6},{8,9},{9,8},{10,11... | collective-permute-start | bytes 4128776 | tf_op jit(solution)/shard_map/ppermute | solution.py:28
  416.8 39.1 %collective-permute-start.14 = (bf16[168,4096]{1,0:T(8,128)(2,1)}, bf16[168,4096]{1,0:T(8,128)(2,1)S(1)}, u32[]{:S(2)}, u32[]{:S(2)}) collective-permute-start(bf16[168,4096]{1,0:T(8,128)(2,1)} %reshape.93), channel_id=1, source_target_pairs={{0,2},{1,3},{2,0},{3,1},{4,6},{5,7},{6,4},{7,5},{8,10},{9,11},{10,... | collective-permute-start | bytes 4128776 | tf_op jit(solution)/shard_map/ppermute | solution.py:28
  418.3 29.7 %collective-permute-start.19 = (f32[2,128]{1,0:T(2,128)S(1)}, f32[2,128]{1,0:T(2,128)S(1)}, u32[]{:S(2)}, u32[]{:S(2)}) collective-permute-start(f32[2,128]{1,0:T(2,128)S(1)} %pad_maximum_fusion.3), channel_id=1, source_target_pairs={{0,1},{1,0},{2,3},{3,2},{4,5},{5,4},{6,7},{7,6},{8,9},{9,8},{10,11... | collective-permute-start | bytes 3080 | tf_op jit(solution)/shard_map/ppermute | solution.py:28
  436.9 17.7 %collective-permute-start.7 = (f32[1,512]{1,0:T(1,128)S(1)}, f32[1,512]{1,0:T(1,128)S(1)}, u32[]{:S(2)}, u32[]{:S(2)}) collective-permute-start(f32[1,512]{1,0:T(1,128)S(1)} %mul.157), channel_id=1, source_target_pairs={{0,1},{1,0},{2,3},{3,2},{4,5},{5,4},{6,7},{7,6},{8,9},{9,8},{10,11... | collective-permute-start | bytes 6152 | tf_op jit(solution)/shard_map/ppermute | solution.py:28
  449.8 115.7 %collective-permute-start.4 = (bf16[1344,512]{1,0:T(8,128)(2,1)S(1)}, bf16[1344,512]{1,0:T(8,128)(2,1)S(1)}, u32[]{:S(2)}, u32[]{:S(2)}) collective-permute-start(bf16[1344,512]{1,0:T(8,128)(2,1)S(1)} %get-tuple-element.54), channel_id=1, source_target_pairs={{0,1},{1,0},{2,3},{3,2},{4,5},{5,4},{6,7},{7,6},{8,9},{9,8},{10,11... | collective-permute-start | bytes 4128776 | tf_op jit(solution)/shard_map/ppermute | solution.py:28
  451.6 113.9 %collective-permute-start.5 = (bf16[1344,512]{1,0:T(8,128)(2,1)S(1)}, bf16[1344,512]{1,0:T(8,128)(2,1)S(1)}, u32[]{:S(2)}, u32[]{:S(2)}) collective-permute-start(bf16[1344,512]{1,0:T(8,128)(2,1)S(1)} %get-tuple-element.56), channel_id=1, source_target_pairs={{0,2},{1,3},{2,0},{3,1},{4,6},{5,7},{6,4},{7,5},{8,10},{9,11},{10,... | collective-permute-start | bytes 4128776 | tf_op jit(solution)/shard_map/ppermute | solution.py:28
  453.1 112.4 %collective-permute-start.6 = (bf16[1344,512]{1,0:T(8,128)(2,1)S(1)}, bf16[1344,512]{1,0:T(8,128)(2,1)S(1)}, u32[]{:S(2)}, u32[]{:S(2)}) collective-permute-start(bf16[1344,512]{1,0:T(8,128)(2,1)S(1)} %get-tuple-element.55), channel_id=1, source_target_pairs={{0,3},{1,2},{2,1},{3,0},{4,7},{5,6},{6,5},{7,4},{8,11},{9,10},{10,... | collective-permute-start | bytes 4128776 | tf_op jit(solution)/shard_map/ppermute | solution.py:28
  455.9 113.6 %collective-permute-start.15 = (bf16[168,4096]{1,0:T(8,128)(2,1)S(1)}, bf16[168,4096]{1,0:T(8,128)(2,1)S(1)}, u32[]{:S(2)}, u32[]{:S(2)}) collective-permute-start(bf16[168,4096]{1,0:T(8,128)(2,1)S(1)} %copy-done.13), channel_id=1, source_target_pairs={{0,3},{1,2},{2,1},{3,0},{4,7},{5,6},{6,5},{7,4},{8,11},{9,10},{10,... | collective-permute-start | bytes 4128776 | tf_op jit(solution)/shard_map/ppermute | solution.py:28
  457.4 84.0 %collective-permute-start.8 = (f32[1,512]{1,0:T(1,128)S(1)}, f32[1,512]{1,0:T(1,128)S(1)}, u32[]{:S(2)}, u32[]{:S(2)}) collective-permute-start(f32[1,512]{1,0:T(1,128)S(1)} %add.136), channel_id=1, source_target_pairs={{0,2},{1,3},{2,0},{3,1},{4,6},{5,7},{6,4},{7,5},{8,10},{9,11},{10,... | collective-permute-start | bytes 6152 | tf_op jit(solution)/shard_map/ppermute | solution.py:28
  541.4 29.3 %collective-permute-start.22 = (f32[2,128]{1,0:T(2,128)S(1)}, f32[2,128]{1,0:T(2,128)S(1)}, u32[]{:S(2)}, u32[]{:S(2)}) collective-permute-start(f32[2,128]{1,0:T(2,128)S(1)} %add.154), channel_id=1, source_target_pairs={{0,8},{4,12},{8,0},{12,4},{16,24},{20,28},{24,16},{28,20},{1,9},{5... | collective-permute-start | bytes 3080 | tf_op jit(solution)/shard_map/ppermute | solution.py:28
  570.8 4.5 collective-permute-start.23
  572.1 3.7 collective-permute-start.17
  575.7 4.5 collective-permute-start.18
  (24 other events, 280.7 us)
Sparse Core Ops, SparseCore 0:
  10.2 106.4 all-gather.6
  118.3 118.8 all-gather.4
  267.1 58.5 all-gather.10
  345.2 138.5 all-gather.8
